TPU v7x, 32 devices: a whole 2x2x4 slice. The times are simulated.
32 devices in a mesh: seq: 8 (over y, x, core), fsdp: 4 (over z).
Axes of the slice: x: 2, y: 2, z: 4, core: 2. Of those that a mesh axis runs over, the one named last changes fastest.
Arguments:
- hidden_in: bfloat16 [4, 2048, 1024], P('fsdp', 'seq'), may hold values from -6 to 6
- cotangent: bfloat16 [4, 2048, 1024], P('fsdp', 'seq'), may hold values from -6 to 6
- doc_position: int32 [4, 2048], P('fsdp', 'seq'), may hold values from 0 to 2047, as said below
- norm_gains: float32 [2, 1024], P(None, ('seq', 'fsdp')), may hold values from 0.5 to 1.5
- conv_taps: float32 [3, 1024], P(None, ('seq', 'fsdp')), may hold values from -3 to 3
- in_proj: float32 [1024, 3072], P(('seq', 'fsdp')), may hold values from -0.1875 to 0.1875
- out_proj: float32 [1024, 1024], P(('seq', 'fsdp')), may hold values from -0.1875 to 0.1875
- gate_up: float32 [1024, 9216], P(('seq', 'fsdp')), may hold values from -0.1875 to 0.1875
- down_proj: float32 [4608, 1024], P(('seq', 'fsdp')), may hold values from -0.09375 to 0.09375
- first_gains: float32 [2, 1024], P(None, ('seq', 'fsdp')), may hold values from -56 to 56
- first_taps: float32 [3, 1024], P(None, ('seq', 'fsdp')), may hold values from -56 to 56
- first_in: float32 [1024, 3072], P(('seq', 'fsdp')), may hold values from -56 to 56
- first_out: float32 [1024, 1024], P(('seq', 'fsdp')), may hold values from -56 to 56
- first_gate_up: float32 [1024, 9216], P(('seq', 'fsdp')), may hold values from -14 to 14
- first_down: float32 [4608, 1024], P(('seq', 'fsdp')), may hold values from -32 to 32
- second_gains: float32 [2, 1024], P(None, ('seq', 'fsdp')), may hold values from 2.4576 to 24.576
- second_taps: float32 [3, 1024], P(None, ('seq', 'fsdp')), may hold values from 2.4576 to 24.576
- second_in: float32 [1024, 3072], P(('seq', 'fsdp')), may hold values from 2.4576 to 24.576
- second_out: float32 [1024, 1024], P(('seq', 'fsdp')), may hold values from 2.4576 to 24.576
- second_gate_up: float32 [1024, 9216], P(('seq', 'fsdp')), may hold values from 0.16384 to 1.6384
- second_down: float32 [4608, 1024], P(('seq', 'fsdp')), may hold values from 0.8192 to 8.192
Outputs:
- block_out: float32 [4, 2048, 1024], P('fsdp', 'seq')
- grad_hidden: float32 [4, 2048, 1024], P('fsdp', 'seq')
- grad_gains: float32 [2, 1024], P(None, ('seq', 'fsdp'))
- grad_taps: float32 [3, 1024], P(None, ('seq', 'fsdp'))
- grad_in: float32 [1024, 3072], P(('seq', 'fsdp'))
- grad_out: float32 [1024, 1024], P(('seq', 'fsdp'))
- grad_gate_up: float32 [1024, 9216], P(('seq', 'fsdp'))
- grad_down: float32 [4608, 1024], P(('seq', 'fsdp'))
- new_gains: float32 [2, 1024], P(None, ('seq', 'fsdp'))
- new_taps: float32 [3, 1024], P(None, ('seq', 'fsdp'))
- new_in: float32 [1024, 3072], P(('seq', 'fsdp'))
- new_out: float32 [1024, 1024], P(('seq', 'fsdp'))
- new_gate_up: float32 [1024, 9216], P(('seq', 'fsdp'))
- new_down: float32 [4608, 1024], P(('seq', 'fsdp'))
- next_first_gains: float32 [2, 1024], P(None, ('seq', 'fsdp'))
- next_first_taps: float32 [3, 1024], P(None, ('seq', 'fsdp'))
- next_first_in: float32 [1024, 3072], P(('seq', 'fsdp'))
- next_first_out: float32 [1024, 1024], P(('seq', 'fsdp'))
- next_first_gate_up: float32 [1024, 9216], P(('seq', 'fsdp'))
- next_first_down: float32 [4608, 1024], P(('seq', 'fsdp'))
- next_second_gains: float32 [2, 1024], P(None, ('seq', 'fsdp'))
- next_second_taps: float32 [3, 1024], P(None, ('seq', 'fsdp'))
- next_second_in: float32 [1024, 3072], P(('seq', 'fsdp'))
- next_second_out: float32 [1024, 1024], P(('seq', 'fsdp'))
- next_second_gate_up: float32 [1024, 9216], P(('seq', 'fsdp'))
- next_second_down: float32 [4608, 1024], P(('seq', 'fsdp'))
Inputs may be any that keep to these rules, and one draw needn't show every extreme that they name: doc_position[s, t] is 0 where a packed document starts (always at t = 0) and doc_position[s, t - 1] + 1 elsewhere; sequence 0 holds a single document.
All inputs are finite; a program needn't handle non-finite values.
Results may differ from a plain program's by a relative error of at most 0.012.
The roundings to bfloat16 on the way count: a program that leaves them out, or rounds other values in their place, can miss the bound.
Values may be sent and summed in bfloat16 or wider, within the bound.
A program may use at most 256 MiB of HBM per device.

v0:
```python
import jax
import jax.numpy as jnp
from jax import lax
from jax.sharding import PartitionSpec as P

STEP = 3


NORM_EPS = 1e-05
BETA_ONE = 0.9
BETA_TWO = 0.999
ADAM_EPS = 1e-08
RATE_MATRIX = 0.005
RATE_VECTOR = 0.2
DECAY = 0.1
LANES = 128


def from_behind(value, axis, steps):
    count = lax.axis_size(axis)
    first, last = (max(0, -steps), min(count, count - steps))
    return lax.ppermute(value, axis, [(source, source + steps) for source in range(first, last)])


def matmul(left, right):
    return jnp.dot(left, right, preferred_element_type=jnp.float32)


def matmul_tn(left, right):
    return lax.dot_general(
        left, right, (((0,), (0,)), ((), ())), preferred_element_type=jnp.float32
    )


def matmul_nt(left, right):
    return lax.dot_general(
        left, right, (((1,), (1,)), ((), ())), preferred_element_type=jnp.float32
    )


def inverse_rms(values):
    return lax.rsqrt(jnp.mean(values * values, axis=-1, keepdims=True) + NORM_EPS)


def norm_backward(values, scale, gain, grad_normed):
    weighted = grad_normed * gain
    grad_gain = jnp.sum(grad_normed * values * scale, axis=0)
    cubed = scale * scale * scale
    grad_values = scale * weighted - values * cubed * jnp.mean(
        weighted * values, axis=-1, keepdims=True
    )
    return (grad_values, grad_gain)


def adamw_update(param, grad, first, second, rate, decay):
    first_new = BETA_ONE * first + (1.0 - BETA_ONE) * grad
    second_new = BETA_TWO * second + (1.0 - BETA_TWO) * grad * grad
    first_hat = first_new / (1.0 - BETA_ONE**STEP)
    second_hat = second_new / (1.0 - BETA_TWO**STEP)
    param_new = param - rate * (first_hat / (jnp.sqrt(second_hat) + ADAM_EPS) + decay * param)
    return (param_new, first_new, second_new)


def local(
    hidden_in,
    cotangent,
    doc_position,
    norm_gains,
    conv_taps,
    in_proj,
    out_proj,
    gate_up,
    down_proj,
    first_gains,
    first_taps,
    first_in,
    first_out,
    first_gate_up,
    first_down,
    second_gains,
    second_taps,
    second_in,
    second_out,
    second_gate_up,
    second_down,
):
    half = jnp.bfloat16
    single = jnp.float32
    row_count, length, width = hidden_in.shape
    tok_count = row_count * length
    axes = ("seq", "fsdp")
    in_width = in_proj.shape[1]
    out_width = out_proj.shape[1]
    vectors = jnp.concatenate([norm_gains, conv_taps], axis=0).T.astype(half)
    packed = jnp.concatenate(
        [
            in_proj.astype(half),
            out_proj.astype(half),
            jnp.pad(vectors, ((0, 0), (0, LANES - vectors.shape[1]))),
        ],
        axis=1,
    )
    packed_full = lax.all_gather(packed, axes, axis=0, tiled=True)
    in_full = packed_full[:, :in_width]
    out_full = packed_full[:, in_width : in_width + out_width]
    vectors_full = packed_full[:, in_width + out_width :].astype(single).T
    mixer_full = (None, None, in_full, out_full)
    gains_f = vectors_full[:2]
    taps_f = vectors_full[2:5]
    resid_one = hidden_in.reshape(tok_count, width).astype(single)
    scale_one = inverse_rms(resid_one)
    normed_one = (resid_one * scale_one * gains_f[0]).astype(half)
    projected = matmul(normed_one, mixer_full[2])
    b_branch = projected[:, :width]
    c_branch = projected[:, width : 2 * width]
    x_branch = projected[:, 2 * width :]
    gated_input = (b_branch * x_branch).astype(half)
    gated_rows = gated_input.reshape(row_count, length, width)
    carried = from_behind(gated_rows[:, length - 2 :, :], "seq", 1)
    extended = jnp.concatenate([carried, gated_rows], axis=1).astype(single)
    gated_f = extended[:, 2:].reshape(tok_count, width)
    prev_one = extended[:, 1 : length + 1].reshape(tok_count, width)
    prev_two = extended[:, :length].reshape(tok_count, width)
    positions = doc_position.reshape(tok_count)
    mask_one = (positions >= 1).astype(single)[:, None]
    mask_two = (positions >= 2).astype(single)[:, None]
    conv_out = (
        taps_f[0] * gated_f + mask_one * taps_f[1] * prev_one + mask_two * taps_f[2] * prev_two
    )
    mixer_act = (c_branch * conv_out).astype(half)
    resid_two = resid_one + matmul(mixer_act, mixer_full[3])
    scale_two = inverse_rms(resid_two)
    normed_two = (resid_two * scale_two * gains_f[1]).astype(half)
    ffn_full = (
        lax.all_gather(gate_up.astype(half), ("seq", "fsdp"), axis=0, tiled=True),
        lax.all_gather(down_proj.astype(half), ("seq", "fsdp"), axis=0, tiled=True),
    )
    hidden_units = ffn_full[0].shape[1] // 2
    ffn_pre = matmul(normed_two, ffn_full[0])
    gate_pre = ffn_pre[:, :hidden_units]
    up_pre = ffn_pre[:, hidden_units:]
    sigmoid_gate = jax.nn.sigmoid(gate_pre)
    silu_gate = gate_pre * sigmoid_gate
    ffn_act = (silu_gate * up_pre).astype(half)
    block_out = resid_two + matmul(ffn_act, ffn_full[1])
    cot_rows = cotangent.reshape(tok_count, width)
    grad_act = matmul_nt(cot_rows, ffn_full[1])
    grad_gate = grad_act * up_pre * sigmoid_gate * (1.0 + gate_pre * (1.0 - sigmoid_gate))
    grad_both = jnp.concatenate([grad_gate, grad_act * silu_gate], axis=1).astype(half)
    grad_normed = matmul_nt(grad_both, ffn_full[0])
    grad_down = matmul_tn(ffn_act, cot_rows)
    grad_gate_up = matmul_tn(normed_two, grad_both)
    norm_part, gain_two_grad = norm_backward(resid_two, scale_two, gains_f[1], grad_normed)
    grad_resid = cot_rows.astype(single) + norm_part
    resid_cast = grad_resid.astype(half)
    grad_mixer = matmul_nt(resid_cast, mixer_full[3])
    grad_cbranch = grad_mixer * conv_out
    grad_conv = grad_mixer * c_branch
    masked_one = mask_one * grad_conv
    masked_two = mask_two * grad_conv
    grad_taps = jnp.stack(
        [
            jnp.sum(grad_conv * gated_f, axis=0),
            jnp.sum(masked_one * prev_one, axis=0),
            jnp.sum(masked_two * prev_two, axis=0),
        ]
    )
    one_rows = masked_one.reshape(row_count, length, width)
    two_rows = masked_two.reshape(row_count, length, width)
    leading = from_behind((one_rows[:, :2, :], two_rows[:, :2, :]), "seq", -1)
    ext_one = jnp.concatenate([one_rows, leading[0]], axis=1)
    ext_two = jnp.concatenate([two_rows, leading[1]], axis=1)
    next_one = ext_one[:, 1 : length + 1].reshape(tok_count, width)
    next_two = ext_two[:, 2 : length + 2].reshape(tok_count, width)
    grad_gated = taps_f[0] * grad_conv + taps_f[1] * next_one + taps_f[2] * next_two
    grad_proj = jnp.concatenate(
        [grad_gated * x_branch, grad_cbranch, grad_gated * b_branch], axis=1
    ).astype(half)
    grad_normone = matmul_nt(grad_proj, mixer_full[2])
    first_part, gain_one_grad = norm_backward(resid_one, scale_one, gains_f[0], grad_normone)
    grad_hidden = grad_resid + first_part
    grad_gains = jnp.stack([gain_one_grad, gain_two_grad])
    grad_in = matmul_tn(normed_one, grad_proj)
    grad_out = matmul_tn(mixer_act, resid_cast)
    vector_grads = jnp.concatenate([grad_gains, grad_taps], axis=0)
    vector_count = vector_grads.shape[0]
    grad_sent = jnp.concatenate(
        [
            grad_gate_up.astype(half),
            grad_down.astype(half).reshape(width, -1),
            grad_in.astype(half),
            grad_out.astype(half),
            jnp.pad(vector_grads.T, ((0, 0), (0, LANES - vector_count))).astype(half),
        ],
        axis=1,
    )
    grad_owned = lax.psum_scatter(grad_sent, axes, scatter_dimension=0, tiled=True).astype(single)
    ends = [grad_gate_up.shape[1]]
    for columns in (grad_down.size // width, in_width, out_width):
        ends.append(ends[-1] + columns)
    vector_owned = grad_owned[:, ends[3] : ends[3] + vector_count].T
    owned = (
        vector_owned[:2],
        vector_owned[2:],
        grad_owned[:, ends[1] : ends[2]],
        grad_owned[:, ends[2] : ends[3]],
        grad_owned[:, : ends[0]],
        grad_owned[:, ends[0] : ends[1]].reshape(down_proj.shape),
    )
    params = (norm_gains, conv_taps, in_proj, out_proj, gate_up, down_proj)
    firsts = (first_gains, first_taps, first_in, first_out, first_gate_up, first_down)
    seconds = (second_gains, second_taps, second_in, second_out, second_gate_up, second_down)
    rates = (RATE_VECTOR, RATE_VECTOR, RATE_MATRIX, RATE_MATRIX, RATE_MATRIX, RATE_MATRIX)
    decays = (0.0, 0.0, DECAY, DECAY, DECAY, DECAY)
    updated = [
        adamw_update(
            params[index], owned[index], firsts[index], seconds[index], rates[index], decays[index]
        )
        for index in range(6)
    ]
    out_rows = block_out.reshape(row_count, length, width)
    grad_rows = grad_hidden.reshape(row_count, length, width)
    return (
        out_rows,
        grad_rows,
        owned[0],
        owned[1],
        owned[2],
        owned[3],
        owned[4],
        owned[5],
        updated[0][0],
        updated[1][0],
        updated[2][0],
        updated[3][0],
        updated[4][0],
        updated[5][0],
        updated[0][1],
        updated[1][1],
        updated[2][1],
        updated[3][1],
        updated[4][1],
        updated[5][1],
        updated[0][2],
        updated[1][2],
        updated[2][2],
        updated[3][2],
        updated[4][2],
        updated[5][2],
    )


def solution(mesh):
    in_specs = (
        P("fsdp", "seq", None),
        P("fsdp", "seq", None),
        P("fsdp", "seq"),
        P(None, ("seq", "fsdp")),
        P(None, ("seq", "fsdp")),
        P(("seq", "fsdp"), None),
        P(("seq", "fsdp"), None),
        P(("seq", "fsdp"), None),
        P(("seq", "fsdp"), None),
        P(None, ("seq", "fsdp")),
        P(None, ("seq", "fsdp")),
        P(("seq", "fsdp"), None),
        P(("seq", "fsdp"), None),
        P(("seq", "fsdp"), None),
        P(("seq", "fsdp"), None),
        P(None, ("seq", "fsdp")),
        P(None, ("seq", "fsdp")),
        P(("seq", "fsdp"), None),
        P(("seq", "fsdp"), None),
        P(("seq", "fsdp"), None),
        P(("seq", "fsdp"), None),
    )
    out_specs = (
        P("fsdp", "seq", None),
        P("fsdp", "seq", None),
        P(None, ("seq", "fsdp")),
        P(None, ("seq", "fsdp")),
        P(("seq", "fsdp"), None),
        P(("seq", "fsdp"), None),
        P(("seq", "fsdp"), None),
        P(("seq", "fsdp"), None),
        P(None, ("seq", "fsdp")),
        P(None, ("seq", "fsdp")),
        P(("seq", "fsdp"), None),
        P(("seq", "fsdp"), None),
        P(("seq", "fsdp"), None),
        P(("seq", "fsdp"), None),
        P(None, ("seq", "fsdp")),
        P(None, ("seq", "fsdp")),
        P(("seq", "fsdp"), None),
        P(("seq", "fsdp"), None),
        P(("seq", "fsdp"), None),
        P(("seq", "fsdp"), None),
        P(None, ("seq", "fsdp")),
        P(None, ("seq", "fsdp")),
        P(("seq", "fsdp"), None),
        P(("seq", "fsdp"), None),
        P(("seq", "fsdp"), None),
        P(("seq", "fsdp"), None),
    )
    return jax.shard_map(local, mesh=mesh, in_specs=in_specs, out_specs=out_specs, check_vma=False)
```

profile of v0, /device:TPU:0, one launch (start us, length us, event | category | flops | bytes accessed | tf_op | source)
XLA Modules:
  0.0 812.8 jit_solution(17906408216686123920)
XLA Ops:
  15.8 77.0 %all-gather.4.cloned.1.call-done = bf16[1024,4224]{1,0:T(8,128)(2,1)} async-done(((bf16[32,4224]{1,0:T(8,128)(2,1)}), bf16[1024,4224]{1,0:T(8,128)(2,1)}) %all-gather.4.cloned.1.call-update) | async-done | bytes 8650768 | tf_op jit(solution)/shard_map/all_gather | solution.py:103
  95.2 4.7 fusion.2
  107.2 112.3 %all-gather.6.cloned.1.call-done = bf16[1024,9216]{1,0:T(8,128)(2,1)} async-done(((bf16[32,9216]{1,0:T(8,128)(2,1)}), bf16[1024,9216]{1,0:T(8,128)(2,1)}) %all-gather.6.cloned.1.call-update) | async-done | bytes 18874384 | tf_op jit(solution)/shard_map/all_gather | solution.py:135
  219.6 14.4 %fusion.49 = f32[256,9216]{1,0:T(8,128)} fusion(bf16[1024,9216]{1,0:T(8,128)(2,1)} %all-gather.6.cloned.1.call-done, f32[256,1024]{1,0:T(8,128)S(1)} %get-tuple-element.232, f32[1024]{0:T(1024)S(1)} %get-tuple-element.189, f32[256]{0:T(256)S(1)} %get-tuple-element.228), kind=kOutput, calls=%fused_computation.122 | convolution fusion | flops 4832624640 | bytes 29365248 | tf_op jit(solution)/shard_map/dot_general | solution.py:26
  234.0 69.2 %all-gather.8.cloned.1.call-done = bf16[4608,1024]{1,0:T(8,128)(2,1)} async-done(((bf16[144,1024]{1,0:T(8,128)(2,1)}), bf16[4608,1024]{1,0:T(8,128)(2,1)}) %all-gather.8.cloned.1.call-update) | async-done | bytes 9437200 | tf_op jit(solution)/shard_map/all_gather | solution.py:136
  303.2 14.1 %multiply_convert_fusion.1 = (bf16[256,4608]{1,0:T(8,128)(2,1)}, bf16[256,4608]{1,0:T(8,128)(2,1)}, bf16[256,4608]{1,0:T(8,128)(2,1)}) fusion(f32[256,9216]{1,0:T(8,128)} %fusion.49, bf16[4608,1024]{1,0:T(8,128)(2,1)} %all-gather.8.cloned.1.call-done, bf16[1,256,1024]{2,1,0:T(8,128)(2,1)S(1)} %copy-done.14), kind=kOutput, calls=%fused_computation.13 | convolution fusion | flops 2433613824 | bytes 26476544 | tf_op jit(solution)/shard_map/dot_general | solution.py:36
  317.3 11.6 %convert_dynamic-update-slice_fusion = bf16[1024,18048]{1,0:T(8,128)(2,1)} fusion(bf16[256,4608]{1,0:T(8,128)(2,1)} %get-tuple-element.220, bf16[256,4608]{1,0:T(8,128)(2,1)} %get-tuple-element.219, f32[256,1024]{1,0:T(8,128)S(1)} %get-tuple-element.232, f32[1024]{0:T(1024)S(1)} %get-tuple-element.189, f32[256]{0:T(256)S(1)} %get-tuple-element.228), kind=kOutput, calls=%fused_computation | convolution fusion | flops 4851499008 | bytes 24646656 | tf_op jit(solution)/shard_map/dot_general | solution.py:30
  328.9 10.6 %multiply_reduce_fusion.3 = (bf16[1024]{0:T(1024)(128)(2,1)S(1)}, f32[256]{0:T(256)S(1)}, f32[256,1024]{1,0:T(8,128)S(1)}) fusion(f32[256,1024]{1,0:T(8,128)S(1)} %get-tuple-element.232, f32[256]{0:T(256)S(1)} %get-tuple-element.228, f32[1024]{0:T(1024)S(1)} %get-tuple-element.189, bf16[1024,9216]{1,0:T(8,128)(2,1)} %all-gather.6.cloned.1.call-done, ...), kind=kOutput, calls=%fused_computation.60 | convolution fusion | flops 4842847232 | bytes 25698304 | tf_op jit(solution)/shard_map/dot_general | solution.py:36
  348.7 5.2 convolution_convert_fusion
  353.9 17.5 %reshape.194 = bf16[1024,4608]{1,0:T(8,128)(2,1)} reshape(bf16[4608,1024]{1,0:T(8,128)(2,1)} %convolution_convert_fusion) | data formatting | bytes 18874368 | tf_op jit(solution)/shard_map/reshape | solution.py:190
  371.4 8.0 constant_dynamic-update-slice_fusion
  383.3 4.6 convert_dynamic-update-slice_fusion.1
  405.9 3.2 copy.205
  409.0 4.2 copy.206
  413.3 9.9 %fusion.14 = f32[1,256,1024]{2,1,0:T(8,128)} fusion(f32[256,1024]{1,0:T(8,128)S(1)} %copy-done.6, bf16[256,4608]{1,0:T(8,128)(2,1)} %get-tuple-element.221, bf16[4608,1024]{1,0:T(8,128)(2,1)} %all-gather.8.cloned.1.call-done), kind=kOutput, calls=%fused_computation.35 | convolution fusion | flops 2416181248 | bytes 13893632 | tf_op jit(solution)/shard_map/dot_general | solution.py:26
  424.4 313.8 %reduce-scatter.4.cloned.1.call-done = bf16[32,18048]{1,0:T(8,128)(2,1)} async-done(((bf16[1024,18048]{1,0:T(8,128)(2,1)}), bf16[32,18048]{1,0:T(8,128)(2,1)}) %reduce-scatter.4.cloned.1.call-update) | async-done | bytes 1155088
  738.2 4.9 copy.223
  743.1 3.6 convert_element_type.120
  755.7 3.8 copy.211
  761.1 5.2 multiply_subtract_fusion.1
  773.7 12.9 %multiply_subtract_fusion = (f32[32,9216]{0,1:T(8,128)}, f32[32,9216]{0,1:T(8,128)}, f32[32,9216]{0,1:T(8,128)}) fusion(f32[32,9216]{0,1:T(8,128)} %copy.208, f32[32,18048]{0,1:T(8,128)} %copy-done.1, f32[32,9216]{0,1:T(8,128)} %copy.205, f32[32,9216]{0,1:T(8,128)} %copy.206), kind=kLoop, calls=%fused_computation.10 | loop fusion | flops 4423680 | bytes 8257536 | tf_op jit(solution)/shard_map/sub | solution.py:60
  786.6 3.8 copy.214
  793.5 3.8 copy.217
  799.5 3.8 copy.220
  (162 shorter events, 76.1 us)
Async XLA Ops:
  7.2 8.4 %copy-start.16 = (bf16[1,256,1024]{2,1,0:T(8,128)(2,1)S(1)}, bf16[1,256,1024]{2,1,0:T(8,128)(2,1)}, u32[]{:S(2)}) copy-start(bf16[1,256,1024]{2,1,0:T(8,128)(2,1)} %param.21) | copy-start | bytes 1572868
  7.2 85.7 %all-gather.4.cloned.1.call-start = ((), (), s32[]{:S(2)}) async-start(), calls=%async_computation.1 | async-start | bytes 8921088 | tf_op jit(solution)/shard_map/all_gather | solution.py:103
  11.5 208.1 %all-gather.6.cloned.1.call-start = ((), (), s32[]{:S(2)}) async-start(), calls=%async_computation.2 | async-start | bytes 19464192 | tf_op jit(solution)/shard_map/all_gather | solution.py:135
  13.7 289.5 %all-gather.8.cloned.1.call-start = ((), (), s32[]{:S(2)}) async-start(), calls=%async_computation.3 | async-start | bytes 9732096 | tf_op jit(solution)/shard_map/all_gather | solution.py:136
  15.6 722.6 %reduce-scatter.4.cloned.1.call-start = ((), (), s32[]{:S(2)}) async-start(), calls=%async_computation.4 | async-start | bytes 38117376
  95.2 7.0 copy-start.33
  100.0 3.0 collective-permute-start
  104.6 129.3 %copy-start.11 = (bf16[256,1024]{1,0:T(8,128)(2,1)}, bf16[256,1024]{1,0:T(8,128)(2,1)S(1)}, u32[]{:S(2)}) copy-start(bf16[256,1024]{1,0:T(8,128)(2,1)S(1)} %get-tuple-element.217) | copy-start | bytes 1572868
  107.2 232.3 %copy-start.5 = (f32[256,1024]{1,0:T(8,128)}, f32[256,1024]{1,0:T(8,128)S(1)}, u32[]{:S(2)}) copy-start(f32[256,1024]{1,0:T(8,128)S(1)} %get-tuple-element.232) | copy-start | bytes 3145732
  219.6 83.6 %copy-start.14 = (bf16[1,256,1024]{2,1,0:T(8,128)(2,1)S(1)}, bf16[1,256,1024]{2,1,0:T(8,128)(2,1)}, u32[]{:S(2)}) copy-start(bf16[1,256,1024]{2,1,0:T(8,128)(2,1)} %param.22) | copy-start | bytes 1572868
  328.9 10.6 %copy-start.15 = (bf16[1,256,1024]{2,1,0:T(8,128)(2,1)S(1)}, bf16[1,256,1024]{2,1,0:T(8,128)(2,1)}, u32[]{:S(2)}) copy-start(bf16[1,256,1024]{2,1,0:T(8,128)(2,1)} %param.22) | copy-start | bytes 1572868
  346.1 33.4 %collective-permute-start.2 = (f32[1,2,1024]{2,1,0:T(2,128)S(1)}, f32[1,2,1024]{2,1,0:T(2,128)S(1)}, u32[]{:S(2)}, u32[]{:S(2)}) collective-permute-start(f32[1,2,1024]{2,1,0:T(2,128)S(1)} %slice.142), channel_id=1, source_target_pairs={{4,0},{8,4},{12,8},{16,12},{20,16},{24,20},{28,24},{5,1},{9,5},{13... | collective-permute-start | bytes 24584 | tf_op jit(solution)/shard_map/ppermute | solution.py:22
  347.4 32.1 %collective-permute-start.1 = (f32[1,2,1024]{2,1,0:T(2,128)S(1)}, f32[1,2,1024]{2,1,0:T(2,128)S(1)}, u32[]{:S(2)}, u32[]{:S(2)}) collective-permute-start(f32[1,2,1024]{2,1,0:T(2,128)S(1)} %slice.141), channel_id=1, source_target_pairs={{4,0},{8,4},{12,8},{16,12},{20,16},{24,20},{28,24},{5,1},{9,5},{13... | collective-permute-start | bytes 24584 | tf_op jit(solution)/shard_map/ppermute | solution.py:22
  379.5 10.5 %slice-start = ((s8[8650752]{0:T(1024)(128)(4,1)}), s8[4194304]{0:T(1024)(128)(4,1)S(1)}, s32[]{:S(2)}) async-start(s8[8650752]{0:T(1024)(128)(4,1)} %bitcast.84), calls=%async_computation.5 | async-start | bytes 8388608
  381.7 8.3 %slice-start.1 = ((s8[8650752]{0:T(1024)(128)(4,1)}), s8[4194304]{0:T(1024)(128)(4,1)S(1)}, s32[]{:S(2)}) async-start(s8[8650752]{0:T(1024)(128)(4,1)} %bitcast.84), calls=%async_computation.6 | async-start | bytes 8388608
  383.3 6.7 slice-start.2
  397.7 7.2 copy-start.29
  405.9 7.4 copy-start.6
  413.3 9.9 %copy-start.18 = (bf16[1,256,1024]{2,1,0:T(8,128)(2,1)S(1)}, bf16[1,256,1024]{2,1,0:T(8,128)(2,1)}, u32[]{:S(2)}) copy-start(bf16[1,256,1024]{2,1,0:T(8,128)(2,1)} %param.21) | copy-start | bytes 1572868
  413.3 9.9 %copy-start.21 = (f32[256,1024]{1,0:T(8,128)S(1)}, f32[256,1024]{1,0:T(8,128)}, u32[]{:S(2)}) copy-start(f32[256,1024]{1,0:T(8,128)} %get-tuple-element.234) | copy-start | bytes 3145732
  791.6 7.0 copy-start.13
  797.4 6.5 copy-start.30
  797.4 7.1 copy-start.9
  797.4 7.1 copy-start.10
  (23 other events, 108.9 us)
Sparse Core Ops, SparseCore 0:
  11.6 81.2 all-gather.3
  96.3 123.2 all-gather.5
  222.9 80.1 all-gather.7
  394.2 344.0 reduce-scatter.3
where the time goes:
time: 818 us; the launch traced here: 813 us
  waiting for transfers between devices  573 us (70%)
  local copies, waits for them, and re-layouts  88.7 us (11%)
  matrix products  85 us (10%)
  other arithmetic  46.5 us (6%)
  between operations  14.5 us (2%)
    unnamed x5, waiting for transfers between devices  314 us
    all_gather x1, waiting for transfers between devices, local(): lax.all_gather(gate_up.astype(half), ('seq', 'fsdp'), axis=0, tiled=True)  112 us
    all_gather x1, waiting for transfers between devices, local(): packed_full = lax.all_gather(packed, axes, axis=0, tiled=True)  77 us
    all_gather x1, waiting for transfers between devices, local(): lax.all_gather(down_proj.astype(half), ('seq', 'fsdp'), axis=0, tiled=True)  69.2 us
    unnamed x104, local copies, waits for them, and re-layouts  62.8 us
    dot_general x4, matrix products, matmul(): return jnp.dot(left, right, preferred_element_type=jnp.float32)  31.5 us
    dot_general x4, matrix products, matmul_nt(): lax.dot_general(left, right, (((1,), (1,)), ((), ())), preferred_element_...  30 us
    sub x6, other arithmetic, adamw_update(): param - rate * (first_hat / (jnp.sqrt(second_hat) + ADAM_EPS) + decay * p...  23.7 us
  transfers between devices with their start and end apart: 7, of which 5 were waited for; matrix products, arithmetic and copies ran while one was open for 11% of the time, Pallas kernels for 0%

commit v1 on v0

--- a/solution.py
+++ b/solution.py
@@ -1,6 +1,11 @@
+import functools
+
 import jax
 import jax.numpy as jnp
 from jax import lax
+from jax.experimental import pallas as pl
+from jax.experimental.pallas import tpu as pltpu
+from jax.sharding import Mesh
 from jax.sharding import PartitionSpec as P
 
 STEP = 3
@@ -14,6 +19,331 @@
 RATE_VECTOR = 0.2
 DECAY = 0.1
 LANES = 128
+MESH_ID = pl.DeviceIdType.MESH
+SEQ = ("ring", "core")
+ALL = ("ring", "core", "fsdp")
+
+
+def snake(index):
+    return 2 * (index // 2) + (index % 2 + index // 2) % 2
+
+
+def halves(columns):
+    first = (columns // 2 + LANES - 1) // LANES * LANES
+    return (pl.ds(0, first), pl.ds(first, columns - first))
+
+
+class Place:
+    def __init__(self, chips, depth):
+        self.chips, self.depth = chips, depth
+        self.core = lax.axis_index("core")
+        self.layer = lax.axis_index("fsdp")
+        self.spot = snake(lax.axis_index("ring"))
+        self.own = lax.axis_index("ring")
+        self.right = self.device(snake((self.spot + 1) % chips), self.core, self.layer)
+        self.left = self.device(snake((self.spot + chips - 1) % chips), self.core, self.layer)
+        self.up = self.device(self.own, self.core, (self.layer + 1) % depth)
+        self.down = self.device(self.own, self.core, (self.layer + depth - 1) % depth)
+        self.sibling = self.device(self.own, 1 - self.core, self.layer)
+
+    def device(self, ring, core, layer):
+        return (ring, core, layer)
+
+    def shard(self, spot, core, layer):
+        return (snake(spot) * 2 + core) * self.depth + layer
+
+    def greet(self):
+        barrier = pltpu.get_barrier_semaphore()
+        for device in (self.right, self.left, self.up, self.down, self.sibling):
+            pl.semaphore_signal(barrier, inc=1, device_id=device, device_id_type=MESH_ID)
+        pl.semaphore_wait(barrier, 5)
+
+
+def gather_kernel(chips, depth, count, *refs):
+    shards = refs[:count]
+    wholes = refs[count : 2 * count]
+    sent, from_sibling, from_below, from_ring, kept = refs[2 * count :]
+    here = Place(chips, depth)
+    here.greet()
+    cuts = [halves(ref.shape[1]) for ref in shards]
+
+    def block(which, shard):
+        return wholes[which].at[shard]
+
+    def piece_of(which, shard, way):
+        return wholes[which].at[shard, :, cuts[which][way]]
+
+    def send(source, target, which, arrived, device):
+        pltpu.make_async_remote_copy(
+            src_ref=source,
+            dst_ref=target,
+            send_sem=sent.at[which],
+            recv_sem=arrived,
+            device_id=device,
+            device_id_type=MESH_ID,
+        ).start()
+
+    def awaited(ref, arrived):
+        pltpu.make_async_copy(ref, ref, arrived).wait()
+
+    own = here.shard(here.spot, here.core, here.layer)
+    for which in range(count):
+        send(shards[which], block(which, own), which, from_below.at[which, 0], here.up)
+        for way in range(2):
+            send(
+                shards[which].at[:, cuts[which][way]],
+                piece_of(which, own, way),
+                which,
+                from_ring.at[which, way, 0],
+                (here.right, here.left)[way],
+            )
+        send(shards[which], block(which, own), which, from_sibling.at[which], here.sibling)
+        pltpu.make_async_copy(shards[which], block(which, own), kept.at[which]).start()
+
+    def around(hop, layer_step):
+        layer = (here.layer + depth - layer_step) % depth
+        for which in range(count):
+            for way in range(2):
+                away = (chips - hop, hop)[way]
+                shard = here.shard((here.spot + away) % chips, here.core, layer)
+                arrived = layer_step * (chips - 1) + hop - 1
+                piece = piece_of(which, shard, way)
+                awaited(piece, from_ring.at[which, way, arrived])
+                if hop < chips - 1:
+                    send(
+                        piece,
+                        piece,
+                        which,
+                        from_ring.at[which, way, arrived + 1],
+                        (here.right, here.left)[way],
+                    )
+                send(piece, piece, which, from_sibling.at[which], here.sibling)
+
+    def layer_arrives(layer_step):
+        layer = (here.layer + depth - layer_step) % depth
+        shard = here.shard(here.spot, here.core, layer)
+        for which in range(count):
+            whole = block(which, shard)
+            awaited(whole, from_below.at[which, layer_step - 1])
+
+            @pl.when(layer_step < depth - 1)
+            def _():
+                send(whole, whole, which, from_below.at[which, layer_step], here.up)
+
+            for way in range(2):
+                piece = piece_of(which, shard, way)
+                send(
+                    piece,
+                    piece,
+                    which,
+                    from_ring.at[which, way, layer_step * (chips - 1)],
+                    (here.right, here.left)[way],
+                )
+            send(whole, whole, which, from_sibling.at[which], here.sibling)
+
+    @pl.loop(0, depth)
+    def _(layer_step):
+        for hop in range(1, chips - 1):
+            around(hop, layer_step)
+
+        @pl.when(layer_step < depth - 1)
+        def _():
+            layer_arrives(layer_step + 1)
+
+        around(chips - 1, layer_step)
+
+    shard_count = 2 * chips * depth
+    for which in range(count):
+        pltpu.make_async_copy(shards[which], block(which, own), kept.at[which]).wait()
+        awaited(wholes[which].at[pl.ds(0, shard_count // 2)], from_sibling.at[which])
+        awaited(wholes[which].at[pl.ds(0, shard_count - 1)], sent.at[which])
+
+
+def gather(chips, depth, *shards):
+    count = len(shards)
+    steps = depth * (chips - 1)
+    anywhere = pl.BlockSpec(memory_space=pl.ANY)
+    shard_count = 2 * chips * depth
+    wholes = pl.pallas_call(
+        functools.partial(gather_kernel, chips, depth, count),
+        out_shape=[jax.ShapeDtypeStruct((shard_count,) + x.shape, x.dtype) for x in shards],
+        in_specs=[anywhere] * count,
+        out_specs=[anywhere] * count,
+        scratch_shapes=[
+            pltpu.SemaphoreType.DMA((count,)),
+            pltpu.SemaphoreType.DMA((count,)),
+            pltpu.SemaphoreType.DMA((count, depth - 1)),
+            pltpu.SemaphoreType.DMA((count, 2, steps)),
+            pltpu.SemaphoreType.DMA((count,)),
+        ],
+        compiler_params=pltpu.CompilerParams(collective_id=0, has_side_effects=True),
+        name="gather_weights",
+    )(*shards)
+    return [x.reshape(-1, x.shape[2]) for x in wholes]
+
+
+def scatter_kernel(chips, depth, count, *refs):
+    grads = refs[:count]
+    owned = refs[count : 2 * count]
+    rest = refs[2 * count :]
+    theirs = rest[:count]
+    staged = rest[count : 2 * count]
+    ringed = rest[2 * count : 3 * count]
+    layered = rest[3 * count : 4 * count]
+    sent, loaded, from_sibling, from_below, from_ring = rest[4 * count :]
+    here = Place(chips, depth)
+    cuts = [halves(ref.shape[1]) for ref in owned]
+    f32 = jnp.float32
+
+    def place(hop, way):
+        away = (chips - hop, hop)[way]
+        return (here.spot + away) % chips
+
+    def layer_of(layer_step):
+        return (here.layer + 2 * depth - 1 - layer_step) % depth
+
+    def slot_of(layer_step, hop):
+        return layer_step * chips + hop - 1
+
+    def load(which, slot, buffer, start):
+        layer_step = slot // chips
+        hop = slot % chips + 1
+        for way, cut in enumerate(cuts[which]):
+            shard = here.shard(place(hop, way), here.core, layer_of(layer_step))
+            copy = pltpu.make_async_copy(
+                grads[which].at[shard, :, cut],
+                staged[which].at[buffer, :, cut],
+                loaded.at[which, way, buffer],
+            )
+            copy.start() if start else copy.wait()
+
+    def hand_over(which, slot):
+        layer_step = slot // chips
+        hop = slot % chips + 1
+        for way, cut in enumerate(cuts[which]):
+            shard = here.shard(place(hop, way), 1 - here.core, layer_of(layer_step))
+            pltpu.make_async_remote_copy(
+                src_ref=grads[which].at[shard, :, cut],
+                dst_ref=theirs[which].at[slot, :, cut],
+                send_sem=sent.at[which],
+                recv_sem=from_sibling.at[which, way, slot],
+                device_id=here.sibling,
+                device_id_type=MESH_ID,
+            ).start()
+
+    slots = chips * depth
+    for which in range(count):
+        load(which, jnp.int32(0), jnp.int32(0), True)
+    here.greet()
+
+    @pl.loop(0, slots)
+    def _(slot):
+        for which in range(count):
+            hand_over(which, slot)
+
+    def got(ref, semaphore):
+        pltpu.make_async_copy(ref, ref, semaphore).wait()
+
+    def step(layer_step, hop):
+        slot = slot_of(layer_step, hop)
+        buffer = slot % 2
+
+        @pl.when(slot + 1 < slots)
+        def _():
+            for which in range(count):
+                load(which, slot + 1, (slot + 1) % 2, True)
+
+        for which in range(count):
+            load(which, slot, buffer, False)
+            if hop == chips:
+                @pl.when(layer_step > 0)
+                def _():
+                    ref = layered[which].at[layer_step - 1]
+                    got(ref, from_below.at[which, layer_step - 1])
+
+            for way, cut in enumerate(cuts[which]):
+                mine = theirs[which].at[slot, :, cut]
+                got(mine, from_sibling.at[which, way, slot])
+                total = mine[...].astype(f32) + staged[which][buffer, :, cut].astype(f32)
+                if hop > 1:
+                    index = layer_step * (chips - 1) + hop - 2
+                    arrived = ringed[which].at[index, :, cut]
+                    got(arrived, from_ring.at[which, way, index])
+                    total = total + arrived[...].astype(f32)
+                if hop < chips:
+                    index = layer_step * (chips - 1) + hop - 1
+                    mine[...] = total.astype(mine.dtype)
+                    pltpu.make_async_remote_copy(
+                        src_ref=mine,
+                        dst_ref=ringed[which].at[index, :, cut],
+                        send_sem=sent.at[which],
+                        recv_sem=from_ring.at[which, way, index],
+                        device_id=(here.right, here.left)[way],
+                        device_id_type=MESH_ID,
+                    ).start()
+                else:
+                    owned[which][:, cut] = total
+
+            if hop == chips:
+                @pl.when(layer_step > 0)
+                def _():
+                    owned[which][...] += layered[which][layer_step - 1].astype(f32)
+
+                @pl.when(layer_step < depth - 1)
+                def _():
+                    mine = theirs[which].at[slot]
+                    mine[...] = owned[which][...].astype(mine.dtype)
+                    pltpu.make_async_remote_copy(
+                        src_ref=mine,
+                        dst_ref=layered[which].at[layer_step],
+                        send_sem=sent.at[which],
+                        recv_sem=from_below.at[which, layer_step],
+                        device_id=here.up,
+                        device_id_type=MESH_ID,
+                    ).start()
+
+    @pl.loop(0, depth)
+    def _(layer_step):
+        for hop in range(1, chips + 1):
+            step(layer_step, hop)
+
+    for which in range(count):
+        most = grads[which].at[pl.ds(0, 2 * slots - 1)]
+        pltpu.make_async_copy(most, most, sent.at[which]).wait()
+
+
+def scatter(chips, depth, *grads):
+    count = len(grads)
+    slots = chips * depth
+    steps = depth * (chips - 1)
+    grads = [g.reshape(2 * slots, -1, g.shape[1]) for g in grads]
+    anywhere = pl.BlockSpec(memory_space=pl.ANY)
+    inner = pl.BlockSpec(memory_space=pltpu.VMEM)
+
+    def room(leading):
+        return [pltpu.VMEM((leading,) + g.shape[1:], g.dtype) for g in grads]
+
+    return pl.pallas_call(
+        functools.partial(scatter_kernel, chips, depth, count),
+        out_shape=[jax.ShapeDtypeStruct(g.shape[1:], jnp.float32) for g in grads],
+        in_specs=[anywhere] * count,
+        out_specs=[inner] * count,
+        scratch_shapes=room(slots)
+        + room(2)
+        + room(steps)
+        + room(depth - 1)
+        + [
+            pltpu.SemaphoreType.DMA((count,)),
+            pltpu.SemaphoreType.DMA((count, 2, 2)),
+            pltpu.SemaphoreType.DMA((count, 2, slots)),
+            pltpu.SemaphoreType.DMA((count, depth - 1)),
+            pltpu.SemaphoreType.DMA((count, 2, steps)),
+        ],
+        compiler_params=pltpu.CompilerParams(
+            collective_id=1, has_side_effects=True, vmem_limit_bytes=56 << 20
+        ),
+        name="scatter_gradients",
+    )(*grads)
 
 
 def from_behind(value, axis, steps):
@@ -88,7 +418,7 @@
     single = jnp.float32
     row_count, length, width = hidden_in.shape
     tok_count = row_count * length
-    axes = ("seq", "fsdp")
+    chips, depth = lax.axis_size("ring"), lax.axis_size("fsdp")
     in_width = in_proj.shape[1]
     out_width = out_proj.shape[1]
     vectors = jnp.concatenate([norm_gains, conv_taps], axis=0).T.astype(half)
@@ -97,13 +427,15 @@
             in_proj.astype(half),
             out_proj.astype(half),
             jnp.pad(vectors, ((0, 0), (0, LANES - vectors.shape[1]))),
+            gate_up.astype(half),
         ],
         axis=1,
     )
-    packed_full = lax.all_gather(packed, axes, axis=0, tiled=True)
+    packed_full, down_full = gather(chips, depth, packed, down_proj.astype(half))
     in_full = packed_full[:, :in_width]
     out_full = packed_full[:, in_width : in_width + out_width]
-    vectors_full = packed_full[:, in_width + out_width :].astype(single).T
+    vector_start = in_width + out_width
+    vectors_full = packed_full[:, vector_start : vector_start + LANES].astype(single).T
     mixer_full = (None, None, in_full, out_full)
     gains_f = vectors_full[:2]
     taps_f = vectors_full[2:5]
@@ -116,7 +448,7 @@
     x_branch = projected[:, 2 * width :]
     gated_input = (b_branch * x_branch).astype(half)
     gated_rows = gated_input.reshape(row_count, length, width)
-    carried = from_behind(gated_rows[:, length - 2 :, :], "seq", 1)
+    carried = from_behind(gated_rows[:, length - 2 :, :], SEQ, 1)
     extended = jnp.concatenate([carried, gated_rows], axis=1).astype(single)
     gated_f = extended[:, 2:].reshape(tok_count, width)
     prev_one = extended[:, 1 : length + 1].reshape(tok_count, width)
@@ -131,10 +463,7 @@
     resid_two = resid_one + matmul(mixer_act, mixer_full[3])
     scale_two = inverse_rms(resid_two)
     normed_two = (resid_two * scale_two * gains_f[1]).astype(half)
-    ffn_full = (
-        lax.all_gather(gate_up.astype(half), ("seq", "fsdp"), axis=0, tiled=True),
-        lax.all_gather(down_proj.astype(half), ("seq", "fsdp"), axis=0, tiled=True),
-    )
+    ffn_full = (packed_full[:, vector_start + LANES :], down_full)
     hidden_units = ffn_full[0].shape[1] // 2
     ffn_pre = matmul(normed_two, ffn_full[0])
     gate_pre = ffn_pre[:, :hidden_units]
@@ -167,7 +496,7 @@
     )
     one_rows = masked_one.reshape(row_count, length, width)
     two_rows = masked_two.reshape(row_count, length, width)
-    leading = from_behind((one_rows[:, :2, :], two_rows[:, :2, :]), "seq", -1)
+    leading = from_behind((one_rows[:, :2, :], two_rows[:, :2, :]), SEQ, -1)
     ext_one = jnp.concatenate([one_rows, leading[0]], axis=1)
     ext_two = jnp.concatenate([two_rows, leading[1]], axis=1)
     next_one = ext_one[:, 1 : length + 1].reshape(tok_count, width)
@@ -186,26 +515,22 @@
     vector_count = vector_grads.shape[0]
     grad_sent = jnp.concatenate(
         [
-            grad_gate_up.astype(half),
-            grad_down.astype(half).reshape(width, -1),
             grad_in.astype(half),
             grad_out.astype(half),
             jnp.pad(vector_grads.T, ((0, 0), (0, LANES - vector_count))).astype(half),
+            grad_gate_up.astype(half),
         ],
         axis=1,
     )
-    grad_owned = lax.psum_scatter(grad_sent, axes, scatter_dimension=0, tiled=True).astype(single)
-    ends = [grad_gate_up.shape[1]]
-    for columns in (grad_down.size // width, in_width, out_width):
-        ends.append(ends[-1] + columns)
-    vector_owned = grad_owned[:, ends[3] : ends[3] + vector_count].T
+    grad_owned, down_owned = scatter(chips, depth, grad_sent, grad_down.astype(half))
+    vector_owned = grad_owned[:, vector_start : vector_start + vector_count].T
     owned = (
         vector_owned[:2],
         vector_owned[2:],
-        grad_owned[:, ends[1] : ends[2]],
-        grad_owned[:, ends[2] : ends[3]],
-        grad_owned[:, : ends[0]],
-        grad_owned[:, ends[0] : ends[1]].reshape(down_proj.shape),
+        grad_owned[:, :in_width],
+        grad_owned[:, in_width:vector_start],
+        grad_owned[:, vector_start + LANES :],
+        down_owned,
     )
     params = (norm_gains, conv_taps, in_proj, out_proj, gate_up, down_proj)
     firsts = (first_gains, first_taps, first_in, first_out, first_gate_up, first_down)
@@ -251,55 +576,57 @@
 
 
 def solution(mesh):
+    tokens, depth = mesh.devices.shape
+    chip_mesh = Mesh(mesh.devices.reshape(tokens // 2, 2, depth), ALL)
     in_specs = (
-        P("fsdp", "seq", None),
-        P("fsdp", "seq", None),
-        P("fsdp", "seq"),
-        P(None, ("seq", "fsdp")),
-        P(None, ("seq", "fsdp")),
-        P(("seq", "fsdp"), None),
-        P(("seq", "fsdp"), None),
-        P(("seq", "fsdp"), None),
-        P(("seq", "fsdp"), None),
-        P(None, ("seq", "fsdp")),
-        P(None, ("seq", "fsdp")),
-        P(("seq", "fsdp"), None),
-        P(("seq", "fsdp"), None),
-        P(("seq", "fsdp"), None),
-        P(("seq", "fsdp"), None),
-        P(None, ("seq", "fsdp")),
-        P(None, ("seq", "fsdp")),
-        P(("seq", "fsdp"), None),
-        P(("seq", "fsdp"), None),
-        P(("seq", "fsdp"), None),
-        P(("seq", "fsdp"), None),
+        P("fsdp", SEQ, None),
+        P("fsdp", SEQ, None),
+        P("fsdp", SEQ),
+        P(None, ALL),
+        P(None, ALL),
+        P(ALL, None),
+        P(ALL, None),
+        P(ALL, None),
+        P(ALL, None),
+        P(None, ALL),
+        P(None, ALL),
+        P(ALL, None),
+        P(ALL, None),
+        P(ALL, None),
+        P(ALL, None),
+        P(None, ALL),
+        P(None, ALL),
+        P(ALL, None),
+        P(ALL, None),
+        P(ALL, None),
+        P(ALL, None),
     )
     out_specs = (
-        P("fsdp", "seq", None),
-        P("fsdp", "seq", None),
-        P(None, ("seq", "fsdp")),
-        P(None, ("seq", "fsdp")),
-        P(("seq", "fsdp"), None),
-        P(("seq", "fsdp"), None),
-        P(("seq", "fsdp"), None),
-        P(("seq", "fsdp"), None),
-        P(None, ("seq", "fsdp")),
-        P(None, ("seq", "fsdp")),
-        P(("seq", "fsdp"), None),
-        P(("seq", "fsdp"), None),
-        P(("seq", "fsdp"), None),
-        P(("seq", "fsdp"), None),
-        P(None, ("seq", "fsdp")),
-        P(None, ("seq", "fsdp")),
-        P(("seq", "fsdp"), None),
-        P(("seq", "fsdp"), None),
-        P(("seq", "fsdp"), None),
-        P(("seq", "fsdp"), None),
-        P(None, ("seq", "fsdp")),
-        P(None, ("seq", "fsdp")),
-        P(("seq", "fsdp"), None),
-        P(("seq", "fsdp"), None),
-        P(("seq", "fsdp"), None),
-        P(("seq", "fsdp"), None),
-    )
-    return jax.shard_map(local, mesh=mesh, in_specs=in_specs, out_specs=out_specs, check_vma=False)
+        P("fsdp", SEQ, None),
+        P("fsdp", SEQ, None),
+        P(None, ALL),
+        P(None, ALL),
+        P(ALL, None),
+        P(ALL, None),
+        P(ALL, None),
+        P(ALL, None),
+        P(None, ALL),
+        P(None, ALL),
+        P(ALL, None),
+        P(ALL, None),
+        P(ALL, None),
+        P(ALL, None),
+        P(None, ALL),
+        P(None, ALL),
+        P(ALL, None),
+        P(ALL, None),
+        P(ALL, None),
+        P(ALL, None),
+        P(None, ALL),
+        P(None, ALL),
+        P(ALL, None),
+        P(ALL, None),
+        P(ALL, None),
+        P(ALL, None),
+    )
+    return jax.shard_map(local, mesh=chip_mesh, in_specs=in_specs, out_specs=out_specs, check_vma=False)

time: 818 us -> 491 us (0.60)
  waiting for transfers between devices: 573 us -> 0.01 us
  Pallas kernels: 0 us -> 325 us
  local copies, waits for them, and re-layouts: 88.7 us -> 28.4 us
  between operations: 14.5 us -> 1.31 us
    pallas_call x0 -> x2, Pallas kernels: none -> 325 us  [the longest x1 166 us: scatter(): pl.pallas_call(functools.partial(scatter_kernel, chips, depth, count), ou...]
    unnamed x5 -> x0, waiting for transfers between devices: 314 us -> none
    all_gather x3 -> x0, waiting for transfers between devices: 259 us -> none  [the longest x1 112 us: local(): lax.all_gather(gate_up.astype(half), ('seq', 'fsdp'), axis=0, tiled=True)]
    unnamed x104 -> x102, local copies, waits for them, and re-layouts: 62.8 us -> 16.4 us
    reshape x2 -> x0, local copies, waits for them, and re-layouts: 18.5 us -> none  [the longest x1 17.5 us: local(): grad_down.astype(half).reshape(width, -1)]
    concatenate x0 -> x2, other arithmetic: none -> 18.2 us  [the longest x1 18.2 us: local(): jnp.concatenate([grad_in.astype(half), grad_out.astype(half), jnp.pad(vec...]
    sub x6, other arithmetic: 23.7 us -> 12.3 us  [adamw_update(): param - rate * (first_hat / (jnp.sqrt(second_hat) + ADAM_EPS) + decay * p...]
  transfers between devices with their start and end apart: 7 -> 3, of which waited for: 5 -> 0; matrix products, arithmetic and copies ran while one was open for 11% -> 2% of each run, Pallas kernels for 0% -> 0%
where the time goes in v1:
time: 491 us; the launch traced here: 490 us
  Pallas kernels  325 us (66%)
  matrix products  78.5 us (16%)
  other arithmetic  52 us (11%)
  local copies, waits for them, and re-layouts  28.4 us (6%)
    pallas_call x1, Pallas kernels, scatter(): pl.pallas_call(functools.partial(scatter_kernel, chips, depth, count), ou...  166 us
    pallas_call x1, Pallas kernels, gather(): pl.pallas_call(functools.partial(gather_kernel, chips, depth, count), out...  159 us
    dot_general x4, matrix products, matmul_nt(): lax.dot_general(left, right, (((1,), (1,)), ((), ())), preferred_element_...  28.2 us
    dot_general x4, matrix products, matmul(): return jnp.dot(left, right, preferred_element_type=jnp.float32)  27.1 us
    dot_general x4, matrix products, matmul_tn(): lax.dot_general(left, right, (((0,), (0,)), ((), ())), preferred_element_...  23.2 us
    concatenate x1, other arithmetic, local(): jnp.concatenate([grad_in.astype(half), grad_out.astype(half), jnp.pad(vec...  18.2 us
    unnamed x102, local copies, waits for them, and re-layouts  16.4 us
    sub x6, other arithmetic, adamw_update(): param - rate * (first_hat / (jnp.sqrt(second_hat) + ADAM_EPS) + decay * p...  12.3 us
  transfers between devices with their start and end apart: 3, of which 0 were waited for; matrix products, arithmetic and copies ran while one was open for 2% of the time, Pallas kernels for 0%

profile of v1, /device:TPU:0, one launch (start us, length us, event | category | flops | bytes accessed | tf_op | source)
XLA Modules:
  0.0 489.7 jit_solution(16828263038225487122)
XLA Ops:
  5.6 1.8 convert_element_type.100.refs_1_
  8.3 159.0 %gather_weights.1 = (bf16[32,32,13440]{2,1,0:T(8,128)(2,1)}, bf16[32,144,1024]{2,1,0:T(8,128)(2,1)}) custom-call(bf16[32,13440]{1,0:T(8,128)(2,1)} %fusion.40.refs_0_, bf16[144,1024]{1,0:T(8,128)(2,1)} %convert_element_type.100.refs_1_), custom_call_target="tpu_custom_call" | custom-call | tf_op jit(solution)/shard_map/gather_weights/pallas_call | solution.py:167
  169.4 4.9 fusion.10
  175.4 2.3 collective-permute-start
  186.1 2.6 multiply_reduce_fusion.5
  188.7 11.6 %fusion.6 = f32[256,9216]{1,0:T(8,128)} fusion(bf16[1024,13440]{1,0:T(8,128)(2,1)} %bitcast.100, f32[256,1024]{1,0:T(8,128)S(1)} %get-tuple-element.196, f32[1024]{0:T(1024)S(1)} %bitcast.93, f32[256]{0:T(256)S(1)} %get-tuple-element.192), kind=kOutput, calls=%fused_computation.9 | convolution fusion | flops 4832624640 | bytes 29365248 | tf_op jit(solution)/shard_map/dot_general | solution.py:356
  200.3 8.8 %multiply_convert_fusion.1 = (bf16[256,4608]{1,0:T(8,128)(2,1)}, bf16[256,4608]{1,0:T(8,128)(2,1)}, bf16[256,4608]{1,0:T(8,128)(2,1)}) fusion(f32[256,9216]{1,0:T(8,128)} %fusion.6, bf16[4608,1024]{1,0:T(8,128)(2,1)S(1)} %bitcast.124, bf16[1,256,1024]{2,1,0:T(8,128)(2,1)S(1)} %copy-done.11), kind=kOutput, calls=%fused_computation.20 | convolution fusion | flops 2433613824 | bytes 26476544 | tf_op jit(solution)/shard_map/dot_general | solution.py:366
  209.2 11.3 %multiply_reduce_fusion.3 = (bf16[1024]{0:T(1024)(128)(2,1)S(1)}, f32[256]{0:T(256)S(1)}, f32[256,1024]{1,0:T(8,128)}) fusion(f32[256,1024]{1,0:T(8,128)S(1)} %get-tuple-element.196, f32[256]{0:T(256)S(1)} %get-tuple-element.192, f32[1024]{0:T(1024)S(1)} %bitcast.94, bf16[1024,13440]{1,0:T(8,128)(2,1)} %bitcast.101, ...), kind=kOutput, calls=%fused_computation.70 | convolution fusion | flops 4842847232 | bytes 25698304 | tf_op jit(solution)/shard_map/dot_general | solution.py:366
  220.4 11.5 %convolution_convert_fusion = bf16[1024,9216]{1,0:T(8,128)(2,1)} fusion(bf16[256,4608]{1,0:T(8,128)(2,1)} %get-tuple-element.173, bf16[256,4608]{1,0:T(8,128)(2,1)} %get-tuple-element.172, f32[256,1024]{1,0:T(8,128)S(1)} %get-tuple-element.196, f32[1024]{0:T(1024)S(1)} %bitcast.95, f32[256]{0:T(256)S(1)} %get-tuple-element.192), kind=kOutput, calls=%fused_computation.6 | convolution fusion | flops 4851499008 | bytes 24646656 | tf_op jit(solution)/shard_map/dot_general | solution.py:360
  232.0 8.1 %fusion.21 = f32[1,256,1024]{2,1,0:T(8,128)} fusion(f32[256,1024]{1,0:T(8,128)S(1)} %get-tuple-element.196, bf16[256,4608]{1,0:T(8,128)(2,1)} %get-tuple-element.174, bf16[4608,1024]{1,0:T(8,128)(2,1)} %bitcast.121), kind=kOutput, calls=%fused_computation.42 | convolution fusion | flops 2416181248 | bytes 13893632 | tf_op jit(solution)/shard_map/dot_general | solution.py:356
  240.1 5.0 %convolution_convert_fusion.1 = bf16[4608,1024]{1,0:T(8,128)(2,1)} fusion(bf16[256,4608]{1,0:T(8,128)(2,1)S(1)} %copy-done.5, bf16[1,256,1024]{2,1,0:T(8,128)(2,1)S(1)} %copy-done.11), kind=kOutput, calls=%fused_computation.11 | convolution fusion | flops 2420637696 | bytes 12320768 | tf_op jit(solution)/shard_map/dot_general | solution.py:360
  245.4 2.3 fusion.13
  247.7 2.6 multiply_reduce_fusion
  254.1 2.1 convolution_convert_fusion.3
  256.3 4.0 copy.145
  260.3 2.1 multiply_convert_fusion.5
  263.8 5.8 %fusion.32 = (bf16[1024]{0:T(1024)(128)(2,1)S(1)}, f32[256]{0:T(256)S(1)}, f32[256,1024]{1,0:T(8,128)}) fusion(bf16[1,256,1024]{2,1,0:T(8,128)(2,1)S(1)} %copy-done.14, f32[256]{0:T(256)S(1)} %get-tuple-element.190, f32[1024]{0:T(1024)S(1)} %bitcast.118, bf16[1024,13440]{1,0:T(8,128)(2,1)} %bitcast.103, bf16[256,1024]{1,0:T(8,128)(2,1)S(1)} %multiply_convert_fusion.3, ...), kind=kOutput, calls=%fused_computation.55 | convolution fusion | flops 1617165056 | bytes 9445376 | tf_op jit(solution)/shard_map/dot_general | solution.py:366
  269.6 4.5 convolution_convert_fusion.2
  275.0 18.2 %fusion.3 = bf16[1024,13440]{1,0:T(8,128)(2,1)} fusion(bf16[1024,5]{1,0:T(8,128)(2,1)S(1)} %bitcast.92, bf16[1024,9216]{1,0:T(8,128)(2,1)} %convolution_convert_fusion, bf16[1024,1024]{1,0:T(8,128)(2,1)S(1)} %copy-done.1, bf16[1024,3072]{1,0:T(8,128)(2,1)} %convolution_convert_fusion.2), kind=kLoop, calls=%fused_computation.5 | loop fusion | flops 165150720 | bytes 54798336 | tf_op jit(solution)/shard_map/concatenate | solution.py:516
  293.2 165.7 %scatter_gradients.1 = (f32[32,13440]{1,0:T(8,128)}, f32[144,1024]{1,0:T(8,128)}) custom-call(bf16[32,32,13440]{2,1,0:T(8,128)(2,1)} %bitcast.90, bf16[32,144,1024]{2,1,0:T(8,128)(2,1)} %bitcast.91), custom_call_target="tpu_custom_call" | custom-call | tf_op jit(solution)/shard_map/scatter_gradients/pallas_call | solution.py:326
  477.7 2.4 multiply_subtract_fusion.2
  480.1 1.8 multiply_subtract_fusion.3
  481.9 3.8 multiply_subtract_fusion
  485.8 1.5 multiply_subtract_fusion.1
  (159 shorter events, 44.8 us)
Async XLA Ops:
  4.5 164.1 %copy-start.12 = (bf16[1,256,1024]{2,1,0:T(8,128)(2,1)S(1)}, bf16[1,256,1024]{2,1,0:T(8,128)(2,1)}, u32[]{:S(2)}) copy-start(bf16[1,256,1024]{2,1,0:T(8,128)(2,1)} %param.21) | copy-start | bytes 1572868
  168.5 101.0 %copy-start.29 = (f32[1,1024]{1,0:T(1,128)}, f32[1,1024]{1,0:T(1,128)S(1)}, u32[]{:S(2)}) copy-start(f32[1,1024]{1,0:T(1,128)S(1)} %get-tuple-element.182) | copy-start | bytes 12292
  169.3 100.3 %copy-start.33 = (f32[256]{0:T(256)}, f32[256]{0:T(256)S(1)}, u32[]{:S(2)}) copy-start(f32[256]{0:T(256)S(1)} %get-tuple-element.190) | copy-start | bytes 3076
  169.3 8.4 %copy-start.40 = (f32[2,32]{1,0:T(2,128)S(1)}, f32[2,32]{1,0:T(2,128)}, u32[]{:S(2)}) copy-start(f32[2,32]{1,0:T(2,128)} %param.36) | copy-start | bytes 772
  169.3 8.4 %copy-start.37 = (f32[3,32]{1,0:T(4,128)S(1)}, f32[3,32]{1,0:T(4,128)}, u32[]{:S(2)}) copy-start(f32[3,32]{1,0:T(4,128)} %param.31) | copy-start | bytes 1156
  169.3 8.4 %copy-start.38 = (f32[3,32]{1,0:T(4,128)S(1)}, f32[3,32]{1,0:T(4,128)}, u32[]{:S(2)}) copy-start(f32[3,32]{1,0:T(4,128)} %param.37) | copy-start | bytes 1156
  169.3 8.4 %copy-start.41 = (f32[2,32]{1,0:T(2,128)S(1)}, f32[2,32]{1,0:T(2,128)}, u32[]{:S(2)}) copy-start(f32[2,32]{1,0:T(2,128)} %param.30) | copy-start | bytes 772
  169.4 8.4 %copy-start.31 = (f32[3,32]{1,0:T(4,128)S(1)}, f32[3,32]{1,0:T(4,128)}, u32[]{:S(2)}) copy-start(f32[3,32]{1,0:T(4,128)} %param.25) | copy-start | bytes 1156
  169.4 9.1 %copy-start.36 = (f32[2,32]{1,0:T(2,128)S(1)}, f32[2,32]{1,0:T(2,128)}, u32[]{:S(2)}) copy-start(f32[2,32]{1,0:T(2,128)} %param.24) | copy-start | bytes 772
  174.3 11.1 %copy-start = (f32[256,3072]{1,0:T(8,128)}, f32[256,3072]{1,0:T(8,128)S(1)}, u32[]{:S(2)}) copy-start(f32[256,3072]{1,0:T(8,128)S(1)} %fusion.10) | copy-start | bytes 9437188
  175.4 7.2 %collective-permute-start = (bf16[1,2,1024]{2,1,0:T(2,128)(2,1)S(1)}, bf16[1,2,1024]{2,1,0:T(2,128)(2,1)S(1)}, u32[]{:S(2)}, u32[]{:S(2)}) collective-permute-start(bf16[1,2,1024]{2,1,0:T(2,128)(2,1)S(1)} %slice.131), channel_id=1, source_target_pairs={{0,4},{4,8},{8,12},{12,16},{16,20},{20,24},{24,28},{1,5},{5,9},{9,... | collective-permute-start | bytes 12296 | tf_op jit(solution)/shard_map/ppermute | solution.py:352
  186.1 14.2 %slice-start = ((s8[9437184]{0:T(1024)(128)(4,1)}), s8[4194304]{0:T(1024)(128)(4,1)S(1)}, s32[]{:S(2)}) async-start(s8[9437184]{0:T(1024)(128)(4,1)} %bitcast.122), calls=%async_computation | async-start | bytes 8388608
  188.7 11.6 %copy-start.11 = (bf16[1,256,1024]{2,1,0:T(8,128)(2,1)S(1)}, bf16[1,256,1024]{2,1,0:T(8,128)(2,1)}, u32[]{:S(2)}) copy-start(bf16[1,256,1024]{2,1,0:T(8,128)(2,1)} %param.22) | copy-start | bytes 1572868
  188.7 11.6 %slice-start.1 = ((s8[9437184]{0:T(1024)(128)(4,1)}), s8[4194304]{0:T(1024)(128)(4,1)S(1)}, s32[]{:S(2)}) async-start(s8[9437184]{0:T(1024)(128)(4,1)} %bitcast.122), calls=%async_computation.1 | async-start | bytes 8388608
  188.7 11.6 %slice-start.2 = ((s8[9437184]{0:T(1024)(128)(4,1)}), s8[1048576]{0:T(1024)(128)(4,1)S(1)}, s32[]{:S(2)}) async-start(s8[9437184]{0:T(1024)(128)(4,1)} %bitcast.122), calls=%async_computation.2 | async-start | bytes 2097152
  251.5 8.7 %collective-permute-start.2 = (f32[1,2,1024]{2,1,0:T(2,128)S(1)}, f32[1,2,1024]{2,1,0:T(2,128)S(1)}, u32[]{:S(2)}, u32[]{:S(2)}) collective-permute-start(f32[1,2,1024]{2,1,0:T(2,128)S(1)} %slice.143), channel_id=1, source_target_pairs={{4,0},{8,4},{12,8},{16,12},{20,16},{24,20},{28,24},{5,1},{9,5},{13... | collective-permute-start | bytes 24584 | tf_op jit(solution)/shard_map/ppermute | solution.py:352
  252.8 7.5 %collective-permute-start.1 = (f32[1,2,1024]{2,1,0:T(2,128)S(1)}, f32[1,2,1024]{2,1,0:T(2,128)S(1)}, u32[]{:S(2)}, u32[]{:S(2)}) collective-permute-start(f32[1,2,1024]{2,1,0:T(2,128)S(1)} %slice.142), channel_id=1, source_target_pairs={{4,0},{8,4},{12,8},{16,12},{20,16},{24,20},{28,24},{5,1},{9,5},{13... | collective-permute-start | bytes 24584 | tf_op jit(solution)/shard_map/ppermute | solution.py:352
  293.1 166.6 %copy-start.27 = (f32[2,32]{0,1:T(8,128)S(1)}, f32[2,32]{0,1:T(8,128)}, u32[]{:S(2)}) copy-start(f32[2,32]{0,1:T(8,128)} %copy.147) | copy-start | bytes 772
  293.2 166.6 %copy-start.28 = (f32[2,32]{0,1:T(8,128)S(1)}, f32[2,32]{0,1:T(8,128)}, u32[]{:S(2)}) copy-start(f32[2,32]{0,1:T(8,128)} %copy.146) | copy-start | bytes 772
  293.2 184.5 %copy-start.17 = (f32[32,3072]{1,0:T(8,128)S(1)}, f32[32,3072]{1,0:T(8,128)}, u32[]{:S(2)}) copy-start(f32[32,3072]{1,0:T(8,128)} %param.26) | copy-start | bytes 1179652
  293.2 184.5 %copy-start.25 = (f32[32,3072]{1,0:T(8,128)S(1)}, f32[32,3072]{1,0:T(8,128)}, u32[]{:S(2)}) copy-start(f32[32,3072]{1,0:T(8,128)} %param.32) | copy-start | bytes 1179652
  293.2 184.5 %copy-start.26 = (f32[32,3072]{1,0:T(8,128)S(1)}, f32[32,3072]{1,0:T(8,128)}, u32[]{:S(2)}) copy-start(f32[32,3072]{1,0:T(8,128)} %param.38) | copy-start | bytes 1179652
  458.9 21.2 %copy-start.24 = (f32[32,1024]{1,0:T(8,128)S(1)}, f32[32,1024]{1,0:T(8,128)}, u32[]{:S(2)}) copy-start(f32[32,1024]{1,0:T(8,128)} %param.27) | copy-start | bytes 393220
  458.9 22.9 %copy-start.2 = (f32[32,9216]{1,0:T(8,128)S(1)}, f32[32,9216]{1,0:T(8,128)}, u32[]{:S(2)}) copy-start(f32[32,9216]{1,0:T(8,128)} %param.28) | copy-start | bytes 3538948
  (24 other events, 78.2 us)

commit v2 on v1

--- a/solution.py
+++ b/solution.py
@@ -205,15 +205,13 @@
     def slot_of(layer_step, hop):
         return layer_step * chips + hop - 1
 
-    def load(which, slot, buffer, start):
-        layer_step = slot // chips
-        hop = slot % chips + 1
+    def load(which, layer_step, hop, start):
         for way, cut in enumerate(cuts[which]):
             shard = here.shard(place(hop, way), here.core, layer_of(layer_step))
             copy = pltpu.make_async_copy(
                 grads[which].at[shard, :, cut],
-                staged[which].at[buffer, :, cut],
-                loaded.at[which, way, buffer],
+                staged[which].at[hop - 1, :, cut],
+                loaded.at[which, way, hop - 1],
             )
             copy.start() if start else copy.wait()
 
@@ -232,8 +230,9 @@
             ).start()
 
     slots = chips * depth
-    for which in range(count):
-        load(which, jnp.int32(0), jnp.int32(0), True)
+    for hop in range(1, chips + 1):
+        for which in range(count):
+            load(which, 0, hop, True)
     here.greet()
 
     @pl.loop(0, slots)
@@ -246,15 +245,8 @@
 
     def step(layer_step, hop):
         slot = slot_of(layer_step, hop)
-        buffer = slot % 2
-
-        @pl.when(slot + 1 < slots)
-        def _():
-            for which in range(count):
-                load(which, slot + 1, (slot + 1) % 2, True)
-
         for which in range(count):
-            load(which, slot, buffer, False)
+            load(which, layer_step, hop, False)
             if hop == chips:
                 @pl.when(layer_step > 0)
                 def _():
@@ -264,7 +256,7 @@
             for way, cut in enumerate(cuts[which]):
                 mine = theirs[which].at[slot, :, cut]
                 got(mine, from_sibling.at[which, way, slot])
-                total = mine[...].astype(f32) + staged[which][buffer, :, cut].astype(f32)
+                total = mine[...].astype(f32) + staged[which][hop - 1, :, cut].astype(f32)
                 if hop > 1:
                     index = layer_step * (chips - 1) + hop - 2
                     arrived = ringed[which].at[index, :, cut]
@@ -302,10 +294,23 @@
                         device_id_type=MESH_ID,
                     ).start()
 
+        @pl.when(layer_step < depth - 1)
+        def _():
+            for which in range(count):
+                load(which, layer_step + 1, hop, True)
+
+    step(0, 1)
+
     @pl.loop(0, depth)
     def _(layer_step):
-        for hop in range(1, chips + 1):
+        for hop in range(2, chips):
             step(layer_step, hop)
+
+        @pl.when(layer_step < depth - 1)
+        def _():
+            step(layer_step + 1, 1)
+
+        step(layer_step, chips)
 
     for which in range(count):
         most = grads[which].at[pl.ds(0, 2 * slots - 1)]
@@ -329,12 +334,12 @@
         in_specs=[anywhere] * count,
         out_specs=[inner] * count,
         scratch_shapes=room(slots)
-        + room(2)
+        + room(chips)
         + room(steps)
         + room(depth - 1)
         + [
             pltpu.SemaphoreType.DMA((count,)),
-            pltpu.SemaphoreType.DMA((count, 2, 2)),
+            pltpu.SemaphoreType.DMA((count, 2, chips)),
             pltpu.SemaphoreType.DMA((count, 2, slots)),
             pltpu.SemaphoreType.DMA((count, depth - 1)),
             pltpu.SemaphoreType.DMA((count, 2, steps)),
@@ -389,6 +394,30 @@
     second_hat = second_new / (1.0 - BETA_TWO**STEP)
     param_new = param - rate * (first_hat / (jnp.sqrt(second_hat) + ADAM_EPS) + decay * param)
     return (param_new, first_new, second_new)
+
+
+def adamw_kernel(*refs):
+    grads, state, outs = refs[:5], refs[5:23], refs[23:]
+    vectors = grads[0][...].T
+    found = [vectors[:2], vectors[2:5]] + [ref[...] for ref in grads[1:]]
+    for index, grad in enumerate(found):
+        rate, decay = (RATE_VECTOR, 0.0) if index < 2 else (RATE_MATRIX, DECAY)
+        param, first, second = (state[6 * kind + index][...] for kind in range(3))
+        new = adamw_update(param, grad, first, second, rate, decay)
+        for kind, value in enumerate((grad,) + new):
+            outs[6 * kind + index][...] = value
+
+
+def adamw(grads, params, firsts, seconds):
+    inner = pl.BlockSpec(memory_space=pltpu.VMEM)
+    return pl.pallas_call(
+        adamw_kernel,
+        out_shape=[jax.ShapeDtypeStruct(p.shape, p.dtype) for p in params] * 4,
+        in_specs=[inner] * 23,
+        out_specs=[inner] * 24,
+        compiler_params=pltpu.CompilerParams(vmem_limit_bytes=48 << 20),
+        name="adamw",
+    )(*grads, *params, *firsts, *seconds)
 
 
 def local(
@@ -478,6 +507,9 @@
     grad_both = jnp.concatenate([grad_gate, grad_act * silu_gate], axis=1).astype(half)
     grad_normed = matmul_nt(grad_both, ffn_full[0])
     grad_down = matmul_tn(ffn_act, cot_rows)
+    down_owned = lax.psum_scatter(
+        grad_down.astype(half), ALL, scatter_dimension=0, tiled=True
+    ).astype(single)
     grad_gate_up = matmul_tn(normed_two, grad_both)
     norm_part, gain_two_grad = norm_backward(resid_two, scale_two, gains_f[1], grad_normed)
     grad_resid = cot_rows.astype(single) + norm_part
@@ -513,65 +545,22 @@
     grad_out = matmul_tn(mixer_act, resid_cast)
     vector_grads = jnp.concatenate([grad_gains, grad_taps], axis=0)
     vector_count = vector_grads.shape[0]
-    grad_sent = jnp.concatenate(
-        [
-            grad_in.astype(half),
-            grad_out.astype(half),
-            jnp.pad(vector_grads.T, ((0, 0), (0, LANES - vector_count))).astype(half),
-            grad_gate_up.astype(half),
-        ],
-        axis=1,
-    )
-    grad_owned, down_owned = scatter(chips, depth, grad_sent, grad_down.astype(half))
-    vector_owned = grad_owned[:, vector_start : vector_start + vector_count].T
-    owned = (
-        vector_owned[:2],
-        vector_owned[2:],
-        grad_owned[:, :in_width],
-        grad_owned[:, in_width:vector_start],
-        grad_owned[:, vector_start + LANES :],
-        down_owned,
+    vector_columns = jnp.pad(vector_grads.T, ((0, 0), (0, LANES - vector_count))).astype(half)
+    grad_side = jnp.concatenate([vector_columns, grad_out.astype(half)], axis=1)
+    gate_owned, in_owned, side_owned = scatter(
+        chips, depth, grad_gate_up.astype(half), grad_in.astype(half), grad_side
     )
     params = (norm_gains, conv_taps, in_proj, out_proj, gate_up, down_proj)
     firsts = (first_gains, first_taps, first_in, first_out, first_gate_up, first_down)
     seconds = (second_gains, second_taps, second_in, second_out, second_gate_up, second_down)
-    rates = (RATE_VECTOR, RATE_VECTOR, RATE_MATRIX, RATE_MATRIX, RATE_MATRIX, RATE_MATRIX)
-    decays = (0.0, 0.0, DECAY, DECAY, DECAY, DECAY)
-    updated = [
-        adamw_update(
-            params[index], owned[index], firsts[index], seconds[index], rates[index], decays[index]
-        )
-        for index in range(6)
-    ]
+    owned = (side_owned[:, :LANES], in_owned, side_owned[:, LANES:], gate_owned, down_owned)
+    results = adamw(owned, params, firsts, seconds)
     out_rows = block_out.reshape(row_count, length, width)
     grad_rows = grad_hidden.reshape(row_count, length, width)
     return (
         out_rows,
         grad_rows,
-        owned[0],
-        owned[1],
-        owned[2],
-        owned[3],
-        owned[4],
-        owned[5],
-        updated[0][0],
-        updated[1][0],
-        updated[2][0],
-        updated[3][0],
-        updated[4][0],
-        updated[5][0],
-        updated[0][1],
-        updated[1][1],
-        updated[2][1],
-        updated[3][1],
-        updated[4][1],
-        updated[5][1],
-        updated[0][2],
-        updated[1][2],
-        updated[2][2],
-        updated[3][2],
-        updated[4][2],
-        updated[5][2],
+        *results,
     )
 
 

time: 491 us -> 446 us (0.908)
  other arithmetic: 52 us -> 19.1 us
  Pallas kernels: 325 us -> 310 us
  local copies, waits for them, and re-layouts: 28.4 us -> 14.9 us
  between operations: 1.31 us -> 14.8 us
    pallas_call x1, Pallas kernels: 166 us -> 144 us  [scatter(): pl.pallas_call(functools.partial(scatter_kernel, chips, depth, count), ou...]
    concatenate x1, other arithmetic: 18.2 us -> 1.99 us  [local(): grad_side = jnp.concatenate([vector_columns, grad_out.astype(half)], axis=1)]
    sub x6 -> x0, other arithmetic: 12.3 us -> none  [adamw_update(): param - rate * (first_hat / (jnp.sqrt(second_hat) + ADAM_EPS) + decay * p...]
    unnamed x102 -> x89, local copies, waits for them, and re-layouts: 16.4 us -> 8.69 us
    pallas_call x0 -> x1, Pallas kernels: none -> 6.83 us  [adamw(): pl.pallas_call(adamw_kernel, out_shape=[jax.ShapeDtypeStruct(p.shape, p.d...]
  transfers between devices with their start and end apart: 3 -> 4, of which waited for: 0 -> 1; matrix products, arithmetic and copies ran while one was open for 2% -> 14% of each run, Pallas kernels for 0% -> 32%
where the time goes in v2:
time: 446 us; the launch traced here: 445 us
  Pallas kernels  310 us (70%)
  matrix products  80.5 us (18%)
  other arithmetic  19.1 us (4%)
  local copies, waits for them, and re-layouts  14.9 us (3%)
  between operations  14.8 us (3%)
  starting transfers between devices  5.21 us (1%)
    pallas_call x1, Pallas kernels, gather(): pl.pallas_call(functools.partial(gather_kernel, chips, depth, count), out...  159 us
    pallas_call x1, Pallas kernels, scatter(): pl.pallas_call(functools.partial(scatter_kernel, chips, depth, count), ou...  144 us
    dot_general x4, matrix products, matmul_nt(): lax.dot_general(left, right, (((1,), (1,)), ((), ())), preferred_element_...  28.7 us
    dot_general x4, matrix products, matmul(): return jnp.dot(left, right, preferred_element_type=jnp.float32)  26.5 us
    dot_general x4, matrix products, matmul_tn(): lax.dot_general(left, right, (((0,), (0,)), ((), ())), preferred_element_...  25.3 us
  transfers between devices with their start and end apart: 4, of which 1 were waited for; matrix products, arithmetic and copies ran while one was open for 14% of the time, Pallas kernels for 32%

profile of v2, /device:TPU:0, one launch (start us, length us, event | category | flops | bytes accessed | tf_op | source)
XLA Modules:
  0.0 444.8 jit_solution(97017966732711340)
XLA Ops:
  11.9 1.8 convert_element_type.103.refs_1_
  13.7 1.4 convert_element_type.102
  16.1 159.0 %gather_weights.1 = (bf16[32,32,13440]{2,1,0:T(8,128)(2,1)}, bf16[32,144,1024]{2,1,0:T(8,128)(2,1)}) custom-call(bf16[32,13440]{1,0:T(8,128)(2,1)} %fusion.37.refs_0_, bf16[144,1024]{1,0:T(8,128)(2,1)} %convert_element_type.103.refs_1_), custom_call_target="tpu_custom_call" | custom-call | tf_op jit(solution)/shard_map/gather_weights/pallas_call | solution.py:167
  176.3 4.7 %fusion.6 = f32[256,3072]{1,0:T(8,128)S(1)} fusion(bf16[1024,13440]{1,0:T(8,128)(2,1)} %bitcast.97, bf16[1,256,1024]{2,1,0:T(8,128)(2,1)S(1)} %copy-done.30, f32[1024]{0:T(1024)S(1)} %bitcast.117, f32[256]{0:T(256)S(1)} %get-tuple-element.108), kind=kOutput, calls=%fused_computation.10 | convolution fusion | flops 1611661312 | bytes 9966592 | tf_op jit(solution)/shard_map/dot_general | solution.py:361
  181.1 2.5 collective-permute-start
  185.7 2.6 multiply_reduce_fusion.5
  188.3 11.6 %fusion.2 = f32[256,9216]{1,0:T(8,128)} fusion(bf16[1024,13440]{1,0:T(8,128)(2,1)} %bitcast.99, f32[256,1024]{1,0:T(8,128)S(1)} %get-tuple-element.114, f32[1024]{0:T(1024)S(1)} %bitcast.92, f32[256]{0:T(256)S(1)} %get-tuple-element.110), kind=kOutput, calls=%fused_computation.3 | convolution fusion | flops 4832624640 | bytes 29365248 | tf_op jit(solution)/shard_map/dot_general | solution.py:361
  199.9 8.6 %multiply_convert_fusion.1 = (bf16[256,4608]{1,0:T(8,128)(2,1)}, bf16[256,4608]{1,0:T(8,128)(2,1)}, bf16[256,4608]{1,0:T(8,128)(2,1)S(1)}) fusion(f32[256,9216]{1,0:T(8,128)} %fusion.2, bf16[4608,1024]{1,0:T(8,128)(2,1)S(1)} %bitcast.124, bf16[1,256,1024]{2,1,0:T(8,128)(2,1)S(1)} %copy-done.28), kind=kOutput, calls=%fused_computation.15 | convolution fusion | flops 2433613824 | bytes 26476544 | tf_op jit(solution)/shard_map/dot_general | solution.py:371
  209.9 5.0 %convolution_convert_fusion.1 = bf16[4608,1024]{1,0:T(8,128)(2,1)} fusion(bf16[256,4608]{1,0:T(8,128)(2,1)S(1)} %get-tuple-element.98, bf16[1,256,1024]{2,1,0:T(8,128)(2,1)S(1)} %copy-done.28), kind=kOutput, calls=%fused_computation.5 | convolution fusion | flops 2420637696 | bytes 12320768 | tf_op jit(solution)/shard_map/dot_general | solution.py:365
  214.9 11.5 %multiply_reduce_fusion.3 = (bf16[1024]{0:T(1024)(128)(2,1)S(1)}, f32[256]{0:T(256)S(1)}, f32[256,1024]{1,0:T(8,128)}) fusion(f32[256,1024]{1,0:T(8,128)S(1)} %get-tuple-element.114, f32[256]{0:T(256)S(1)} %get-tuple-element.110, f32[1024]{0:T(1024)S(1)} %bitcast.93, bf16[1024,13440]{1,0:T(8,128)(2,1)} %bitcast.100, ...), kind=kOutput, calls=%fused_computation.63 | convolution fusion | flops 4842847232 | bytes 25698304 | tf_op jit(solution)/shard_map/dot_general | solution.py:371
  226.4 1.6 subtract_add_fusion
  228.1 2.8 fusion.11
  230.9 2.7 multiply_reduce_fusion
  233.9 1.4 collective-permute-start.2
  236.6 7.7 %fusion.19 = f32[1,256,1024]{2,1,0:T(8,128)} fusion(f32[256,1024]{1,0:T(8,128)S(1)} %copy-done.23, bf16[256,4608]{1,0:T(8,128)(2,1)S(1)} %copy-done.25, bf16[4608,1024]{1,0:T(8,128)(2,1)} %bitcast.121), kind=kOutput, calls=%fused_computation.38 | convolution fusion | flops 2416181248 | bytes 13893632 | tf_op jit(solution)/shard_map/dot_general | solution.py:361
  244.3 12.5 %convolution_convert_fusion = bf16[1024,9216]{1,0:T(8,128)(2,1)} fusion(bf16[256,4608]{1,0:T(8,128)(2,1)} %get-tuple-element.97, bf16[256,4608]{1,0:T(8,128)(2,1)} %get-tuple-element.96, f32[256,1024]{1,0:T(8,128)} %copy-done.22, f32[1024]{0:T(1024)S(1)} %bitcast.95, f32[256]{0:T(256)S(1)} %get-tuple-element.110), kind=kOutput, calls=%fused_computation | convolution fusion | flops 4851499008 | bytes 24646656 | tf_op jit(solution)/shard_map/dot_general | solution.py:365
  256.8 2.1 convolution_convert_fusion.3
  260.2 5.7 %fusion.29 = (bf16[1024]{0:T(1024)(128)(2,1)S(1)}, f32[256]{0:T(256)S(1)}, f32[256,1024]{1,0:T(8,128)}) fusion(bf16[1,256,1024]{2,1,0:T(8,128)(2,1)S(1)} %copy-done.32, f32[256]{0:T(256)S(1)} %get-tuple-element.108, f32[1024]{0:T(1024)S(1)} %bitcast.118, bf16[1024,13440]{1,0:T(8,128)(2,1)} %bitcast.102, bf16[256,1024]{1,0:T(8,128)(2,1)S(1)} %multiply_convert_fusion.3, ...), kind=kOutput, calls=%fused_computation.48 | convolution fusion | flops 1617165056 | bytes 9445376 | tf_op jit(solution)/shard_map/dot_general | solution.py:371
  266.0 2.0 fusion.10
  268.1 2.6 copy.59
  270.6 5.8 %convolution_convert_fusion.2 = bf16[1024,3072]{1,0:T(8,128)(2,1)} fusion(bf16[256,1024]{1,0:T(8,128)(2,1)} %copy-done.39, bf16[256,1024]{1,0:T(8,128)(2,1)S(1)} %copy-done.37, bf16[256,1024]{1,0:T(8,128)(2,1)} %copy-done.38, bf16[1,256,1024]{2,1,0:T(8,128)(2,1)S(1)} %copy-done.33, f32[1024]{0:T(1024)S(1)} %bitcast.119, f32[256]{0:T(256)S(1)} %get-tuple-element.108), kind=kOutput, calls=%fused_computation.7 | convolution fusion | flops 1619525632 | bytes 8393728 | tf_op jit(solution)/shard_map/dot_general | solution.py:365
  276.4 143.9 %scatter_gradients.1 = (f32[32,9216]{1,0:T(8,128)}, f32[32,3072]{1,0:T(8,128)}, f32[32,1152]{1,0:T(8,128)}) custom-call(bf16[32,32,9216]{2,1,0:T(8,128)(2,1)} %bitcast.89, bf16[32,32,3072]{2,1,0:T(8,128)(2,1)} %bitcast.91, bf16[32,32,1152]{2,1,0:T(8,128)(2,1)} %bitcast.90), custom_call_target="tpu_custom_call" | custom-call | tf_op jit(solution)/shard_map/scatter_gradients/pallas_call | solution.py:331
  421.3 1.7 slice.107.refs_2_
  431.1 6.8 %adamw.1 = (f32[2,32]{1,0:T(2,128)}, f32[3,32]{1,0:T(4,128)}, f32[32,3072]{1,0:T(8,128)}, f32[32,1024]{1,0:T(8,128)}, f32[32,9216]{1,0:T(8,128)}, /*index=5*/f32...) custom-call(f32[32,128]{1,0:T(8,128)S(1)} %slice.106.refs_0_, ...), custom_call_target="tpu_custom_call" | custom-call | tf_op jit(solution)/shard_map/adamw/pallas_call | solution.py:413
  (131 shorter events, 22.2 us)
Async XLA Ops:
  7.2 417.0 %reduce-scatter.2.cloned.1.call-start = ((), (), s32[]{:S(2)}) async-start(), calls=%async_computation.1 | async-start | bytes 9732096 | tf_op jit(solution)/shard_map/reduce_scatter | solution.py:510
  13.7 162.5 %copy-start.30 = (bf16[1,256,1024]{2,1,0:T(8,128)(2,1)S(1)}, bf16[1,256,1024]{2,1,0:T(8,128)(2,1)}, u32[]{:S(2)}) copy-start(bf16[1,256,1024]{2,1,0:T(8,128)(2,1)} %param.21) | copy-start | bytes 1572868
  176.3 7.3 %copy-start.40 = (s32[1,256]{1,0:T(1,128)S(1)}, s32[1,256]{1,0:T(1,128)}, u32[]{:S(2)}) copy-start(s32[1,256]{1,0:T(1,128)} %param.23) | copy-start | bytes 3076
  181.1 3.1 collective-permute-start
  185.7 14.2 %slice-start = ((s8[9437184]{0:T(1024)(128)(4,1)}), s8[4194304]{0:T(1024)(128)(4,1)S(1)}, s32[]{:S(2)}) async-start(s8[9437184]{0:T(1024)(128)(4,1)} %bitcast.122), calls=%async_computation.2 | async-start | bytes 8388608
  188.3 38.2 %copy-start.22 = (f32[256,1024]{1,0:T(8,128)}, f32[256,1024]{1,0:T(8,128)S(1)}, u32[]{:S(2)}) copy-start(f32[256,1024]{1,0:T(8,128)S(1)} %get-tuple-element.114) | copy-start | bytes 3145732
  188.3 11.6 %copy-start.28 = (bf16[1,256,1024]{2,1,0:T(8,128)(2,1)S(1)}, bf16[1,256,1024]{2,1,0:T(8,128)(2,1)}, u32[]{:S(2)}) copy-start(bf16[1,256,1024]{2,1,0:T(8,128)(2,1)} %param.22) | copy-start | bytes 1572868
  188.3 11.6 %slice-start.1 = ((s8[9437184]{0:T(1024)(128)(4,1)}), s8[4194304]{0:T(1024)(128)(4,1)S(1)}, s32[]{:S(2)}) async-start(s8[9437184]{0:T(1024)(128)(4,1)} %bitcast.122), calls=%async_computation.3 | async-start | bytes 8388608
  188.3 11.6 %slice-start.2 = ((s8[9437184]{0:T(1024)(128)(4,1)}), s8[1048576]{0:T(1024)(128)(4,1)S(1)}, s32[]{:S(2)}) async-start(s8[9437184]{0:T(1024)(128)(4,1)} %bitcast.122), calls=%async_computation.4 | async-start | bytes 2097152
  214.9 11.5 %copy-start.29 = (bf16[1,256,1024]{2,1,0:T(8,128)(2,1)S(1)}, bf16[1,256,1024]{2,1,0:T(8,128)(2,1)}, u32[]{:S(2)}) copy-start(bf16[1,256,1024]{2,1,0:T(8,128)(2,1)} %param.22) | copy-start | bytes 1572868
  228.1 28.7 %copy-start.18 = (f32[256,1024]{1,0:T(8,128)}, f32[256,1024]{1,0:T(8,128)S(1)}, u32[]{:S(2)}) copy-start(f32[256,1024]{1,0:T(8,128)S(1)} %subtract_add_fusion) | copy-start | bytes 3145732
  230.9 5.7 %copy-start.25 = (bf16[256,4608]{1,0:T(8,128)(2,1)S(1)}, bf16[256,4608]{1,0:T(8,128)(2,1)}, u32[]{:S(2)}) copy-start(bf16[256,4608]{1,0:T(8,128)(2,1)} %copy-done.24) | copy-start | bytes 7077892
  233.9 25.1 %collective-permute-start.2 = (f32[1,2,1024]{2,1,0:T(2,128)S(1)}, f32[1,2,1024]{2,1,0:T(2,128)S(1)}, u32[]{:S(2)}, u32[]{:S(2)}) collective-permute-start(f32[1,2,1024]{2,1,0:T(2,128)S(1)} %slice.127), channel_id=1, source_target_pairs={{4,0},{8,4},{12,8},{16,12},{20,16},{24,20},{28,24},{5,1},{9,5},{13... | collective-permute-start | bytes 24584 | tf_op jit(solution)/shard_map/ppermute | solution.py:357
  235.3 23.7 %collective-permute-start.1 = (f32[1,2,1024]{2,1,0:T(2,128)S(1)}, f32[1,2,1024]{2,1,0:T(2,128)S(1)}, u32[]{:S(2)}, u32[]{:S(2)}) collective-permute-start(f32[1,2,1024]{2,1,0:T(2,128)S(1)} %slice.126), channel_id=1, source_target_pairs={{4,0},{8,4},{12,8},{16,12},{20,16},{24,20},{28,24},{5,1},{9,5},{13... | collective-permute-start | bytes 24584 | tf_op jit(solution)/shard_map/ppermute | solution.py:357
  244.3 12.5 %copy-start.27 = (bf16[256,1024]{1,0:T(8,128)(2,1)S(1)}, bf16[256,1024]{1,0:T(8,128)(2,1)}, u32[]{:S(2)}) copy-start(bf16[256,1024]{1,0:T(8,128)(2,1)} %copy-done.26) | copy-start | bytes 1572868
  259.8 6.2 %copy-start.38 = (bf16[256,1024]{1,0:T(8,128)(2,1)}, bf16[256,1024]{1,0:T(8,128)(2,1)S(1)}, u32[]{:S(2)}) copy-start(bf16[256,1024]{1,0:T(8,128)(2,1)S(1)} %get-tuple-element.92) | copy-start | bytes 1572868
  260.0 6.0 %copy-start.39 = (bf16[256,1024]{1,0:T(8,128)(2,1)}, bf16[256,1024]{1,0:T(8,128)(2,1)S(1)}, u32[]{:S(2)}) copy-start(bf16[256,1024]{1,0:T(8,128)(2,1)S(1)} %multiply_convert_fusion.3) | copy-start | bytes 1572868
  276.4 146.6 %copy-start.19 = (f32[256,1024]{1,0:T(8,128)S(1)}, f32[256,1024]{1,0:T(8,128)}, u32[]{:S(2)}) copy-start(f32[256,1024]{1,0:T(8,128)} %copy-done.18) | copy-start | bytes 3145732
  276.4 146.6 %copy-start.34 = (bf16[1,256,1024]{2,1,0:T(8,128)(2,1)S(1)}, bf16[1,256,1024]{2,1,0:T(8,128)(2,1)}, u32[]{:S(2)}) copy-start(bf16[1,256,1024]{2,1,0:T(8,128)(2,1)} %param.21) | copy-start | bytes 1572868
  276.4 146.6 %copy-start.35 = (f32[256,1024]{1,0:T(8,128)S(1)}, f32[256,1024]{1,0:T(8,128)}, u32[]{:S(2)}) copy-start(f32[256,1024]{1,0:T(8,128)} %get-tuple-element.116) | copy-start | bytes 3145732
  420.3 5.0 %copy-start = (f32[144,1024]{1,0:T(8,128)S(1)}, f32[144,1024]{1,0:T(8,128)}, u32[]{:S(2)}) copy-start(f32[144,1024]{1,0:T(8,128)} %refs_10_.1) | copy-start | bytes 1769476
  420.3 5.0 %copy-start.1 = (f32[32,3072]{1,0:T(8,128)S(1)}, f32[32,3072]{1,0:T(8,128)}, u32[]{:S(2)}) copy-start(f32[32,3072]{1,0:T(8,128)} %refs_7_.1) | copy-start | bytes 1179652
  420.3 5.0 %copy-start.2 = (f32[32,9216]{1,0:T(8,128)S(1)}, f32[32,9216]{1,0:T(8,128)}, u32[]{:S(2)}) copy-start(f32[32,9216]{1,0:T(8,128)} %get-tuple-element.59.refs_3_) | copy-start | bytes 3538948
  420.3 5.0 %copy-start.3 = (f32[144,1024]{1,0:T(8,128)S(1)}, f32[144,1024]{1,0:T(8,128)}, u32[]{:S(2)}) copy-start(f32[144,1024]{1,0:T(8,128)} %refs_16_.1) | copy-start | bytes 1769476
  (24 other events, 65.9 us)
Sparse Core Ops, SparseCore 0:
  215.0 169.7 reduce-scatter.1

commit v3 on v2

--- a/solution.py
+++ b/solution.py
@@ -19,6 +19,7 @@
 RATE_VECTOR = 0.2
 DECAY = 0.1
 LANES = 128
+VMEM_SCATTER = 46 << 20
 MESH_ID = pl.DeviceIdType.MESH
 SEQ = ("ring", "core")
 ALL = ("ring", "core", "fsdp")
@@ -62,9 +63,10 @@
 def gather_kernel(chips, depth, count, *refs):
     shards = refs[:count]
     wholes = refs[count : 2 * count]
-    sent, from_sibling, from_below, from_ring, kept = refs[2 * count :]
+    sent, from_sibling, from_below, from_ring, kept, late_ring, late_below = refs[2 * count :]
     here = Place(chips, depth)
     here.greet()
+    late = count - 1
     cuts = [halves(ref.shape[1]) for ref in shards]
 
     def block(which, shard):
@@ -87,7 +89,7 @@
         pltpu.make_async_copy(ref, ref, arrived).wait()
 
     own = here.shard(here.spot, here.core, here.layer)
-    for which in range(count):
+    for which in range(late):
         send(shards[which], block(which, own), which, from_below.at[which, 0], here.up)
         for way in range(2):
             send(
@@ -97,12 +99,51 @@
                 from_ring.at[which, way, 0],
                 (here.right, here.left)[way],
             )
+    for way in range(2):
+        part = shards[late].at[:, cuts[late][way]]
+        piece = piece_of(late, own, way)
+        send(part, piece, late, late_ring.at[way, 0], (here.right, here.left)[way])
+        send(part, piece, late, late_below.at[way, 0], here.up)
+    for which in range(count):
         send(shards[which], block(which, own), which, from_sibling.at[which], here.sibling)
         pltpu.make_async_copy(shards[which], block(which, own), kept.at[which]).start()
 
+    def late_around(hop):
+        for way in range(2):
+            away = (chips - hop, hop)[way]
+            piece = piece_of(late, here.shard((here.spot + away) % chips, here.core, here.layer), way)
+            awaited(piece, late_ring.at[way, hop - 1])
+            if hop < chips - 1:
+                send(piece, piece, late, late_ring.at[way, hop], (here.right, here.left)[way])
+            send(piece, piece, late, late_below.at[way, hop], here.up)
+            send(piece, piece, late, from_sibling.at[late], here.sibling)
+
+    def late_layer(layer_step, hop):
+        layer = (here.layer + depth - layer_step) % depth
+        for way in range(2):
+            away = (chips - hop, hop)[way]
+            piece = piece_of(late, here.shard((here.spot + away) % chips, here.core, layer), way)
+            awaited(piece, late_below.at[way, (layer_step - 1) * chips + hop])
+
+            @pl.when(layer_step < depth - 1)
+            def _():
+                send(piece, piece, late, late_below.at[way, layer_step * chips + hop], here.up)
+
+            send(piece, piece, late, from_sibling.at[late], here.sibling)
+
+    def late_step(layer_step, hop):
+        if hop > 0:
+            @pl.when(layer_step == 0)
+            def _():
+                late_around(hop)
+
+        @pl.when(layer_step > 0)
+        def _():
+            late_layer(layer_step, hop)
+
     def around(hop, layer_step):
         layer = (here.layer + depth - layer_step) % depth
-        for which in range(count):
+        for which in range(late):
             for way in range(2):
                 away = (chips - hop, hop)[way]
                 shard = here.shard((here.spot + away) % chips, here.core, layer)
@@ -122,7 +163,7 @@
     def layer_arrives(layer_step):
         layer = (here.layer + depth - layer_step) % depth
         shard = here.shard(here.spot, here.core, layer)
-        for which in range(count):
+        for which in range(late):
             whole = block(which, shard)
             awaited(whole, from_below.at[which, layer_step - 1])
 
@@ -143,14 +184,17 @@
 
     @pl.loop(0, depth)
     def _(layer_step):
+        late_step(layer_step, 0)
         for hop in range(1, chips - 1):
             around(hop, layer_step)
+            late_step(layer_step, hop)
 
         @pl.when(layer_step < depth - 1)
         def _():
             layer_arrives(layer_step + 1)
 
         around(chips - 1, layer_step)
+        late_step(layer_step, chips - 1)
 
     shard_count = 2 * chips * depth
     for which in range(count):
@@ -175,6 +219,8 @@
             pltpu.SemaphoreType.DMA((count, depth - 1)),
             pltpu.SemaphoreType.DMA((count, 2, steps)),
             pltpu.SemaphoreType.DMA((count,)),
+            pltpu.SemaphoreType.DMA((2, chips - 1)),
+            pltpu.SemaphoreType.DMA((2, chips * (depth - 1))),
         ],
         compiler_params=pltpu.CompilerParams(collective_id=0, has_side_effects=True),
         name="gather_weights",
@@ -190,8 +236,9 @@
     staged = rest[count : 2 * count]
     ringed = rest[2 * count : 3 * count]
     layered = rest[3 * count : 4 * count]
-    sent, loaded, from_sibling, from_below, from_ring = rest[4 * count :]
+    sent, loaded, from_sibling, from_below, from_ring, late_below = rest[4 * count :]
     here = Place(chips, depth)
+    late = count - 1
     cuts = [halves(ref.shape[1]) for ref in owned]
     f32 = jnp.float32
 
@@ -245,7 +292,7 @@
 
     def step(layer_step, hop):
         slot = slot_of(layer_step, hop)
-        for which in range(count):
+        for which in range(late):
             load(which, layer_step, hop, False)
             if hop == chips:
                 @pl.when(layer_step > 0)
@@ -296,20 +343,75 @@
 
         @pl.when(layer_step < depth - 1)
         def _():
-            for which in range(count):
+            for which in range(late):
                 load(which, layer_step + 1, hop, True)
+
+    def late_step(layer_step, hop):
+        slot = slot_of(layer_step, hop)
+        load(late, layer_step, hop, False)
+        for way, cut in enumerate(cuts[late]):
+            mine = theirs[late].at[slot, :, cut]
+            got(mine, from_sibling.at[late, way, slot])
+            total = mine[...].astype(f32) + staged[late][hop - 1, :, cut].astype(f32)
+            mine[...] = total.astype(mine.dtype)
+
+            @pl.when(layer_step > 0)
+            def _():
+                before = slot_of(layer_step - 1, hop)
+                arrived = layered[late].at[before, :, cut]
+                got(arrived, late_below.at[way, before])
+                both = total + arrived[...].astype(f32)
+                mine[...] = both.astype(mine.dtype)
+
+            @pl.when(layer_step < depth - 1)
+            def _():
+                pltpu.make_async_remote_copy(
+                    src_ref=mine,
+                    dst_ref=layered[late].at[slot, :, cut],
+                    send_sem=sent.at[late],
+                    recv_sem=late_below.at[way, slot],
+                    device_id=here.up,
+                    device_id_type=MESH_ID,
+                ).start()
+
+            @pl.when(layer_step == depth - 1)
+            def _():
+                around = mine[...].astype(f32)
+                if hop > 1:
+                    arrived = ringed[late].at[hop - 2, :, cut]
+                    got(arrived, from_ring.at[late, way, hop - 2])
+                    around = around + arrived[...].astype(f32)
+                if hop < chips:
+                    mine[...] = around.astype(mine.dtype)
+                    pltpu.make_async_remote_copy(
+                        src_ref=mine,
+                        dst_ref=ringed[late].at[hop - 1, :, cut],
+                        send_sem=sent.at[late],
+                        recv_sem=from_ring.at[late, way, hop - 1],
+                        device_id=(here.right, here.left)[way],
+                        device_id_type=MESH_ID,
+                    ).start()
+                else:
+                    owned[late][:, cut] = around
+
+        @pl.when(layer_step < depth - 1)
+        def _():
+            load(late, layer_step + 1, hop, True)
 
     step(0, 1)
 
     @pl.loop(0, depth)
     def _(layer_step):
+        late_step(layer_step, 1)
         for hop in range(2, chips):
             step(layer_step, hop)
+            late_step(layer_step, hop)
 
         @pl.when(layer_step < depth - 1)
         def _():
             step(layer_step + 1, 1)
 
+        late_step(layer_step, chips)
         step(layer_step, chips)
 
     for which in range(count):
@@ -325,27 +427,29 @@
     anywhere = pl.BlockSpec(memory_space=pl.ANY)
     inner = pl.BlockSpec(memory_space=pltpu.VMEM)
 
-    def room(leading):
-        return [pltpu.VMEM((leading,) + g.shape[1:], g.dtype) for g in grads]
+    def room(most, last):
+        leading = [most] * (count - 1) + [last]
+        return [pltpu.VMEM((n,) + g.shape[1:], g.dtype) for n, g in zip(leading, grads)]
 
     return pl.pallas_call(
         functools.partial(scatter_kernel, chips, depth, count),
         out_shape=[jax.ShapeDtypeStruct(g.shape[1:], jnp.float32) for g in grads],
         in_specs=[anywhere] * count,
         out_specs=[inner] * count,
-        scratch_shapes=room(slots)
-        + room(chips)
-        + room(steps)
-        + room(depth - 1)
+        scratch_shapes=room(slots, slots)
+        + room(chips, chips)
+        + room(steps, chips - 1)
+        + room(depth - 1, chips * (depth - 1))
         + [
             pltpu.SemaphoreType.DMA((count,)),
             pltpu.SemaphoreType.DMA((count, 2, chips)),
             pltpu.SemaphoreType.DMA((count, 2, slots)),
             pltpu.SemaphoreType.DMA((count, depth - 1)),
             pltpu.SemaphoreType.DMA((count, 2, steps)),
+            pltpu.SemaphoreType.DMA((2, chips * (depth - 1))),
         ],
         compiler_params=pltpu.CompilerParams(
-            collective_id=1, has_side_effects=True, vmem_limit_bytes=56 << 20
+            collective_id=1, has_side_effects=True, vmem_limit_bytes=VMEM_SCATTER
         ),
         name="scatter_gradients",
     )(*grads)
@@ -507,9 +611,6 @@
     grad_both = jnp.concatenate([grad_gate, grad_act * silu_gate], axis=1).astype(half)
     grad_normed = matmul_nt(grad_both, ffn_full[0])
     grad_down = matmul_tn(ffn_act, cot_rows)
-    down_owned = lax.psum_scatter(
-        grad_down.astype(half), ALL, scatter_dimension=0, tiled=True
-    ).astype(single)
     grad_gate_up = matmul_tn(normed_two, grad_both)
     norm_part, gain_two_grad = norm_backward(resid_two, scale_two, gains_f[1], grad_normed)
     grad_resid = cot_rows.astype(single) + norm_part
@@ -547,8 +648,13 @@
     vector_count = vector_grads.shape[0]
     vector_columns = jnp.pad(vector_grads.T, ((0, 0), (0, LANES - vector_count))).astype(half)
     grad_side = jnp.concatenate([vector_columns, grad_out.astype(half)], axis=1)
-    gate_owned, in_owned, side_owned = scatter(
-        chips, depth, grad_gate_up.astype(half), grad_in.astype(half), grad_side
+    gate_owned, in_owned, side_owned, down_owned = scatter(
+        chips,
+        depth,
+        grad_gate_up.astype(half),
+        grad_in.astype(half),
+        grad_side,
+        grad_down.astype(half),
     )
     params = (norm_gains, conv_taps, in_proj, out_proj, gate_up, down_proj)
     firsts = (first_gains, first_taps, first_in, first_out, first_gate_up, first_down)

time: 446 us -> 405 us (0.908)
  between operations: 14.8 us -> 1.45 us
  local copies, waits for them, and re-layouts: 14.9 us -> 5.23 us
  matrix products: 80.5 us -> 71.8 us
  Pallas kernels: 310 us -> 303 us
    pallas_call x1, Pallas kernels: 159 us -> 144 us  [gather(): pl.pallas_call(functools.partial(gather_kernel, chips, depth, count), out...]
    pallas_call x1, Pallas kernels: 144 us -> 152 us  [scatter(): pl.pallas_call(functools.partial(scatter_kernel, chips, depth, count), ou...]
    unnamed x89 -> x57, local copies, waits for them, and re-layouts: 8.69 us -> 1.03 us
  transfers between devices with their start and end apart: 4 -> 3, of which waited for: 1 -> 2; matrix products, arithmetic and copies ran while one was open for 14% -> 0% of each run, Pallas kernels for 32% -> 0%
where the time goes in v3:
time: 405 us; the launch traced here: 404 us
  Pallas kernels  303 us (75%)
  matrix products  71.8 us (18%)
  other arithmetic  15.8 us (4%)
  local copies, waits for them, and re-layouts  5.23 us (1%)
  starting transfers between devices  5.04 us (1%)
    pallas_call x1, Pallas kernels, scatter(): pl.pallas_call(functools.partial(scatter_kernel, chips, depth, count), ou...  152 us
    pallas_call x1, Pallas kernels, gather(): pl.pallas_call(functools.partial(gather_kernel, chips, depth, count), out...  144 us
    dot_general x4, matrix products, matmul_nt(): lax.dot_general(left, right, (((1,), (1,)), ((), ())), preferred_element_...  27.8 us
    dot_general x4, matrix products, matmul(): return jnp.dot(left, right, preferred_element_type=jnp.float32)  22.2 us
    dot_general x4, matrix products, matmul_tn(): lax.dot_general(left, right, (((0,), (0,)), ((), ())), preferred_element_...  21.8 us
  transfers between devices with their start and end apart: 3, of which 2 were waited for; matrix products, arithmetic and copies ran while one was open for 0% of the time, Pallas kernels for 0%

profile of v3, /device:TPU:0, one launch (start us, length us, event | category | flops | bytes accessed | tf_op | source)
XLA Modules:
  0.0 404.5 jit_solution(716013749983217562)
XLA Ops:
  5.3 1.8 convert_element_type.100.refs_1_
  7.1 1.4 convert_element_type.99
  9.5 144.0 %gather_weights.1 = (bf16[32,32,13440]{2,1,0:T(8,128)(2,1)}, bf16[32,144,1024]{2,1,0:T(8,128)(2,1)}) custom-call(bf16[32,13440]{1,0:T(8,128)(2,1)} %fusion.37.refs_0_, bf16[144,1024]{1,0:T(8,128)(2,1)} %convert_element_type.100.refs_1_), custom_call_target="tpu_custom_call" | custom-call | tf_op jit(solution)/shard_map/gather_weights/pallas_call | solution.py:211
  154.8 4.7 %fusion.6 = f32[256,3072]{1,0:T(8,128)S(1)} fusion(bf16[1024,13440]{1,0:T(8,128)(2,1)} %bitcast.99, bf16[1,256,1024]{2,1,0:T(8,128)(2,1)S(1)} %copy-done.20, f32[1024]{0:T(1024)S(1)} %bitcast.119, f32[256]{0:T(256)S(1)} %get-tuple-element.110), kind=kOutput, calls=%fused_computation.10 | convolution fusion | flops 1611661312 | bytes 9966592 | tf_op jit(solution)/shard_map/dot_general | solution.py:465
  159.6 2.5 collective-permute-start
  163.4 2.6 multiply_reduce_fusion.5
  166.1 11.3 %fusion.2 = f32[256,9216]{1,0:T(8,128)} fusion(bf16[1024,13440]{1,0:T(8,128)(2,1)} %bitcast.101, f32[256,1024]{1,0:T(8,128)S(1)} %get-tuple-element.116, f32[1024]{0:T(1024)S(1)} %bitcast.94, f32[256]{0:T(256)S(1)} %get-tuple-element.112), kind=kOutput, calls=%fused_computation.3 | convolution fusion | flops 4832624640 | bytes 29365248 | tf_op jit(solution)/shard_map/dot_general | solution.py:465
  177.5 8.5 %multiply_convert_fusion.1 = (bf16[256,4608]{1,0:T(8,128)(2,1)}, bf16[256,4608]{1,0:T(8,128)(2,1)}, bf16[256,4608]{1,0:T(8,128)(2,1)S(1)}) fusion(f32[256,9216]{1,0:T(8,128)} %fusion.2, bf16[4608,1024]{1,0:T(8,128)(2,1)S(1)} %bitcast.125, bf16[1,256,1024]{2,1,0:T(8,128)(2,1)S(1)} %copy-done.19), kind=kOutput, calls=%fused_computation.15 | convolution fusion | flops 2433613824 | bytes 26476544 | tf_op jit(solution)/shard_map/dot_general | solution.py:475
  185.9 3.6 fusion.19
  189.5 5.0 %convolution_convert_fusion.1 = bf16[4608,1024]{1,0:T(8,128)(2,1)} fusion(bf16[256,4608]{1,0:T(8,128)(2,1)S(1)} %get-tuple-element.100, bf16[1,256,1024]{2,1,0:T(8,128)(2,1)S(1)} %copy-done.19), kind=kOutput, calls=%fused_computation.5 | convolution fusion | flops 2420637696 | bytes 12320768 | tf_op jit(solution)/shard_map/dot_general | solution.py:469
  194.6 11.2 %multiply_reduce_fusion.3 = (bf16[1024]{0:T(1024)(128)(2,1)S(1)}, f32[256]{0:T(256)S(1)}, f32[256,1024]{1,0:T(8,128)}) fusion(f32[256,1024]{1,0:T(8,128)S(1)} %get-tuple-element.116, f32[256]{0:T(256)S(1)} %get-tuple-element.112, f32[1024]{0:T(1024)S(1)} %bitcast.95, bf16[1024,13440]{1,0:T(8,128)(2,1)} %bitcast.102, ...), kind=kOutput, calls=%fused_computation.63 | convolution fusion | flops 4842847232 | bytes 25698304 | tf_op jit(solution)/shard_map/dot_general | solution.py:475
  205.8 11.5 %convolution_convert_fusion = bf16[1024,9216]{1,0:T(8,128)(2,1)} fusion(bf16[256,4608]{1,0:T(8,128)(2,1)} %get-tuple-element.99, bf16[256,4608]{1,0:T(8,128)(2,1)} %get-tuple-element.98, f32[256,1024]{1,0:T(8,128)S(1)} %get-tuple-element.116, f32[1024]{0:T(1024)S(1)} %bitcast.96, f32[256]{0:T(256)S(1)} %get-tuple-element.112), kind=kOutput, calls=%fused_computation | convolution fusion | flops 4851499008 | bytes 24646656 | tf_op jit(solution)/shard_map/dot_general | solution.py:469
  217.3 1.8 subtract_add_fusion
  219.1 2.3 fusion.11
  222.2 1.3 collective-permute-start.2
  223.5 1.3 collective-permute-start.1
  225.7 1.5 collective-permute-done.1
  227.9 5.7 %fusion.29 = (bf16[1024]{0:T(1024)(128)(2,1)S(1)}, f32[256]{0:T(256)S(1)}, f32[256,1024]{1,0:T(8,128)}) fusion(bf16[1,256,1024]{2,1,0:T(8,128)(2,1)S(1)} %copy-done.21, f32[256]{0:T(256)S(1)} %get-tuple-element.110, f32[1024]{0:T(1024)S(1)} %bitcast.120, bf16[1024,13440]{1,0:T(8,128)(2,1)} %bitcast.104, bf16[256,1024]{1,0:T(8,128)(2,1)S(1)} %multiply_convert_fusion.3, ...), kind=kOutput, calls=%fused_computation.48 | convolution fusion | flops 1617165056 | bytes 9445376 | tf_op jit(solution)/shard_map/dot_general | solution.py:475
  233.7 4.6 %convolution_convert_fusion.2 = bf16[1024,3072]{1,0:T(8,128)(2,1)} fusion(bf16[256,1024]{1,0:T(8,128)(2,1)S(1)} %multiply_convert_fusion.3, bf16[256,1024]{1,0:T(8,128)(2,1)S(1)} %get-tuple-element.101, bf16[256,1024]{1,0:T(8,128)(2,1)S(1)} %get-tuple-element.94, bf16[1,256,1024]{2,1,0:T(8,128)(2,1)S(1)} %copy-done.21, f32[1024]{0:T(1024)S(1)} %bitcast.121, ...), kind=kOutput, calls=%fused_computation.7 | convolution fusion | flops 1619525632 | bytes 8393728 | tf_op jit(solution)/shard_map/dot_general | solution.py:469
  238.3 1.7 fusion.10
  240.0 3.0 copy.59
  243.0 152.0 %scatter_gradients.1 = (f32[32,9216]{1,0:T(8,128)S(1)}, f32[32,3072]{1,0:T(8,128)S(1)}, f32[32,1152]{1,0:T(8,128)S(1)}, f32[144,1024]{1,0:T(8,128)S(1)}) custom-call(bf16[32,32,9216]{2,1,0:T(8,128)(2,1)} %bitcast.91, bf16[32,32,3072]{2,1,0:T(8,128)(2,1)} %bitcast.93, bf16[32,32,1152]{2,1,0:T(8,128)(2,1)S(1)} %bitcast.90, bf16[32,144,1024]{2,1,0:T(8,128)(2,1)} %bitcast.92), custom_call_target="tpu_custom_call" | custom-call | tf_op jit(solution)/shard_map/scatter_gradients/pallas_call | solution.py:434
  395.3 1.3 fusion.26
  397.3 6.9 %adamw.1 = (f32[2,32]{1,0:T(2,128)}, f32[3,32]{1,0:T(4,128)}, f32[32,3072]{1,0:T(8,128)}, f32[32,1024]{1,0:T(8,128)}, f32[32,9216]{1,0:T(8,128)}, /*index=5*/f32...) custom-call(f32[32,128]{1,0:T(8,128)S(1)} %slice.106.refs_0_, ...), custom_call_target="tpu_custom_call" | custom-call | tf_op jit(solution)/shard_map/adamw/pallas_call | solution.py:517
  (95 shorter events, 11.4 us)
Async XLA Ops:
  7.1 147.6 %copy-start.20 = (bf16[1,256,1024]{2,1,0:T(8,128)(2,1)S(1)}, bf16[1,256,1024]{2,1,0:T(8,128)(2,1)}, u32[]{:S(2)}) copy-start(bf16[1,256,1024]{2,1,0:T(8,128)(2,1)} %param.21) | copy-start | bytes 1572868
  154.7 7.3 %copy-start.24 = (s32[1,256]{1,0:T(1,128)S(1)}, s32[1,256]{1,0:T(1,128)}, u32[]{:S(2)}) copy-start(s32[1,256]{1,0:T(1,128)} %param.23) | copy-start | bytes 3076
  159.4 4.0 copy-start.15
  159.6 3.1 collective-permute-start
  163.4 14.0 %copy-start.17 = (bf16[256,1024]{1,0:T(8,128)(2,1)}, bf16[256,1024]{1,0:T(8,128)(2,1)S(1)}, u32[]{:S(2)}) copy-start(bf16[256,1024]{1,0:T(8,128)(2,1)S(1)} %get-tuple-element.96) | copy-start | bytes 1572868
  163.4 14.0 %slice-start = ((s8[9437184]{0:T(1024)(128)(4,1)}), s8[4194304]{0:T(1024)(128)(4,1)S(1)}, s32[]{:S(2)}) async-start(s8[9437184]{0:T(1024)(128)(4,1)} %bitcast.123), calls=%async_computation | async-start | bytes 8388608
  166.1 11.4 %copy-start.19 = (bf16[1,256,1024]{2,1,0:T(8,128)(2,1)S(1)}, bf16[1,256,1024]{2,1,0:T(8,128)(2,1)}, u32[]{:S(2)}) copy-start(bf16[1,256,1024]{2,1,0:T(8,128)(2,1)} %param.22) | copy-start | bytes 1572868
  166.1 11.3 %slice-start.1 = ((s8[9437184]{0:T(1024)(128)(4,1)}), s8[4194304]{0:T(1024)(128)(4,1)S(1)}, s32[]{:S(2)}) async-start(s8[9437184]{0:T(1024)(128)(4,1)} %bitcast.123), calls=%async_computation.1 | async-start | bytes 8388608
  166.1 11.3 %slice-start.2 = ((s8[9437184]{0:T(1024)(128)(4,1)}), s8[1048576]{0:T(1024)(128)(4,1)S(1)}, s32[]{:S(2)}) async-start(s8[9437184]{0:T(1024)(128)(4,1)} %bitcast.123), calls=%async_computation.2 | async-start | bytes 2097152
  217.3 4.2 %copy-start.16 = (f32[256,3072]{1,0:T(8,128)S(1)}, f32[256,3072]{1,0:T(8,128)}, u32[]{:S(2)}) copy-start(f32[256,3072]{1,0:T(8,128)} %copy-done.15) | copy-start | bytes 9437188
  222.0 2.8 copy-start.18
  222.2 3.4 collective-permute-start.2
  223.5 3.7 collective-permute-start.1
  225.7 2.3 copy-start.21
  243.0 152.3 %copy-start.22 = (bf16[1,256,1024]{2,1,0:T(8,128)(2,1)S(1)}, bf16[1,256,1024]{2,1,0:T(8,128)(2,1)}, u32[]{:S(2)}) copy-start(bf16[1,256,1024]{2,1,0:T(8,128)(2,1)} %param.21) | copy-start | bytes 1572868
  243.0 152.3 %copy-start.23 = (f32[256,1024]{1,0:T(8,128)S(1)}, f32[256,1024]{1,0:T(8,128)}, u32[]{:S(2)}) copy-start(f32[256,1024]{1,0:T(8,128)} %get-tuple-element.118) | copy-start | bytes 3145732
  395.1 2.1 copy-start.6
  395.1 2.1 copy-start.7
  395.1 2.2 copy-start.8
  395.1 2.2 copy-start.9
  395.2 2.2 copy-start.10
  395.2 2.1 copy-start.11
  395.2 2.1 copy-start.12
  395.2 2.1 copy-start.13
  (7 other events, 12.2 us)

commit v4 on v3

--- a/solution.py
+++ b/solution.py
@@ -20,6 +20,7 @@
 DECAY = 0.1
 LANES = 128
 VMEM_SCATTER = 46 << 20
+UNIT_TILE = 512
 MESH_ID = pl.DeviceIdType.MESH
 SEQ = ("ring", "core")
 ALL = ("ring", "core", "fsdp")
@@ -54,18 +55,32 @@
         return (snake(spot) * 2 + core) * self.depth + layer
 
     def greet(self):
-        barrier = pltpu.get_barrier_semaphore()
         for device in (self.right, self.left, self.up, self.down, self.sibling):
-            pl.semaphore_signal(barrier, inc=1, device_id=device, device_id_type=MESH_ID)
-        pl.semaphore_wait(barrier, 5)
-
-
-def gather_kernel(chips, depth, count, *refs):
-    shards = refs[:count]
-    wholes = refs[count : 2 * count]
-    sent, from_sibling, from_below, from_ring, kept, late_ring, late_below = refs[2 * count :]
+            pl.semaphore_signal(
+                pltpu.get_barrier_semaphore(), inc=1, device_id=device, device_id_type=MESH_ID
+            )
+
+    def await_greetings(self):
+        pl.semaphore_wait(pltpu.get_barrier_semaphore(), 5)
+
+
+def gather_kernel(chips, depth, groups, *refs):
+    count, inputs = len(groups), sum(groups)
+    wholes = refs[inputs : inputs + count]
+    shards = refs[inputs + count : inputs + 2 * count]
+    sent, from_sibling, from_below, from_ring, kept, late_ring, late_below = refs[
+        inputs + 2 * count :
+    ]
     here = Place(chips, depth)
     here.greet()
+    taken = 0
+    for shard, members in zip(shards, groups):
+        start = 0
+        for member in refs[taken : taken + members]:
+            shard[:, start : start + member.shape[1]] = member[...].astype(shard.dtype)
+            start += member.shape[1]
+        taken += members
+    here.await_greetings()
     late = count - 1
     cuts = [halves(ref.shape[1]) for ref in shards]
 
@@ -203,17 +218,19 @@
         awaited(wholes[which].at[pl.ds(0, shard_count - 1)], sent.at[which])
 
 
-def gather(chips, depth, *shards):
-    count = len(shards)
+def gather(chips, depth, *groups):
+    count = len(groups)
     steps = depth * (chips - 1)
-    anywhere = pl.BlockSpec(memory_space=pl.ANY)
     shard_count = 2 * chips * depth
-    wholes = pl.pallas_call(
-        functools.partial(gather_kernel, chips, depth, count),
-        out_shape=[jax.ShapeDtypeStruct((shard_count,) + x.shape, x.dtype) for x in shards],
-        in_specs=[anywhere] * count,
-        out_specs=[anywhere] * count,
-        scratch_shapes=[
+    shapes = [(g[0].shape[0], sum(x.shape[1] for x in g)) for g in groups]
+    half = jnp.bfloat16
+    return pl.pallas_call(
+        functools.partial(gather_kernel, chips, depth, [len(g) for g in groups]),
+        out_shape=[jax.ShapeDtypeStruct((shard_count,) + shape, half) for shape in shapes],
+        in_specs=[pl.BlockSpec(memory_space=pltpu.VMEM)] * sum(len(g) for g in groups),
+        out_specs=[pl.BlockSpec(memory_space=pl.ANY)] * count,
+        scratch_shapes=[pltpu.VMEM(shape, half) for shape in shapes]
+        + [
             pltpu.SemaphoreType.DMA((count,)),
             pltpu.SemaphoreType.DMA((count,)),
             pltpu.SemaphoreType.DMA((count, depth - 1)),
@@ -222,10 +239,11 @@
             pltpu.SemaphoreType.DMA((2, chips - 1)),
             pltpu.SemaphoreType.DMA((2, chips * (depth - 1))),
         ],
-        compiler_params=pltpu.CompilerParams(collective_id=0, has_side_effects=True),
+        compiler_params=pltpu.CompilerParams(
+            collective_id=0, has_side_effects=True, vmem_limit_bytes=16 << 20
+        ),
         name="gather_weights",
-    )(*shards)
-    return [x.reshape(-1, x.shape[2]) for x in wholes]
+    )(*[x for g in groups for x in g])
 
 
 def scatter_kernel(chips, depth, count, *refs):
@@ -242,6 +260,11 @@
     cuts = [halves(ref.shape[1]) for ref in owned]
     f32 = jnp.float32
 
+    def part(which, shard, way):
+        if len(grads[which].shape) == 4:
+            return grads[which].at[way, shard]
+        return grads[which].at[shard, :, cuts[which][way]]
+
     def place(hop, way):
         away = (chips - hop, hop)[way]
         return (here.spot + away) % chips
@@ -256,7 +279,7 @@
         for way, cut in enumerate(cuts[which]):
             shard = here.shard(place(hop, way), here.core, layer_of(layer_step))
             copy = pltpu.make_async_copy(
-                grads[which].at[shard, :, cut],
+                part(which, shard, way),
                 staged[which].at[hop - 1, :, cut],
                 loaded.at[which, way, hop - 1],
             )
@@ -268,7 +291,7 @@
         for way, cut in enumerate(cuts[which]):
             shard = here.shard(place(hop, way), 1 - here.core, layer_of(layer_step))
             pltpu.make_async_remote_copy(
-                src_ref=grads[which].at[shard, :, cut],
+                src_ref=part(which, shard, way),
                 dst_ref=theirs[which].at[slot, :, cut],
                 send_sem=sent.at[which],
                 recv_sem=from_sibling.at[which, way, slot],
@@ -281,6 +304,7 @@
         for which in range(count):
             load(which, 0, hop, True)
     here.greet()
+    here.await_greetings()
 
     @pl.loop(0, slots)
     def _(slot):
@@ -415,7 +439,8 @@
         step(layer_step, chips)
 
     for which in range(count):
-        most = grads[which].at[pl.ds(0, 2 * slots - 1)]
+        some = pl.ds(0, 2 * slots - 1)
+        most = grads[which].at[:, some] if len(grads[which].shape) == 4 else grads[which].at[some]
         pltpu.make_async_copy(most, most, sent.at[which]).wait()
 
 
@@ -423,17 +448,19 @@
     count = len(grads)
     slots = chips * depth
     steps = depth * (chips - 1)
-    grads = [g.reshape(2 * slots, -1, g.shape[1]) for g in grads]
+    shapes = [
+        (g.shape[1], g.shape[2]) if g.ndim == 3 else (g.shape[2], 2 * g.shape[3]) for g in grads
+    ]
     anywhere = pl.BlockSpec(memory_space=pl.ANY)
     inner = pl.BlockSpec(memory_space=pltpu.VMEM)
 
     def room(most, last):
         leading = [most] * (count - 1) + [last]
-        return [pltpu.VMEM((n,) + g.shape[1:], g.dtype) for n, g in zip(leading, grads)]
+        return [pltpu.VMEM((n,) + x, jnp.bfloat16) for n, x in zip(leading, shapes)]
 
     return pl.pallas_call(
         functools.partial(scatter_kernel, chips, depth, count),
-        out_shape=[jax.ShapeDtypeStruct(g.shape[1:], jnp.float32) for g in grads],
+        out_shape=[jax.ShapeDtypeStruct(x, jnp.float32) for x in shapes],
         in_specs=[anywhere] * count,
         out_specs=[inner] * count,
         scratch_shapes=room(slots, slots)
@@ -501,9 +528,11 @@
 
 
 def adamw_kernel(*refs):
-    grads, state, outs = refs[:5], refs[5:23], refs[23:]
-    vectors = grads[0][...].T
-    found = [vectors[:2], vectors[2:5]] + [ref[...] for ref in grads[1:]]
+    grads, state, outs = refs[:4], refs[4:22], refs[22:]
+    side, lanes, width = grads[0], outs[0].shape[1], outs[3].shape[1]
+    vectors = side[:8, width:]
+    found = [vectors[:2, :lanes], vectors[2:5, :lanes], grads[1][...], side[:, :width]]
+    found += [ref[...] for ref in grads[2:]]
     for index, grad in enumerate(found):
         rate, decay = (RATE_VECTOR, 0.0) if index < 2 else (RATE_MATRIX, DECAY)
         param, first, second = (state[6 * kind + index][...] for kind in range(3))
@@ -517,11 +546,80 @@
     return pl.pallas_call(
         adamw_kernel,
         out_shape=[jax.ShapeDtypeStruct(p.shape, p.dtype) for p in params] * 4,
-        in_specs=[inner] * 23,
+        in_specs=[inner] * 22,
         out_specs=[inner] * 24,
         compiler_params=pltpu.CompilerParams(vmem_limit_bytes=48 << 20),
         name="adamw",
     )(*grads, *params, *firsts, *seconds)
+
+
+def feed_forward_kernel(
+    normed, turned, resid, cot, gate, up, down, out, grad_normed, grad_down, grad_gate_up
+):
+    half = jnp.bfloat16
+
+    @pl.when(pl.program_id(0) == 0)
+    def _():
+        out[...] = resid[...]
+        grad_normed[...] = jnp.zeros_like(grad_normed)
+
+    gate_pre = matmul(normed[...], gate[...])
+    up_pre = matmul(normed[...], up[...])
+    grad_act = matmul_nt(cot[...], down[...])
+    sigmoid_gate = jax.nn.sigmoid(gate_pre)
+    silu_gate = gate_pre * sigmoid_gate
+    act = (silu_gate * up_pre).astype(half)
+    grad_gate = grad_act * up_pre * sigmoid_gate * (1.0 + gate_pre * (1.0 - sigmoid_gate))
+    grad_gate = grad_gate.astype(half)
+    grad_up = (grad_act * silu_gate).astype(half)
+    out[...] += matmul(act, down[...])
+    grad_normed[...] += matmul_nt(grad_gate, gate[...]) + matmul_nt(grad_up, up[...])
+    grad_down[...] = matmul_tn(act, cot[...]).astype(half)
+    grad_gate_up[0] = matmul(turned[...], grad_gate).astype(half)
+    grad_gate_up[1] = matmul(turned[...], grad_up).astype(half)
+
+
+def feed_forward(normed, resid, cot, packed, down):
+    tokens, width = normed.shape
+    units = down.shape[0]
+    tile = UNIT_TILE
+    tiles = units // tile
+    half, single = jnp.bfloat16, jnp.float32
+
+    def fixed(rows, columns):
+        return pl.BlockSpec((rows, columns), lambda i: (0, 0))
+
+    flops = 2 * tokens * width * units * 9
+    return pl.pallas_call(
+        feed_forward_kernel,
+        grid=(tiles,),
+        out_shape=[
+            jax.ShapeDtypeStruct((tokens, width), single),
+            jax.ShapeDtypeStruct((tokens, width), single),
+            jax.ShapeDtypeStruct((units, width), half),
+            jax.ShapeDtypeStruct((2, width, units), half),
+        ],
+        in_specs=[
+            fixed(tokens, width),
+            fixed(width, tokens),
+            fixed(tokens, width),
+            fixed(tokens, width),
+            pl.BlockSpec((width, tile), lambda i: (0, i)),
+            pl.BlockSpec((width, tile), lambda i: (0, i + tiles)),
+            pl.BlockSpec((tile, width), lambda i: (i, 0)),
+        ],
+        out_specs=[
+            fixed(tokens, width),
+            fixed(tokens, width),
+            pl.BlockSpec((tile, width), lambda i: (i, 0)),
+            pl.BlockSpec((2, width, tile), lambda i: (0, 0, i)),
+        ],
+        compiler_params=pltpu.CompilerParams(vmem_limit_bytes=48 << 20),
+        cost_estimate=pl.CostEstimate(
+            flops=flops, bytes_accessed=12 * width * units, transcendentals=tokens * units
+        ),
+        name="feed_forward",
+    )(normed, normed.T, resid, cot, packed, packed, down)
 
 
 def local(
@@ -554,21 +652,21 @@
     chips, depth = lax.axis_size("ring"), lax.axis_size("fsdp")
     in_width = in_proj.shape[1]
     out_width = out_proj.shape[1]
-    vectors = jnp.concatenate([norm_gains, conv_taps], axis=0).T.astype(half)
-    packed = jnp.concatenate(
-        [
-            in_proj.astype(half),
-            out_proj.astype(half),
-            jnp.pad(vectors, ((0, 0), (0, LANES - vectors.shape[1]))),
-            gate_up.astype(half),
-        ],
-        axis=1,
-    )
-    packed_full, down_full = gather(chips, depth, packed, down_proj.astype(half))
-    in_full = packed_full[:, :in_width]
-    out_full = packed_full[:, in_width : in_width + out_width]
-    vector_start = in_width + out_width
-    vectors_full = packed_full[:, vector_start : vector_start + LANES].astype(single).T
+    rows, unit_columns = gate_up.shape
+    shards = 2 * chips * depth
+    vectors = jnp.concatenate([norm_gains, conv_taps], axis=0)
+    vector_count, lanes = vectors.shape
+    corner = ((0, rows - vector_count), (0, LANES - lanes))
+    packed_shards, down_shards = gather(
+        chips, depth, (gate_up, in_proj, out_proj, jnp.pad(vectors, corner)), (down_proj,)
+    )
+    packed_full = packed_shards.reshape(width, -1)
+    down_full = down_shards.reshape(-1, width)
+    out_start = unit_columns + in_width
+    in_full = packed_full[:, unit_columns:out_start]
+    out_full = packed_full[:, out_start : out_start + out_width]
+    vectors_full = packed_shards[:, :vector_count, -LANES:][:, :, :lanes].astype(single)
+    vectors_full = vectors_full.transpose(1, 0, 2).reshape(vector_count, width)
     mixer_full = (None, None, in_full, out_full)
     gains_f = vectors_full[:2]
     taps_f = vectors_full[2:5]
@@ -596,22 +694,10 @@
     resid_two = resid_one + matmul(mixer_act, mixer_full[3])
     scale_two = inverse_rms(resid_two)
     normed_two = (resid_two * scale_two * gains_f[1]).astype(half)
-    ffn_full = (packed_full[:, vector_start + LANES :], down_full)
-    hidden_units = ffn_full[0].shape[1] // 2
-    ffn_pre = matmul(normed_two, ffn_full[0])
-    gate_pre = ffn_pre[:, :hidden_units]
-    up_pre = ffn_pre[:, hidden_units:]
-    sigmoid_gate = jax.nn.sigmoid(gate_pre)
-    silu_gate = gate_pre * sigmoid_gate
-    ffn_act = (silu_gate * up_pre).astype(half)
-    block_out = resid_two + matmul(ffn_act, ffn_full[1])
     cot_rows = cotangent.reshape(tok_count, width)
-    grad_act = matmul_nt(cot_rows, ffn_full[1])
-    grad_gate = grad_act * up_pre * sigmoid_gate * (1.0 + gate_pre * (1.0 - sigmoid_gate))
-    grad_both = jnp.concatenate([grad_gate, grad_act * silu_gate], axis=1).astype(half)
-    grad_normed = matmul_nt(grad_both, ffn_full[0])
-    grad_down = matmul_tn(ffn_act, cot_rows)
-    grad_gate_up = matmul_tn(normed_two, grad_both)
+    block_out, grad_normed, grad_down, grad_gate_up = feed_forward(
+        normed_two, resid_two, cot_rows, packed_full, down_full
+    )
     norm_part, gain_two_grad = norm_backward(resid_two, scale_two, gains_f[1], grad_normed)
     grad_resid = cot_rows.astype(single) + norm_part
     resid_cast = grad_resid.astype(half)
@@ -645,21 +731,23 @@
     grad_in = matmul_tn(normed_one, grad_proj)
     grad_out = matmul_tn(mixer_act, resid_cast)
     vector_grads = jnp.concatenate([grad_gains, grad_taps], axis=0)
-    vector_count = vector_grads.shape[0]
-    vector_columns = jnp.pad(vector_grads.T, ((0, 0), (0, LANES - vector_count))).astype(half)
-    grad_side = jnp.concatenate([vector_columns, grad_out.astype(half)], axis=1)
+    vector_shards = vector_grads.reshape(vector_count, shards, lanes).transpose(1, 0, 2)
+    vector_shards = jnp.pad(vector_shards.astype(half), ((0, 0),) + corner)
+    grad_side = jnp.concatenate(
+        [grad_out.astype(half).reshape(shards, rows, out_width), vector_shards], axis=2
+    )
     gate_owned, in_owned, side_owned, down_owned = scatter(
         chips,
         depth,
-        grad_gate_up.astype(half),
-        grad_in.astype(half),
+        grad_gate_up.reshape(2, shards, rows, -1),
+        grad_in.astype(half).reshape(shards, rows, in_width),
         grad_side,
-        grad_down.astype(half),
+        grad_down.reshape(shards, -1, width),
     )
     params = (norm_gains, conv_taps, in_proj, out_proj, gate_up, down_proj)
     firsts = (first_gains, first_taps, first_in, first_out, first_gate_up, first_down)
     seconds = (second_gains, second_taps, second_in, second_out, second_gate_up, second_down)
-    owned = (side_owned[:, :LANES], in_owned, side_owned[:, LANES:], gate_owned, down_owned)
+    owned = (side_owned, in_owned, gate_owned, down_owned)
     results = adamw(owned, params, firsts, seconds)
     out_rows = block_out.reshape(row_count, length, width)
     grad_rows = grad_hidden.reshape(row_count, length, width)

time: 405 us -> 397 us (0.980)
  matrix products: 71.8 us -> 22.1 us
  Pallas kernels: 303 us -> 331 us
  local copies, waits for them, and re-layouts: 5.23 us -> 22.6 us
    pallas_call x1 -> x2, Pallas kernels: 144 us -> 171 us  [the longest x1 143 us: gather(): pl.pallas_call(functools.partial(gather_kernel, chips, depth, [len(g) for...]
    unnamed x57 -> x72, local copies, waits for them, and re-layouts: 1.03 us -> 21.3 us
    dot_general x4 -> x2, matrix products: 27.8 us -> 8.23 us  [matmul_nt(): lax.dot_general(left, right, (((1,), (1,)), ((), ())), preferred_element_...]
    dot_general x4 -> x2, matrix products: 21.8 us -> 6.65 us  [matmul_tn(): lax.dot_general(left, right, (((0,), (0,)), ((), ())), preferred_element_...]
    dot_general x4 -> x2, matrix products: 22.2 us -> 7.25 us  [matmul(): return jnp.dot(left, right, preferred_element_type=jnp.float32)]
    convert_element_type x4 -> x1, other arithmetic: 5.14 us -> 0.15 us  [local(): normed_two = (resid_two * scale_two * gains_f[1]).astype(half)]
  transfers between devices with their start and end apart: 3 -> 3, of which waited for: 2 -> 1; matrix products, arithmetic and copies ran while one was open for 0% -> 1% of each run, Pallas kernels for 0% -> 0%
where the time goes in v4:
time: 397 us; the launch traced here: 396 us
  Pallas kernels  331 us (83%)
  local copies, waits for them, and re-layouts  22.6 us (6%)
  matrix products  22.1 us (6%)
  other arithmetic  14.1 us (4%)
  starting transfers between devices  5.03 us (1%)
    pallas_call x1, Pallas kernels, scatter(): pl.pallas_call(functools.partial(scatter_kernel, chips, depth, count), ou...  153 us
    pallas_call x1, Pallas kernels, gather(): pl.pallas_call(functools.partial(gather_kernel, chips, depth, [len(g) for...  143 us
    pallas_call x1, Pallas kernels, feed_forward(): pl.pallas_call(feed_forward_kernel, grid=(tiles,), out_shape=[jax.ShapeDt...  28.4 us
    unnamed x72, local copies, waits for them, and re-layouts  21.3 us
    dot_general x2, matrix products, matmul_nt(): lax.dot_general(left, right, (((1,), (1,)), ((), ())), preferred_element_...  8.23 us
  transfers between devices with their start and end apart: 3, of which 1 were waited for; matrix products, arithmetic and copies ran while one was open for 1% of the time, Pallas kernels for 0%

profile of v4, /device:TPU:0, one launch (start us, length us, event | category | flops | bytes accessed | tf_op | source)
XLA Modules:
  0.0 396.5 jit_solution(15925048944303853238)
XLA Ops:
  0.7 1.3 fusion.12
  2.7 1.3 copy-done
  4.0 1.1 copy-done.1
  6.9 142.7 %gather_weights.1 = (bf16[32,32,13440]{2,1,0:T(8,128)(2,1)S(1)}, bf16[32,144,1024]{2,1,0:T(8,128)(2,1)S(1)}) custom-call(f32[32,9216]{1,0:T(8,128)S(1)} %copy-done, f32[32,3072]{1,0:T(8,128)S(1)} %copy-done.3, f32[32,1024]{1,0:T(8,128)S(1)} %copy-done.7, f32[32,128]{1,0:T(8,128)S(1)} %select_maximum_fusion.refs_3_, f32[144,1024]{1,0:T(8,128)S(1)} %copy-done.1), custom_call_target="tpu_custom_call" | custom-call | tf_op jit(solution)/shard_map/gather_weights/pallas_call | solution.py:227
  149.7 3.6 copy-done.21
  153.3 9.1 %copy-done.12 = bf16[32,32,13440]{2,1,0:T(8,128)(2,1)} copy-done((bf16[32,32,13440]{2,1,0:T(8,128)(2,1)}, bf16[32,32,13440]{2,1,0:T(8,128)(2,1)S(1)}, u32[]{:S(2)}) %copy-start.12) | copy-done | bytes 27525144
  162.7 4.7 %fusion.2 = f32[256,3072]{1,0:T(8,128)S(1)} fusion(bf16[1024,13440]{1,0:T(8,128)(2,1)} %bitcast.74, bf16[1,256,1024]{2,1,0:T(8,128)(2,1)S(1)} %copy-done.30, f32[1024]{0:T(1024)S(1)} %mul.260, f32[256]{0:T(256)S(1)} %get-tuple-element.115), kind=kOutput, calls=%fused_computation.3 | convolution fusion | flops 1611661312 | bytes 9966592 | tf_op jit(solution)/shard_map/dot_general | solution.py:492
  167.4 1.7 copy-done.24
  169.2 2.3 collective-permute-start
  172.5 3.1 multiply_convert_fusion.4
  175.6 2.6 multiply_reduce_fusion.5
  179.2 28.4 %feed_forward.1 = (f32[256,1024]{1,0:T(8,128)}, f32[256,1024]{1,0:T(8,128)S(1)}, bf16[4608,1024]{1,0:T(8,128)(2,1)}, bf16[2,1024,4608]{2,1,0:T(8,128)(2,1)}) custom-call(bf16[256,1024]{1,0:T(8,128)(2,1)S(1)} %multiply_convert_fusion.3.normed, bf16[1024,256]{1,0:T(8,128)(2,1)S(1)} %copy.48.turned, f32[256,1024]{1,0:T(8,128)S(1)} %get-tuple-element.121.resid, ...), custom_call_target="tpu_custom_call" | custom-call | flops 21743271936 | bytes 56623104 | tf_op jit(solution)/shard_map/feed_forward/pallas_call | solution.py:593
  208.2 2.5 fusion.6
  210.8 2.5 multiply_reduce_fusion
  214.5 1.3 collective-permute-start.2
  215.8 1.5 collective-permute-start.1
  217.3 2.1 convolution_convert_fusion.1
  219.7 2.1 multiply_convert_fusion.2
  221.8 1.4 multiply_convert_fusion
  223.2 5.7 %fusion.21 = (bf16[1024]{0:T(1024)(128)(2,1)S(1)}, f32[256]{0:T(256)S(1)}, f32[256,1024]{1,0:T(8,128)}) fusion(bf16[1,256,1024]{2,1,0:T(8,128)(2,1)S(1)} %copy-done.31, f32[256]{0:T(256)S(1)} %get-tuple-element.115, f32[1024]{0:T(1024)S(1)} %mul.260, bf16[1024,13440]{1,0:T(8,128)(2,1)} %bitcast.79, bf16[256,1024]{1,0:T(8,128)(2,1)S(1)} %multiply_convert_fusion, ...), kind=kOutput, calls=%fused_computation.29 | convolution fusion | flops 1617165056 | bytes 9445376 | tf_op jit(solution)/shard_map/dot_general | solution.py:502
  229.0 4.6 %convolution_convert_fusion = bf16[1024,3072]{1,0:T(8,128)(2,1)} fusion(bf16[256,1024]{1,0:T(8,128)(2,1)S(1)} %multiply_convert_fusion, bf16[256,1024]{1,0:T(8,128)(2,1)S(1)} %copy-done.34, bf16[256,1024]{1,0:T(8,128)(2,1)S(1)} %get-tuple-element.107, bf16[1,256,1024]{2,1,0:T(8,128)(2,1)S(1)} %copy-done.31, f32[1024]{0:T(1024)S(1)} %mul.260, ...), kind=kOutput, calls=%fused_computation | convolution fusion | flops 1619525632 | bytes 8393728 | tf_op jit(solution)/shard_map/dot_general | solution.py:496
  235.1 1.3 fusion.18
  236.6 153.3 %scatter_gradients.1 = (f32[32,9216]{1,0:T(8,128)S(1)}, f32[32,3072]{1,0:T(8,128)S(1)}, f32[32,1152]{1,0:T(8,128)S(1)}, f32[144,1024]{1,0:T(8,128)S(1)}) custom-call(bf16[2,32,32,4608]{3,2,1,0:T(8,128)(2,1)} %bitcast.81, bf16[32,32,3072]{2,1,0:T(8,128)(2,1)} %bitcast.84, bf16[32,32,1152]{2,1,0:T(8,128)(2,1)S(1)} %fusion.5.refs_2_, ...), custom_call_target="tpu_custom_call" | custom-call | tf_op jit(solution)/shard_map/scatter_gradients/pallas_call | solution.py:461
  390.1 6.2 %adamw.1 = (f32[2,32]{1,0:T(2,128)}, f32[3,32]{1,0:T(4,128)}, f32[32,3072]{1,0:T(8,128)}, f32[32,1024]{1,0:T(8,128)}, f32[32,9216]{1,0:T(8,128)}, /*index=5*/f32...) custom-call(f32[32,1152]{1,0:T(8,128)S(1)} %get-tuple-element.66.ref, ...), custom_call_target="tpu_custom_call" | custom-call | tf_op jit(solution)/shard_map/adamw/pallas_call | solution.py:546
  (101 shorter events, 8.8 us)
Async XLA Ops:
  0.7 162.1 %copy-start.30 = (bf16[1,256,1024]{2,1,0:T(8,128)(2,1)S(1)}, bf16[1,256,1024]{2,1,0:T(8,128)(2,1)}, u32[]{:S(2)}) copy-start(bf16[1,256,1024]{2,1,0:T(8,128)(2,1)} %param.21) | copy-start | bytes 1572868
  153.3 9.1 %copy-start.12 = (bf16[32,32,13440]{2,1,0:T(8,128)(2,1)}, bf16[32,32,13440]{2,1,0:T(8,128)(2,1)S(1)}, u32[]{:S(2)}) copy-start(bf16[32,32,13440]{2,1,0:T(8,128)(2,1)S(1)} %get-tuple-element.60) | copy-start | bytes 82575360
  162.7 8.8 %copy-start.35 = (s32[1,256]{1,0:T(1,128)S(1)}, s32[1,256]{1,0:T(1,128)}, u32[]{:S(2)}) copy-start(s32[1,256]{1,0:T(1,128)} %param.23) | copy-start | bytes 3076
  169.2 3.1 collective-permute-start
  172.5 5.7 %copy-start.22 = (f32[1,258,1024]{2,1,0:T(8,128)}, f32[1,258,1024]{2,1,0:T(8,128)S(1)}, u32[]{:S(2)}) copy-start(f32[1,258,1024]{2,1,0:T(8,128)S(1)} %maximum_convert_fusion) | copy-start | bytes 3170308
  213.3 4.0 copy-start.29
  214.5 5.2 %collective-permute-start.2 = (f32[1,2,1024]{2,1,0:T(2,128)S(1)}, f32[1,2,1024]{2,1,0:T(2,128)S(1)}, u32[]{:S(2)}, u32[]{:S(2)}) collective-permute-start(f32[1,2,1024]{2,1,0:T(2,128)S(1)} %slice.112), channel_id=1, source_target_pairs={{4,0},{8,4},{12,8},{16,12},{20,16},{24,20},{28,24},{5,1},{9,5},{13... | collective-permute-start | bytes 24584 | tf_op jit(solution)/shard_map/ppermute | solution.py:488
  215.8 3.9 collective-permute-start.1
  229.0 4.8 %copy-start.25 = (bf16[1024,1024]{1,0:T(8,128)(2,1)S(1)}, bf16[1024,1024]{1,0:T(8,128)(2,1)}, u32[]{:S(2)}) copy-start(bf16[1024,1024]{1,0:T(8,128)(2,1)} %convolution_convert_fusion.1) | copy-start | bytes 6291460
  236.4 153.5 %copy-start.2 = (f32[144,1024]{1,0:T(8,128)S(1)}, f32[144,1024]{1,0:T(8,128)}, u32[]{:S(2)}) copy-start(f32[144,1024]{1,0:T(8,128)} %refs_9_.1) | copy-start | bytes 1769476
  236.4 153.5 %copy-start.4 = (f32[32,3072]{1,0:T(8,128)S(1)}, f32[32,3072]{1,0:T(8,128)}, u32[]{:S(2)}) copy-start(f32[32,3072]{1,0:T(8,128)} %refs_6_.1) | copy-start | bytes 1179652
  236.4 153.5 %copy-start.5 = (f32[144,1024]{1,0:T(8,128)S(1)}, f32[144,1024]{1,0:T(8,128)}, u32[]{:S(2)}) copy-start(f32[144,1024]{1,0:T(8,128)} %refs_15_.1) | copy-start | bytes 1769476
  236.4 153.5 %copy-start.6 = (f32[144,1024]{1,0:T(8,128)S(1)}, f32[144,1024]{1,0:T(8,128)}, u32[]{:S(2)}) copy-start(f32[144,1024]{1,0:T(8,128)} %refs_21_.1) | copy-start | bytes 1769476
  236.4 153.5 %copy-start.8 = (f32[32,1024]{1,0:T(8,128)S(1)}, f32[32,1024]{1,0:T(8,128)}, u32[]{:S(2)}) copy-start(f32[32,1024]{1,0:T(8,128)} %refs_7_.1) | copy-start | bytes 393220
  236.4 153.5 %copy-start.10 = (f32[32,3072]{1,0:T(8,128)S(1)}, f32[32,3072]{1,0:T(8,128)}, u32[]{:S(2)}) copy-start(f32[32,3072]{1,0:T(8,128)} %refs_12_.1) | copy-start | bytes 1179652
  236.5 153.5 %copy-start.11 = (f32[32,3072]{1,0:T(8,128)S(1)}, f32[32,3072]{1,0:T(8,128)}, u32[]{:S(2)}) copy-start(f32[32,3072]{1,0:T(8,128)} %refs_18_.1) | copy-start | bytes 1179652
  236.5 153.5 %copy-start.13 = (f32[32,1024]{1,0:T(8,128)S(1)}, f32[32,1024]{1,0:T(8,128)}, u32[]{:S(2)}) copy-start(f32[32,1024]{1,0:T(8,128)} %refs_13_.1) | copy-start | bytes 393220
  236.5 153.5 %copy-start.14 = (f32[32,1024]{1,0:T(8,128)S(1)}, f32[32,1024]{1,0:T(8,128)}, u32[]{:S(2)}) copy-start(f32[32,1024]{1,0:T(8,128)} %refs_19_.1) | copy-start | bytes 393220
  236.5 153.5 %copy-start.15 = (f32[3,32]{1,0:T(4,128)S(1)}, f32[3,32]{1,0:T(4,128)}, u32[]{:S(2)}) copy-start(f32[3,32]{1,0:T(4,128)} %refs_5_.1) | copy-start | bytes 1156
  236.5 153.5 %copy-start.16 = (f32[2,32]{1,0:T(2,128)S(1)}, f32[2,32]{1,0:T(2,128)}, u32[]{:S(2)}) copy-start(f32[2,32]{1,0:T(2,128)} %refs_4_.3) | copy-start | bytes 772
  236.5 153.5 %copy-start.17 = (f32[3,32]{1,0:T(4,128)S(1)}, f32[3,32]{1,0:T(4,128)}, u32[]{:S(2)}) copy-start(f32[3,32]{1,0:T(4,128)} %refs_11_.1) | copy-start | bytes 1156
  236.5 153.5 %copy-start.18 = (f32[3,32]{1,0:T(4,128)S(1)}, f32[3,32]{1,0:T(4,128)}, u32[]{:S(2)}) copy-start(f32[3,32]{1,0:T(4,128)} %refs_17_.1) | copy-start | bytes 1156
  236.5 153.5 %copy-start.19 = (f32[2,32]{1,0:T(2,128)S(1)}, f32[2,32]{1,0:T(2,128)}, u32[]{:S(2)}) copy-start(f32[2,32]{1,0:T(2,128)} %refs_10_.1) | copy-start | bytes 772
  236.6 153.5 %copy-start.20 = (f32[2,32]{1,0:T(2,128)S(1)}, f32[2,32]{1,0:T(2,128)}, u32[]{:S(2)}) copy-start(f32[2,32]{1,0:T(2,128)} %refs_16_.1) | copy-start | bytes 772
  (15 other events, 29.4 us)

commit v5 on v4

--- a/solution.py
+++ b/solution.py
@@ -20,6 +20,7 @@
 DECAY = 0.1
 LANES = 128
 VMEM_SCATTER = 46 << 20
+VMEM_GATHER = 60 << 20
 UNIT_TILE = 512
 MESH_ID = pl.DeviceIdType.MESH
 SEQ = ("ring", "core")
@@ -68,15 +69,24 @@
     count, inputs = len(groups), sum(groups)
     wholes = refs[inputs : inputs + count]
     shards = refs[inputs + count : inputs + 2 * count]
-    sent, from_sibling, from_below, from_ring, kept, late_ring, late_below = refs[
-        inputs + 2 * count :
+    wide = refs[inputs + 2 * count : 2 * inputs + 2 * count]
+    loaded, sent, from_sibling, from_below, from_ring, kept, late_ring, late_below = refs[
+        2 * inputs + 2 * count :
     ]
+    loads = [
+        pltpu.make_async_copy(refs[index], wide[index], loaded.at[index])
+        for index in range(inputs)
+    ]
+    for load in loads:
+        load.start()
     here = Place(chips, depth)
     here.greet()
+    for load in loads:
+        load.wait()
     taken = 0
     for shard, members in zip(shards, groups):
         start = 0
-        for member in refs[taken : taken + members]:
+        for member in wide[taken : taken + members]:
             shard[:, start : start + member.shape[1]] = member[...].astype(shard.dtype)
             start += member.shape[1]
         taken += members
@@ -227,10 +237,12 @@
     return pl.pallas_call(
         functools.partial(gather_kernel, chips, depth, [len(g) for g in groups]),
         out_shape=[jax.ShapeDtypeStruct((shard_count,) + shape, half) for shape in shapes],
-        in_specs=[pl.BlockSpec(memory_space=pltpu.VMEM)] * sum(len(g) for g in groups),
+        in_specs=[pl.BlockSpec(memory_space=pl.ANY)] * sum(len(g) for g in groups),
         out_specs=[pl.BlockSpec(memory_space=pl.ANY)] * count,
         scratch_shapes=[pltpu.VMEM(shape, half) for shape in shapes]
+        + [pltpu.VMEM(x.shape, x.dtype) for g in groups for x in g]
         + [
+            pltpu.SemaphoreType.DMA((sum(len(g) for g in groups),)),
             pltpu.SemaphoreType.DMA((count,)),
             pltpu.SemaphoreType.DMA((count,)),
             pltpu.SemaphoreType.DMA((count, depth - 1)),
@@ -240,7 +252,7 @@
             pltpu.SemaphoreType.DMA((2, chips * (depth - 1))),
         ],
         compiler_params=pltpu.CompilerParams(
-            collective_id=0, has_side_effects=True, vmem_limit_bytes=16 << 20
+            collective_id=0, has_side_effects=True, vmem_limit_bytes=VMEM_GATHER
         ),
         name="gather_weights",
     )(*[x for g in groups for x in g])
@@ -422,18 +434,19 @@
         def _():
             load(late, layer_step + 1, hop, True)
 
-    step(0, 1)
+    for place_in_line in range(1, chips - 1):
+        for layer_step in range(min(place_in_line, depth)):
+            step(layer_step, place_in_line - layer_step)
 
     @pl.loop(0, depth)
     def _(layer_step):
-        late_step(layer_step, 1)
-        for hop in range(2, chips):
-            step(layer_step, hop)
-            late_step(layer_step, hop)
-
-        @pl.when(layer_step < depth - 1)
-        def _():
-            step(layer_step + 1, 1)
+        for hop in range(chips - 1, 0, -1):
+            late_step(layer_step, chips - hop)
+            ahead = chips - 1 - hop
+
+            @pl.when(layer_step + ahead < depth)
+            def _():
+                step(layer_step + ahead, hop)
 
         late_step(layer_step, chips)
         step(layer_step, chips)

time: 397 us -> 393 us (0.990)
  local copies, waits for them, and re-layouts: 22.6 us -> 5.66 us
  Pallas kernels: 331 us -> 342 us
    unnamed x72 -> x60, local copies, waits for them, and re-layouts: 21.3 us -> 4.32 us
    pallas_call x1, Pallas kernels: 153 us -> 163 us  [scatter(): pl.pallas_call(functools.partial(scatter_kernel, chips, depth, count), ou...]
where the time goes in v5:
time: 393 us
  Pallas kernels  342 us (87%)
  matrix products  22.2 us (6%)
  other arithmetic  15.5 us (4%)
  local copies, waits for them, and re-layouts  5.66 us (1%)
  starting transfers between devices  5.03 us (1%)
    pallas_call x1, Pallas kernels, scatter(): pl.pallas_call(functools.partial(scatter_kernel, chips, depth, count), ou...  163 us
    pallas_call x1, Pallas kernels, gather(): pl.pallas_call(functools.partial(gather_kernel, chips, depth, [len(g) for...  144 us
    pallas_call x1, Pallas kernels, feed_forward(): pl.pallas_call(feed_forward_kernel, grid=(tiles,), out_shape=[jax.ShapeDt...  28.4 us
    dot_general x2, matrix products, matmul_nt(): lax.dot_general(left, right, (((1,), (1,)), ((), ())), preferred_element_...  8.23 us
  transfers between devices with their start and end apart: 3, of which 1 were waited for; matrix products, arithmetic and copies ran while one was open for 1% of the time, Pallas kernels for 0%

profile of v5, /device:TPU:0, one launch (start us, length us, event | category | flops | bytes accessed | tf_op | source)
XLA Modules:
  0.0 392.6 jit_solution(14483552218416097095)
XLA Ops:
  0.7 1.3 fusion.12
  2.0 1.3 select_maximum_fusion.refs_3_
  3.3 144.4 %gather_weights.1 = (bf16[32,32,13440]{2,1,0:T(8,128)(2,1)}, bf16[32,144,1024]{2,1,0:T(8,128)(2,1)}) custom-call(f32[32,9216]{1,0:T(8,128)} %refs_8_.1, f32[32,3072]{1,0:T(8,128)} %refs_6_.1, f32[32,1024]{1,0:T(8,128)} %refs_7_.1, f32[32,128]{1,0:T(8,128)} %select_maximum_fusion.refs_3_, f32[144,1024]{1,0:T(8,128)} %refs_9_.1), custom_call_target="tpu_custom_call" | custom-call | tf_op jit(solution)/shard_map/gather_weights/pallas_call | solution.py:237
  147.7 0.9 convert_bitcast_fusion
  148.9 4.7 %fusion.2 = f32[256,3072]{1,0:T(8,128)S(1)} fusion(bf16[1024,13440]{1,0:T(8,128)(2,1)} %bitcast.79, bf16[1,256,1024]{2,1,0:T(8,128)(2,1)S(1)} %copy-done.24, f32[1024]{0:T(1024)S(1)} %mul.260, f32[256]{0:T(256)S(1)} %get-tuple-element.115), kind=kOutput, calls=%fused_computation.3 | convolution fusion | flops 1611661312 | bytes 9966592 | tf_op jit(solution)/shard_map/dot_general | solution.py:505
  153.6 1.6 copy-done.18
  155.4 2.3 collective-permute-start
  158.6 3.1 multiply_convert_fusion.4
  161.7 2.6 multiply_reduce_fusion.5
  165.4 28.4 %feed_forward.1 = (f32[256,1024]{1,0:T(8,128)}, f32[256,1024]{1,0:T(8,128)S(1)}, bf16[4608,1024]{1,0:T(8,128)(2,1)}, bf16[2,1024,4608]{2,1,0:T(8,128)(2,1)}) custom-call(bf16[256,1024]{1,0:T(8,128)(2,1)S(1)} %multiply_convert_fusion.3.normed, bf16[1024,256]{1,0:T(8,128)(2,1)S(1)} %copy.48.turned, f32[256,1024]{1,0:T(8,128)S(1)} %get-tuple-element.121.resid, ...), custom_call_target="tpu_custom_call" | custom-call | flops 21743271936 | bytes 56623104 | tf_op jit(solution)/shard_map/feed_forward/pallas_call | solution.py:606
  194.3 2.5 fusion.6
  196.9 2.5 multiply_reduce_fusion
  199.7 0.9 copy-done.20
  200.6 1.3 collective-permute-start.2
  201.9 1.5 collective-permute-start.1
  203.4 2.1 convolution_convert_fusion.1
  205.8 2.1 multiply_convert_fusion.2
  208.0 1.4 multiply_convert_fusion
  209.4 5.7 %fusion.21 = (bf16[1024]{0:T(1024)(128)(2,1)S(1)}, f32[256]{0:T(256)S(1)}, f32[256,1024]{1,0:T(8,128)}) fusion(bf16[1,256,1024]{2,1,0:T(8,128)(2,1)S(1)} %copy-done.25, f32[256]{0:T(256)S(1)} %get-tuple-element.115, f32[1024]{0:T(1024)S(1)} %mul.260, bf16[1024,13440]{1,0:T(8,128)(2,1)} %bitcast.84, bf16[256,1024]{1,0:T(8,128)(2,1)S(1)} %multiply_convert_fusion, ...), kind=kOutput, calls=%fused_computation.29 | convolution fusion | flops 1617165056 | bytes 9445376 | tf_op jit(solution)/shard_map/dot_general | solution.py:515
  215.1 4.6 %convolution_convert_fusion = bf16[1024,3072]{1,0:T(8,128)(2,1)} fusion(bf16[256,1024]{1,0:T(8,128)(2,1)S(1)} %multiply_convert_fusion, bf16[256,1024]{1,0:T(8,128)(2,1)S(1)} %copy-done.28, bf16[256,1024]{1,0:T(8,128)(2,1)S(1)} %get-tuple-element.107, bf16[1,256,1024]{2,1,0:T(8,128)(2,1)S(1)} %copy-done.25, f32[1024]{0:T(1024)S(1)} %mul.260, ...), kind=kOutput, calls=%fused_computation | convolution fusion | flops 1619525632 | bytes 8393728 | tf_op jit(solution)/shard_map/dot_general | solution.py:509
  220.2 0.8 copy-done.26
  221.3 1.3 fusion.18
  222.7 163.3 %scatter_gradients.1 = (f32[32,9216]{1,0:T(8,128)S(1)}, f32[32,3072]{1,0:T(8,128)S(1)}, f32[32,1152]{1,0:T(8,128)S(1)}, f32[144,1024]{1,0:T(8,128)S(1)}) custom-call(bf16[2,32,32,4608]{3,2,1,0:T(8,128)(2,1)} %bitcast.74, bf16[32,32,3072]{2,1,0:T(8,128)(2,1)} %bitcast.77, bf16[32,32,1152]{2,1,0:T(8,128)(2,1)S(1)} %fusion.5.refs_2_, ...), custom_call_target="tpu_custom_call" | custom-call | tf_op jit(solution)/shard_map/scatter_gradients/pallas_call | solution.py:474
  386.2 6.2 %adamw.1 = (f32[2,32]{1,0:T(2,128)}, f32[3,32]{1,0:T(4,128)}, f32[32,3072]{1,0:T(8,128)}, f32[32,1024]{1,0:T(8,128)}, f32[32,9216]{1,0:T(8,128)}, /*index=5*/f32...) custom-call(f32[32,1152]{1,0:T(8,128)S(1)} %get-tuple-element.66.ref, ...), custom_call_target="tpu_custom_call" | custom-call | tf_op jit(solution)/shard_map/adamw/pallas_call | solution.py:559
  (89 shorter events, 4.5 us)
Async XLA Ops:
  0.7 148.2 %copy-start.24 = (bf16[1,256,1024]{2,1,0:T(8,128)(2,1)S(1)}, bf16[1,256,1024]{2,1,0:T(8,128)(2,1)}, u32[]{:S(2)}) copy-start(bf16[1,256,1024]{2,1,0:T(8,128)(2,1)} %param.21) | copy-start | bytes 1572868
  148.9 8.8 %copy-start.29 = (s32[1,256]{1,0:T(1,128)S(1)}, s32[1,256]{1,0:T(1,128)}, u32[]{:S(2)}) copy-start(s32[1,256]{1,0:T(1,128)} %param.23) | copy-start | bytes 3076
  155.4 3.1 collective-permute-start
  158.6 5.7 %copy-start.16 = (f32[1,258,1024]{2,1,0:T(8,128)}, f32[1,258,1024]{2,1,0:T(8,128)S(1)}, u32[]{:S(2)}) copy-start(f32[1,258,1024]{2,1,0:T(8,128)S(1)} %maximum_convert_fusion) | copy-start | bytes 3170308
  199.4 4.0 %copy-start.23 = (bf16[256,1024]{1,0:T(8,128)(2,1)S(1)}, bf16[256,1024]{1,0:T(8,128)(2,1)}, u32[]{:S(2)}) copy-start(bf16[256,1024]{1,0:T(8,128)(2,1)} %copy-done.22) | copy-start | bytes 1572868
  200.6 5.2 %collective-permute-start.2 = (f32[1,2,1024]{2,1,0:T(2,128)S(1)}, f32[1,2,1024]{2,1,0:T(2,128)S(1)}, u32[]{:S(2)}, u32[]{:S(2)}) collective-permute-start(f32[1,2,1024]{2,1,0:T(2,128)S(1)} %slice.112), channel_id=1, source_target_pairs={{4,0},{8,4},{12,8},{16,12},{20,16},{24,20},{28,24},{5,1},{9,5},{13... | collective-permute-start | bytes 24584 | tf_op jit(solution)/shard_map/ppermute | solution.py:501
  201.9 3.9 collective-permute-start.1
  205.8 3.6 copy-start.28
  215.1 4.8 %copy-start.19 = (bf16[1024,1024]{1,0:T(8,128)(2,1)S(1)}, bf16[1024,1024]{1,0:T(8,128)(2,1)}, u32[]{:S(2)}) copy-start(bf16[1024,1024]{1,0:T(8,128)(2,1)} %convolution_convert_fusion.1) | copy-start | bytes 6291460
  222.6 163.5 %copy-start = (f32[144,1024]{1,0:T(8,128)S(1)}, f32[144,1024]{1,0:T(8,128)}, u32[]{:S(2)}) copy-start(f32[144,1024]{1,0:T(8,128)} %refs_9_.1) | copy-start | bytes 1769476
  222.6 163.5 %copy-start.1 = (f32[32,3072]{1,0:T(8,128)S(1)}, f32[32,3072]{1,0:T(8,128)}, u32[]{:S(2)}) copy-start(f32[32,3072]{1,0:T(8,128)} %refs_6_.1) | copy-start | bytes 1179652
  222.6 163.5 %copy-start.2 = (f32[144,1024]{1,0:T(8,128)S(1)}, f32[144,1024]{1,0:T(8,128)}, u32[]{:S(2)}) copy-start(f32[144,1024]{1,0:T(8,128)} %refs_15_.1) | copy-start | bytes 1769476
  222.6 163.5 %copy-start.3 = (f32[144,1024]{1,0:T(8,128)S(1)}, f32[144,1024]{1,0:T(8,128)}, u32[]{:S(2)}) copy-start(f32[144,1024]{1,0:T(8,128)} %refs_21_.1) | copy-start | bytes 1769476
  222.6 163.5 %copy-start.4 = (f32[32,1024]{1,0:T(8,128)S(1)}, f32[32,1024]{1,0:T(8,128)}, u32[]{:S(2)}) copy-start(f32[32,1024]{1,0:T(8,128)} %refs_7_.1) | copy-start | bytes 393220
  222.6 163.5 %copy-start.6 = (f32[32,3072]{1,0:T(8,128)S(1)}, f32[32,3072]{1,0:T(8,128)}, u32[]{:S(2)}) copy-start(f32[32,3072]{1,0:T(8,128)} %refs_12_.1) | copy-start | bytes 1179652
  222.6 163.5 %copy-start.7 = (f32[32,3072]{1,0:T(8,128)S(1)}, f32[32,3072]{1,0:T(8,128)}, u32[]{:S(2)}) copy-start(f32[32,3072]{1,0:T(8,128)} %refs_18_.1) | copy-start | bytes 1179652
  222.6 163.5 %copy-start.8 = (f32[32,1024]{1,0:T(8,128)S(1)}, f32[32,1024]{1,0:T(8,128)}, u32[]{:S(2)}) copy-start(f32[32,1024]{1,0:T(8,128)} %refs_13_.1) | copy-start | bytes 393220
  222.6 163.5 %copy-start.9 = (f32[32,1024]{1,0:T(8,128)S(1)}, f32[32,1024]{1,0:T(8,128)}, u32[]{:S(2)}) copy-start(f32[32,1024]{1,0:T(8,128)} %refs_19_.1) | copy-start | bytes 393220
  222.6 163.5 %copy-start.10 = (f32[3,32]{1,0:T(4,128)S(1)}, f32[3,32]{1,0:T(4,128)}, u32[]{:S(2)}) copy-start(f32[3,32]{1,0:T(4,128)} %refs_5_.1) | copy-start | bytes 1156
  222.6 163.5 %copy-start.11 = (f32[2,32]{1,0:T(2,128)S(1)}, f32[2,32]{1,0:T(2,128)}, u32[]{:S(2)}) copy-start(f32[2,32]{1,0:T(2,128)} %refs_4_.3) | copy-start | bytes 772
  222.7 163.5 %copy-start.12 = (f32[3,32]{1,0:T(4,128)S(1)}, f32[3,32]{1,0:T(4,128)}, u32[]{:S(2)}) copy-start(f32[3,32]{1,0:T(4,128)} %refs_11_.1) | copy-start | bytes 1156
  222.7 163.5 %copy-start.13 = (f32[3,32]{1,0:T(4,128)S(1)}, f32[3,32]{1,0:T(4,128)}, u32[]{:S(2)}) copy-start(f32[3,32]{1,0:T(4,128)} %refs_17_.1) | copy-start | bytes 1156
  222.7 163.5 %copy-start.14 = (f32[2,32]{1,0:T(2,128)S(1)}, f32[2,32]{1,0:T(2,128)}, u32[]{:S(2)}) copy-start(f32[2,32]{1,0:T(2,128)} %refs_10_.1) | copy-start | bytes 772
  222.7 163.5 %copy-start.15 = (f32[2,32]{1,0:T(2,128)S(1)}, f32[2,32]{1,0:T(2,128)}, u32[]{:S(2)}) copy-start(f32[2,32]{1,0:T(2,128)} %refs_16_.1) | copy-start | bytes 772
  (9 other events, 18.0 us)

commit v6 on v5

--- a/solution.py
+++ b/solution.py
@@ -320,7 +320,7 @@
 
     @pl.loop(0, slots)
     def _(slot):
-        for which in range(count):
+        for which in reversed(range(count)):
             hand_over(which, slot)
 
     def got(ref, semaphore):
@@ -434,22 +434,29 @@
         def _():
             load(late, layer_step + 1, hop, True)
 
-    for place_in_line in range(1, chips - 1):
-        for layer_step in range(min(place_in_line, depth)):
-            step(layer_step, place_in_line - layer_step)
+    late_step(0, 1)
+    step(0, 1)
+    for hop in range(2, chips + 1):
+        late_step(0, hop)
 
     @pl.loop(0, depth)
     def _(layer_step):
-        for hop in range(chips - 1, 0, -1):
-            late_step(layer_step, chips - hop)
-            ahead = chips - 1 - hop
-
-            @pl.when(layer_step + ahead < depth)
+        def late_ahead(hop):
+            @pl.when(layer_step < depth - 1)
             def _():
-                step(layer_step + ahead, hop)
-
-        late_step(layer_step, chips)
+                late_step(layer_step + 1, hop)
+
+        for hop in range(2, chips):
+            step(layer_step, hop)
+            late_ahead(hop - 1)
+
+        @pl.when(layer_step < depth - 1)
+        def _():
+            step(layer_step + 1, 1)
+
+        late_ahead(chips - 1)
         step(layer_step, chips)
+        late_ahead(chips)
 
     for which in range(count):
         some = pl.ds(0, 2 * slots - 1)
@@ -567,12 +574,13 @@
 
 
 def feed_forward_kernel(
-    normed, turned, resid, cot, gate, up, down, out, grad_normed, grad_down, grad_gate_up
+    normed, resid, cot, gate, up, down, out, grad_normed, grad_down, grad_gate_up, turned
 ):
     half = jnp.bfloat16
 
     @pl.when(pl.program_id(0) == 0)
     def _():
+        turned[...] = normed[...].T
         out[...] = resid[...]
         grad_normed[...] = jnp.zeros_like(grad_normed)
 
@@ -614,7 +622,6 @@
         ],
         in_specs=[
             fixed(tokens, width),
-            fixed(width, tokens),
             fixed(tokens, width),
             fixed(tokens, width),
             pl.BlockSpec((width, tile), lambda i: (0, i)),
@@ -627,12 +634,13 @@
             pl.BlockSpec((tile, width), lambda i: (i, 0)),
             pl.BlockSpec((2, width, tile), lambda i: (0, 0, i)),
         ],
+        scratch_shapes=[pltpu.VMEM((width, tokens), half)],
         compiler_params=pltpu.CompilerParams(vmem_limit_bytes=48 << 20),
         cost_estimate=pl.CostEstimate(
             flops=flops, bytes_accessed=12 * width * units, transcendentals=tokens * units
         ),
         name="feed_forward",
-    )(normed, normed.T, resid, cot, packed, packed, down)
+    )(normed, resid, cot, packed, packed, down)
 
 
 def local(

time: 393 us -> 374 us (0.952)
  Pallas kernels: 342 us -> 326 us
    pallas_call x1, Pallas kernels: 163 us -> 147 us  [scatter(): pl.pallas_call(functools.partial(scatter_kernel, chips, depth, count), ou...]
where the time goes in v6:
time: 374 us; the launch traced here: 373 us
  Pallas kernels  326 us (87%)
  matrix products  22 us (6%)
  other arithmetic  13.8 us (4%)
  starting transfers between devices  5.03 us (1%)
  local copies, waits for them, and re-layouts  4.79 us (1%)
    pallas_call x1, Pallas kernels, scatter(): pl.pallas_call(functools.partial(scatter_kernel, chips, depth, count), ou...  147 us
    pallas_call x1, Pallas kernels, gather(): pl.pallas_call(functools.partial(gather_kernel, chips, depth, [len(g) for...  144 us
    pallas_call x1, Pallas kernels, feed_forward(): pl.pallas_call(feed_forward_kernel, grid=(tiles,), out_shape=[jax.ShapeDt...  28.6 us
    dot_general x2, matrix products, matmul_nt(): lax.dot_general(left, right, (((1,), (1,)), ((), ())), preferred_element_...  8.07 us
  transfers between devices with their start and end apart: 3, of which 1 were waited for; matrix products, arithmetic and copies ran while one was open for 1% of the time, Pallas kernels for 0%

profile of v6, /device:TPU:0, one launch (start us, length us, event | category | flops | bytes accessed | tf_op | source)
XLA Modules:
  0.0 373.5 jit_solution(7591667237643949081)
XLA Ops:
  0.7 1.2 fusion.12
  1.9 1.3 select_maximum_fusion.refs_3_
  3.2 144.4 %gather_weights.1 = (bf16[32,32,13440]{2,1,0:T(8,128)(2,1)}, bf16[32,144,1024]{2,1,0:T(8,128)(2,1)}) custom-call(f32[32,9216]{1,0:T(8,128)} %refs_8_.1, f32[32,3072]{1,0:T(8,128)} %refs_6_.1, f32[32,1024]{1,0:T(8,128)} %refs_7_.1, f32[32,128]{1,0:T(8,128)} %select_maximum_fusion.refs_3_, f32[144,1024]{1,0:T(8,128)} %refs_9_.1), custom_call_target="tpu_custom_call" | custom-call | tf_op jit(solution)/shard_map/gather_weights/pallas_call | solution.py:237
  147.6 0.9 convert_bitcast_fusion
  148.8 4.9 %fusion.2 = f32[256,3072]{1,0:T(8,128)S(1)} fusion(bf16[1024,13440]{1,0:T(8,128)(2,1)} %bitcast.77, bf16[1,256,1024]{2,1,0:T(8,128)(2,1)} %param.21, f32[1024]{0:T(1024)S(1)} %mul.260, f32[256]{0:T(256)S(1)} %get-tuple-element.115), kind=kOutput, calls=%fused_computation.3 | convolution fusion | flops 1611661312 | bytes 9966592 | tf_op jit(solution)/shard_map/dot_general | solution.py:512
  153.8 0.9 copy-done.19
  154.8 2.3 collective-permute-start
  157.9 1.2 maximum_convert_fusion
  160.1 2.5 multiply_reduce_fusion.5
  162.8 28.6 %feed_forward.1 = (f32[256,1024]{1,0:T(8,128)}, f32[256,1024]{1,0:T(8,128)S(1)}, bf16[4608,1024]{1,0:T(8,128)(2,1)}, bf16[2,1024,4608]{2,1,0:T(8,128)(2,1)}) custom-call(bf16[256,1024]{1,0:T(8,128)(2,1)S(1)} %multiply_convert_fusion.3.normed, f32[256,1024]{1,0:T(8,128)S(1)} %get-tuple-element.121.resid, bf16[256,1024]{1,0:T(8,128)(2,1)S(1)} %bitcast.71, ...), custom_call_target="tpu_custom_call" | custom-call | flops 21743271936 | bytes 56623104 | tf_op jit(solution)/shard_map/feed_forward/pallas_call | solution.py:614
  191.9 2.3 fusion.6
  194.3 2.5 multiply_reduce_fusion
  197.0 0.9 copy-done.18
  198.0 1.3 collective-permute-start.2
  199.3 1.5 collective-permute-start.1
  200.8 2.1 convolution_convert_fusion.1
  203.2 2.1 multiply_convert_fusion.2
  205.3 1.4 multiply_convert_fusion
  206.7 5.7 %fusion.21 = (bf16[1024]{0:T(1024)(128)(2,1)S(1)}, f32[256]{0:T(256)S(1)}, f32[256,1024]{1,0:T(8,128)}) fusion(bf16[1,256,1024]{2,1,0:T(8,128)(2,1)S(1)} %copy-done.21, f32[256]{0:T(256)S(1)} %get-tuple-element.115, f32[1024]{0:T(1024)S(1)} %mul.260, bf16[1024,13440]{1,0:T(8,128)(2,1)} %bitcast.82, bf16[256,1024]{1,0:T(8,128)(2,1)S(1)} %multiply_convert_fusion, ...), kind=kOutput, calls=%fused_computation.29 | convolution fusion | flops 1617165056 | bytes 9445376 | tf_op jit(solution)/shard_map/dot_general | solution.py:522
  212.4 4.6 %convolution_convert_fusion = bf16[1024,3072]{1,0:T(8,128)(2,1)} fusion(bf16[256,1024]{1,0:T(8,128)(2,1)S(1)} %multiply_convert_fusion, bf16[256,1024]{1,0:T(8,128)(2,1)S(1)} %copy-done.24, bf16[256,1024]{1,0:T(8,128)(2,1)S(1)} %get-tuple-element.107, bf16[1,256,1024]{2,1,0:T(8,128)(2,1)S(1)} %copy-done.21, f32[1024]{0:T(1024)S(1)} %mul.260, ...), kind=kOutput, calls=%fused_computation | convolution fusion | flops 1619525632 | bytes 8393728 | tf_op jit(solution)/shard_map/dot_general | solution.py:516
  217.5 0.8 copy-done.22
  218.6 1.3 fusion.18
  220.0 146.9 %scatter_gradients.1 = (f32[32,9216]{1,0:T(8,128)S(1)}, f32[32,3072]{1,0:T(8,128)S(1)}, f32[32,1152]{1,0:T(8,128)S(1)}, f32[144,1024]{1,0:T(8,128)S(1)}) custom-call(bf16[2,32,32,4608]{3,2,1,0:T(8,128)(2,1)} %bitcast.72, bf16[32,32,3072]{2,1,0:T(8,128)(2,1)} %bitcast.75, bf16[32,32,1152]{2,1,0:T(8,128)(2,1)S(1)} %fusion.5.refs_2_, ...), custom_call_target="tpu_custom_call" | custom-call | tf_op jit(solution)/shard_map/scatter_gradients/pallas_call | solution.py:481
  367.1 6.2 %adamw.1 = (f32[2,32]{1,0:T(2,128)}, f32[3,32]{1,0:T(4,128)}, f32[32,3072]{1,0:T(8,128)}, f32[32,1024]{1,0:T(8,128)}, f32[32,9216]{1,0:T(8,128)}, /*index=5*/f32...) custom-call(f32[32,1152]{1,0:T(8,128)S(1)} %get-tuple-element.66.ref, ...), custom_call_target="tpu_custom_call" | custom-call | tf_op jit(solution)/shard_map/adamw/pallas_call | solution.py:566
  (79 shorter events, 4.5 us)
Async XLA Ops:
  148.8 8.3 %copy-start.25 = (s32[1,256]{1,0:T(1,128)S(1)}, s32[1,256]{1,0:T(1,128)}, u32[]{:S(2)}) copy-start(s32[1,256]{1,0:T(1,128)} %param.23) | copy-start | bytes 3076
  153.7 5.9 %copy-start.16 = (f32[256,3072]{1,0:T(8,128)}, f32[256,3072]{1,0:T(8,128)S(1)}, u32[]{:S(2)}) copy-start(f32[256,3072]{1,0:T(8,128)S(1)} %fusion.2) | copy-start | bytes 9437188
  154.8 3.1 collective-permute-start
  160.1 2.6 copy-start.5
  198.0 5.2 %collective-permute-start.2 = (f32[1,2,1024]{2,1,0:T(2,128)S(1)}, f32[1,2,1024]{2,1,0:T(2,128)S(1)}, u32[]{:S(2)}, u32[]{:S(2)}) collective-permute-start(f32[1,2,1024]{2,1,0:T(2,128)S(1)} %slice.112), channel_id=1, source_target_pairs={{4,0},{8,4},{12,8},{16,12},{20,16},{24,20},{28,24},{5,1},{9,5},{13... | collective-permute-start | bytes 24584 | tf_op jit(solution)/shard_map/ppermute | solution.py:508
  199.3 3.9 %collective-permute-start.1 = (f32[1,2,1024]{2,1,0:T(2,128)S(1)}, f32[1,2,1024]{2,1,0:T(2,128)S(1)}, u32[]{:S(2)}, u32[]{:S(2)}) collective-permute-start(f32[1,2,1024]{2,1,0:T(2,128)S(1)} %slice.111), channel_id=1, source_target_pairs={{4,0},{8,4},{12,8},{16,12},{20,16},{24,20},{28,24},{5,1},{9,5},{13... | collective-permute-start | bytes 24584 | tf_op jit(solution)/shard_map/ppermute | solution.py:508
  203.1 3.6 copy-start.21
  203.1 3.6 copy-start.24
  212.4 4.8 %copy-start.17 = (bf16[1024,1024]{1,0:T(8,128)(2,1)S(1)}, bf16[1024,1024]{1,0:T(8,128)(2,1)}, u32[]{:S(2)}) copy-start(bf16[1024,1024]{1,0:T(8,128)(2,1)} %convolution_convert_fusion.1) | copy-start | bytes 6291460
  219.9 147.0 %copy-start = (f32[144,1024]{1,0:T(8,128)S(1)}, f32[144,1024]{1,0:T(8,128)}, u32[]{:S(2)}) copy-start(f32[144,1024]{1,0:T(8,128)} %refs_9_.1) | copy-start | bytes 1769476
  219.9 147.0 %copy-start.1 = (f32[32,3072]{1,0:T(8,128)S(1)}, f32[32,3072]{1,0:T(8,128)}, u32[]{:S(2)}) copy-start(f32[32,3072]{1,0:T(8,128)} %refs_6_.1) | copy-start | bytes 1179652
  219.9 147.0 %copy-start.2 = (f32[144,1024]{1,0:T(8,128)S(1)}, f32[144,1024]{1,0:T(8,128)}, u32[]{:S(2)}) copy-start(f32[144,1024]{1,0:T(8,128)} %refs_15_.1) | copy-start | bytes 1769476
  219.9 147.0 %copy-start.3 = (f32[144,1024]{1,0:T(8,128)S(1)}, f32[144,1024]{1,0:T(8,128)}, u32[]{:S(2)}) copy-start(f32[144,1024]{1,0:T(8,128)} %refs_21_.1) | copy-start | bytes 1769476
  219.9 147.0 %copy-start.4 = (f32[32,1024]{1,0:T(8,128)S(1)}, f32[32,1024]{1,0:T(8,128)}, u32[]{:S(2)}) copy-start(f32[32,1024]{1,0:T(8,128)} %refs_7_.1) | copy-start | bytes 393220
  219.9 147.0 %copy-start.6 = (f32[32,3072]{1,0:T(8,128)S(1)}, f32[32,3072]{1,0:T(8,128)}, u32[]{:S(2)}) copy-start(f32[32,3072]{1,0:T(8,128)} %refs_12_.1) | copy-start | bytes 1179652
  219.9 147.0 %copy-start.7 = (f32[32,3072]{1,0:T(8,128)S(1)}, f32[32,3072]{1,0:T(8,128)}, u32[]{:S(2)}) copy-start(f32[32,3072]{1,0:T(8,128)} %refs_18_.1) | copy-start | bytes 1179652
  219.9 147.0 %copy-start.8 = (f32[32,1024]{1,0:T(8,128)S(1)}, f32[32,1024]{1,0:T(8,128)}, u32[]{:S(2)}) copy-start(f32[32,1024]{1,0:T(8,128)} %refs_13_.1) | copy-start | bytes 393220
  220.0 147.0 %copy-start.9 = (f32[32,1024]{1,0:T(8,128)S(1)}, f32[32,1024]{1,0:T(8,128)}, u32[]{:S(2)}) copy-start(f32[32,1024]{1,0:T(8,128)} %refs_19_.1) | copy-start | bytes 393220
  220.0 147.0 %copy-start.10 = (f32[3,32]{1,0:T(4,128)S(1)}, f32[3,32]{1,0:T(4,128)}, u32[]{:S(2)}) copy-start(f32[3,32]{1,0:T(4,128)} %refs_5_.1) | copy-start | bytes 1156
  220.0 147.0 %copy-start.11 = (f32[2,32]{1,0:T(2,128)S(1)}, f32[2,32]{1,0:T(2,128)}, u32[]{:S(2)}) copy-start(f32[2,32]{1,0:T(2,128)} %refs_4_.3) | copy-start | bytes 772
  220.0 147.0 %copy-start.12 = (f32[3,32]{1,0:T(4,128)S(1)}, f32[3,32]{1,0:T(4,128)}, u32[]{:S(2)}) copy-start(f32[3,32]{1,0:T(4,128)} %refs_11_.1) | copy-start | bytes 1156
  220.0 147.0 %copy-start.13 = (f32[3,32]{1,0:T(4,128)S(1)}, f32[3,32]{1,0:T(4,128)}, u32[]{:S(2)}) copy-start(f32[3,32]{1,0:T(4,128)} %refs_17_.1) | copy-start | bytes 1156
  220.0 147.0 %copy-start.14 = (f32[2,32]{1,0:T(2,128)S(1)}, f32[2,32]{1,0:T(2,128)}, u32[]{:S(2)}) copy-start(f32[2,32]{1,0:T(2,128)} %refs_10_.1) | copy-start | bytes 772
  220.0 147.0 %copy-start.15 = (f32[2,32]{1,0:T(2,128)S(1)}, f32[2,32]{1,0:T(2,128)}, u32[]{:S(2)}) copy-start(f32[2,32]{1,0:T(2,128)} %refs_16_.1) | copy-start | bytes 772
  (5 other events, 5.4 us)

commit v7 on v6

--- a/solution.py
+++ b/solution.py
@@ -209,16 +209,16 @@
 
     @pl.loop(0, depth)
     def _(layer_step):
-        late_step(layer_step, 0)
         for hop in range(1, chips - 1):
             around(hop, layer_step)
-            late_step(layer_step, hop)
+            late_step(layer_step, hop - 1)
 
         @pl.when(layer_step < depth - 1)
         def _():
             layer_arrives(layer_step + 1)
 
         around(chips - 1, layer_step)
+        late_step(layer_step, chips - 2)
         late_step(layer_step, chips - 1)
 
     shard_count = 2 * chips * depth
@@ -600,7 +600,7 @@
     grad_gate_up[1] = matmul(turned[...], grad_up).astype(half)
 
 
-def feed_forward(normed, resid, cot, packed, down):
+def feed_forward(normed, resid, cot, gate_up, down):
     tokens, width = normed.shape
     units = down.shape[0]
     tile = UNIT_TILE
@@ -640,7 +640,7 @@
             flops=flops, bytes_accessed=12 * width * units, transcendentals=tokens * units
         ),
         name="feed_forward",
-    )(normed, resid, cot, packed, packed, down)
+    )(normed, resid, cot, gate_up, gate_up, down)
 
 
 def local(
@@ -673,20 +673,20 @@
     chips, depth = lax.axis_size("ring"), lax.axis_size("fsdp")
     in_width = in_proj.shape[1]
     out_width = out_proj.shape[1]
-    rows, unit_columns = gate_up.shape
+    rows = gate_up.shape[0]
     shards = 2 * chips * depth
     vectors = jnp.concatenate([norm_gains, conv_taps], axis=0)
     vector_count, lanes = vectors.shape
     corner = ((0, rows - vector_count), (0, LANES - lanes))
-    packed_shards, down_shards = gather(
-        chips, depth, (gate_up, in_proj, out_proj, jnp.pad(vectors, corner)), (down_proj,)
-    )
-    packed_full = packed_shards.reshape(width, -1)
+    gate_shards, down_shards, mixer_shards = gather(
+        chips, depth, (gate_up,), (down_proj,), (in_proj, out_proj, jnp.pad(vectors, corner))
+    )
+    gate_full = gate_shards.reshape(width, -1)
     down_full = down_shards.reshape(-1, width)
-    out_start = unit_columns + in_width
-    in_full = packed_full[:, unit_columns:out_start]
-    out_full = packed_full[:, out_start : out_start + out_width]
-    vectors_full = packed_shards[:, :vector_count, -LANES:][:, :, :lanes].astype(single)
+    mixer_columns = mixer_shards.reshape(width, -1)
+    in_full = mixer_columns[:, :in_width]
+    out_full = mixer_columns[:, in_width : in_width + out_width]
+    vectors_full = mixer_shards[:, :vector_count, -LANES:][:, :, :lanes].astype(single)
     vectors_full = vectors_full.transpose(1, 0, 2).reshape(vector_count, width)
     mixer_full = (None, None, in_full, out_full)
     gains_f = vectors_full[:2]
@@ -717,7 +717,7 @@
     normed_two = (resid_two * scale_two * gains_f[1]).astype(half)
     cot_rows = cotangent.reshape(tok_count, width)
     block_out, grad_normed, grad_down, grad_gate_up = feed_forward(
-        normed_two, resid_two, cot_rows, packed_full, down_full
+        normed_two, resid_two, cot_rows, gate_full, down_full
     )
     norm_part, gain_two_grad = norm_backward(resid_two, scale_two, gains_f[1], grad_normed)
     grad_resid = cot_rows.astype(single) + norm_part

time: 374 us -> 367 us (0.981)
  Pallas kernels: 326 us -> 319 us
    pallas_call x1, Pallas kernels: 144 us -> 136 us  [gather(): pl.pallas_call(functools.partial(gather_kernel, chips, depth, [len(g) for...]
  transfers between devices with their start and end apart: 3 -> 3, of which waited for: 1 -> 2; matrix products, arithmetic and copies ran while one was open for 1% -> 1% of each run, Pallas kernels for 0% -> 0%
where the time goes in v7:
time: 367 us
  Pallas kernels  319 us (87%)
  matrix products  21.8 us (6%)
  other arithmetic  13.9 us (4%)
  starting transfers between devices  5.02 us (1%)
  local copies, waits for them, and re-layouts  4.97 us (1%)
    pallas_call x1, Pallas kernels, scatter(): pl.pallas_call(functools.partial(scatter_kernel, chips, depth, count), ou...  148 us
    pallas_call x1, Pallas kernels, gather(): pl.pallas_call(functools.partial(gather_kernel, chips, depth, [len(g) for...  136 us
    pallas_call x1, Pallas kernels, feed_forward(): pl.pallas_call(feed_forward_kernel, grid=(tiles,), out_shape=[jax.ShapeDt...  28.5 us
    dot_general x2, matrix products, matmul_nt(): lax.dot_general(left, right, (((1,), (1,)), ((), ())), preferred_element_...  8.06 us
  transfers between devices with their start and end apart: 3, of which 2 were waited for; matrix products, arithmetic and copies ran while one was open for 1% of the time, Pallas kernels for 0%

profile of v7, /device:TPU:0, one launch (start us, length us, event | category | flops | bytes accessed | tf_op | source)
XLA Modules:
  0.0 366.9 jit_solution(1868832559550312771)
XLA Ops:
  0.7 1.3 fusion.12
  2.0 1.3 select_maximum_fusion.refs_4_
  3.3 136.4 %gather_weights.1 = (bf16[32,32,9216]{2,1,0:T(8,128)(2,1)}, bf16[32,144,1024]{2,1,0:T(8,128)(2,1)}, bf16[32,32,4224]{2,1,0:T(8,128)(2,1)}) custom-call(f32[32,9216]{1,0:T(8,128)} %refs_8_.1, f32[144,1024]{1,0:T(8,128)} %refs_9_.1, f32[32,3072]{1,0:T(8,128)} %refs_6_.1, f32[32,1024]{1,0:T(8,128)} %refs_7_.1, f32[32,128]{1,0:T(8,128)} %select_maximum_fusion.refs_4_), custom_call_target="tpu_custom_call" | custom-call | tf_op jit(solution)/shard_map/gather_weights/pallas_call | solution.py:237
  139.7 0.9 convert_bitcast_fusion
  140.8 4.7 %fusion.2 = f32[256,3072]{1,0:T(8,128)S(1)} fusion(bf16[1024,4224]{1,0:T(8,128)(2,1)} %bitcast.77, bf16[1,256,1024]{2,1,0:T(8,128)(2,1)S(1)} %copy-done.19, f32[1024]{0:T(1024)S(1)} %mul.260, f32[256]{0:T(256)S(1)} %get-tuple-element.117), kind=kOutput, calls=%fused_computation.3 | convolution fusion | flops 1611661312 | bytes 9966592 | tf_op jit(solution)/shard_map/dot_general | solution.py:512
  145.5 1.6 copy-done.16
  147.3 2.3 collective-permute-start
  150.6 1.7 multiply_convert_fusion.4
  152.3 2.5 multiply_reduce_fusion.5
  154.9 28.5 %feed_forward.1 = (f32[256,1024]{1,0:T(8,128)}, f32[256,1024]{1,0:T(8,128)S(1)}, bf16[4608,1024]{1,0:T(8,128)(2,1)}, bf16[2,1024,4608]{2,1,0:T(8,128)(2,1)}) custom-call(bf16[256,1024]{1,0:T(8,128)(2,1)S(1)} %multiply_convert_fusion.3.normed, f32[256,1024]{1,0:T(8,128)S(1)} %get-tuple-element.123.resid, bf16[256,1024]{1,0:T(8,128)(2,1)S(1)} %bitcast.72, ...), custom_call_target="tpu_custom_call" | custom-call | flops 21743271936 | bytes 56623104 | tf_op jit(solution)/shard_map/feed_forward/pallas_call | solution.py:614
  184.1 2.3 fusion.6
  186.4 2.5 multiply_reduce_fusion
  189.2 0.9 copy-done.18
  190.1 1.3 collective-permute-start.2
  191.4 1.5 collective-permute-start.1
  192.9 2.1 convolution_convert_fusion.1
  195.8 2.1 multiply_convert_fusion.2
  197.8 1.4 multiply_convert_fusion
  199.2 5.7 %fusion.21 = (bf16[1024]{0:T(1024)(128)(2,1)S(1)}, f32[256]{0:T(256)S(1)}, f32[256,1024]{1,0:T(8,128)}) fusion(bf16[1,256,1024]{2,1,0:T(8,128)(2,1)S(1)} %copy-done.20, f32[256]{0:T(256)S(1)} %get-tuple-element.117, f32[1024]{0:T(1024)S(1)} %mul.260, bf16[1024,4224]{1,0:T(8,128)(2,1)} %bitcast.80, bf16[256,1024]{1,0:T(8,128)(2,1)S(1)} %multiply_convert_fusion, ...), kind=kOutput, calls=%fused_computation.29 | convolution fusion | flops 1617165056 | bytes 9445376 | tf_op jit(solution)/shard_map/dot_general | solution.py:522
  205.0 4.5 %convolution_convert_fusion = bf16[1024,3072]{1,0:T(8,128)(2,1)} fusion(bf16[256,1024]{1,0:T(8,128)(2,1)S(1)} %multiply_convert_fusion, bf16[256,1024]{1,0:T(8,128)(2,1)S(1)} %copy-done.23, bf16[256,1024]{1,0:T(8,128)(2,1)S(1)} %get-tuple-element.109, bf16[1,256,1024]{2,1,0:T(8,128)(2,1)S(1)} %copy-done.20, f32[1024]{0:T(1024)S(1)} %mul.260, ...), kind=kOutput, calls=%fused_computation | convolution fusion | flops 1619525632 | bytes 8393728 | tf_op jit(solution)/shard_map/dot_general | solution.py:516
  210.0 0.8 copy-done.21
  211.1 1.3 fusion.18
  212.5 147.8 %scatter_gradients.1 = (f32[32,9216]{1,0:T(8,128)S(1)}, f32[32,3072]{1,0:T(8,128)S(1)}, f32[32,1152]{1,0:T(8,128)S(1)}, f32[144,1024]{1,0:T(8,128)S(1)}) custom-call(bf16[2,32,32,4608]{3,2,1,0:T(8,128)(2,1)} %bitcast.73, bf16[32,32,3072]{2,1,0:T(8,128)(2,1)} %bitcast.76, bf16[32,32,1152]{2,1,0:T(8,128)(2,1)S(1)} %fusion.5.refs_2_, ...), custom_call_target="tpu_custom_call" | custom-call | tf_op jit(solution)/shard_map/scatter_gradients/pallas_call | solution.py:481
  360.5 6.2 %adamw.1 = (f32[2,32]{1,0:T(2,128)}, f32[3,32]{1,0:T(4,128)}, f32[32,3072]{1,0:T(8,128)}, f32[32,1024]{1,0:T(8,128)}, f32[32,9216]{1,0:T(8,128)}, /*index=5*/f32...) custom-call(f32[32,1152]{1,0:T(8,128)S(1)} %get-tuple-element.68.ref, ...), custom_call_target="tpu_custom_call" | custom-call | tf_op jit(solution)/shard_map/adamw/pallas_call | solution.py:566
  (77 shorter events, 4.1 us)
Async XLA Ops:
  0.7 140.2 %copy-start.19 = (bf16[1,256,1024]{2,1,0:T(8,128)(2,1)S(1)}, bf16[1,256,1024]{2,1,0:T(8,128)(2,1)}, u32[]{:S(2)}) copy-start(bf16[1,256,1024]{2,1,0:T(8,128)(2,1)} %param.21) | copy-start | bytes 1572868
  140.8 8.8 %copy-start.24 = (s32[1,256]{1,0:T(1,128)S(1)}, s32[1,256]{1,0:T(1,128)}, u32[]{:S(2)}) copy-start(s32[1,256]{1,0:T(1,128)} %param.23) | copy-start | bytes 3076
  147.3 3.1 collective-permute-start
  152.3 2.7 copy-start.5
  190.1 5.2 %collective-permute-start.2 = (f32[1,2,1024]{2,1,0:T(2,128)S(1)}, f32[1,2,1024]{2,1,0:T(2,128)S(1)}, u32[]{:S(2)}, u32[]{:S(2)}) collective-permute-start(f32[1,2,1024]{2,1,0:T(2,128)S(1)} %slice.112), channel_id=1, source_target_pairs={{4,0},{8,4},{12,8},{16,12},{20,16},{24,20},{28,24},{5,1},{9,5},{13... | collective-permute-start | bytes 24584 | tf_op jit(solution)/shard_map/ppermute | solution.py:508
  191.4 4.4 %collective-permute-start.1 = (f32[1,2,1024]{2,1,0:T(2,128)S(1)}, f32[1,2,1024]{2,1,0:T(2,128)S(1)}, u32[]{:S(2)}, u32[]{:S(2)}) collective-permute-start(f32[1,2,1024]{2,1,0:T(2,128)S(1)} %slice.111), channel_id=1, source_target_pairs={{4,0},{8,4},{12,8},{16,12},{20,16},{24,20},{28,24},{5,1},{9,5},{13... | collective-permute-start | bytes 24584 | tf_op jit(solution)/shard_map/ppermute | solution.py:508
  195.3 3.9 %copy-start.20 = (bf16[1,256,1024]{2,1,0:T(8,128)(2,1)S(1)}, bf16[1,256,1024]{2,1,0:T(8,128)(2,1)}, u32[]{:S(2)}) copy-start(bf16[1,256,1024]{2,1,0:T(8,128)(2,1)} %param.21) | copy-start | bytes 1572868
  195.3 3.9 %copy-start.23 = (bf16[256,1024]{1,0:T(8,128)(2,1)S(1)}, bf16[256,1024]{1,0:T(8,128)(2,1)}, u32[]{:S(2)}) copy-start(bf16[256,1024]{1,0:T(8,128)(2,1)} %get-tuple-element.113) | copy-start | bytes 1572868
  205.0 4.8 %copy-start.17 = (bf16[1024,1024]{1,0:T(8,128)(2,1)S(1)}, bf16[1024,1024]{1,0:T(8,128)(2,1)}, u32[]{:S(2)}) copy-start(bf16[1024,1024]{1,0:T(8,128)(2,1)} %convolution_convert_fusion.1) | copy-start | bytes 6291460
  212.4 148.0 %copy-start = (f32[144,1024]{1,0:T(8,128)S(1)}, f32[144,1024]{1,0:T(8,128)}, u32[]{:S(2)}) copy-start(f32[144,1024]{1,0:T(8,128)} %refs_9_.1) | copy-start | bytes 1769476
  212.4 148.0 %copy-start.1 = (f32[32,3072]{1,0:T(8,128)S(1)}, f32[32,3072]{1,0:T(8,128)}, u32[]{:S(2)}) copy-start(f32[32,3072]{1,0:T(8,128)} %refs_6_.1) | copy-start | bytes 1179652
  212.4 148.0 %copy-start.2 = (f32[144,1024]{1,0:T(8,128)S(1)}, f32[144,1024]{1,0:T(8,128)}, u32[]{:S(2)}) copy-start(f32[144,1024]{1,0:T(8,128)} %refs_15_.1) | copy-start | bytes 1769476
  212.4 148.0 %copy-start.3 = (f32[144,1024]{1,0:T(8,128)S(1)}, f32[144,1024]{1,0:T(8,128)}, u32[]{:S(2)}) copy-start(f32[144,1024]{1,0:T(8,128)} %refs_21_.1) | copy-start | bytes 1769476
  212.4 148.0 %copy-start.4 = (f32[32,1024]{1,0:T(8,128)S(1)}, f32[32,1024]{1,0:T(8,128)}, u32[]{:S(2)}) copy-start(f32[32,1024]{1,0:T(8,128)} %refs_7_.1) | copy-start | bytes 393220
  212.4 148.0 %copy-start.6 = (f32[32,3072]{1,0:T(8,128)S(1)}, f32[32,3072]{1,0:T(8,128)}, u32[]{:S(2)}) copy-start(f32[32,3072]{1,0:T(8,128)} %refs_12_.1) | copy-start | bytes 1179652
  212.4 148.0 %copy-start.7 = (f32[32,3072]{1,0:T(8,128)S(1)}, f32[32,3072]{1,0:T(8,128)}, u32[]{:S(2)}) copy-start(f32[32,3072]{1,0:T(8,128)} %refs_18_.1) | copy-start | bytes 1179652
  212.4 148.0 %copy-start.8 = (f32[32,1024]{1,0:T(8,128)S(1)}, f32[32,1024]{1,0:T(8,128)}, u32[]{:S(2)}) copy-start(f32[32,1024]{1,0:T(8,128)} %refs_13_.1) | copy-start | bytes 393220
  212.4 148.0 %copy-start.9 = (f32[32,1024]{1,0:T(8,128)S(1)}, f32[32,1024]{1,0:T(8,128)}, u32[]{:S(2)}) copy-start(f32[32,1024]{1,0:T(8,128)} %refs_19_.1) | copy-start | bytes 393220
  212.4 148.0 %copy-start.10 = (f32[3,32]{1,0:T(4,128)S(1)}, f32[3,32]{1,0:T(4,128)}, u32[]{:S(2)}) copy-start(f32[3,32]{1,0:T(4,128)} %refs_5_.1) | copy-start | bytes 1156
  212.4 148.0 %copy-start.11 = (f32[2,32]{1,0:T(2,128)S(1)}, f32[2,32]{1,0:T(2,128)}, u32[]{:S(2)}) copy-start(f32[2,32]{1,0:T(2,128)} %refs_4_.1) | copy-start | bytes 772
  212.5 148.0 %copy-start.12 = (f32[3,32]{1,0:T(4,128)S(1)}, f32[3,32]{1,0:T(4,128)}, u32[]{:S(2)}) copy-start(f32[3,32]{1,0:T(4,128)} %refs_11_.1) | copy-start | bytes 1156
  212.5 148.0 %copy-start.13 = (f32[3,32]{1,0:T(4,128)S(1)}, f32[3,32]{1,0:T(4,128)}, u32[]{:S(2)}) copy-start(f32[3,32]{1,0:T(4,128)} %refs_17_.1) | copy-start | bytes 1156
  212.5 148.0 %copy-start.14 = (f32[2,32]{1,0:T(2,128)S(1)}, f32[2,32]{1,0:T(2,128)}, u32[]{:S(2)}) copy-start(f32[2,32]{1,0:T(2,128)} %refs_10_.1) | copy-start | bytes 772
  212.5 148.0 %copy-start.15 = (f32[2,32]{1,0:T(2,128)S(1)}, f32[2,32]{1,0:T(2,128)}, u32[]{:S(2)}) copy-start(f32[2,32]{1,0:T(2,128)} %refs_16_.1) | copy-start | bytes 772
  (4 other events, 5.1 us)

commit v8 on v7

--- a/solution.py
+++ b/solution.py
@@ -446,16 +446,18 @@
             def _():
                 late_step(layer_step + 1, hop)
 
-        for hop in range(2, chips):
+        step(layer_step, 2)
+        for hop in range(3, chips):
             step(layer_step, hop)
-            late_ahead(hop - 1)
+            late_ahead(hop - 2)
 
         @pl.when(layer_step < depth - 1)
         def _():
             step(layer_step + 1, 1)
 
+        late_ahead(chips - 2)
+        step(layer_step, chips)
         late_ahead(chips - 1)
-        step(layer_step, chips)
         late_ahead(chips)
 
     for which in range(count):

time: 367 us -> 367 us (level)
  no operation moved by 1% of the time
where the time goes in v8:
time: 367 us
  Pallas kernels  319 us (87%)
  matrix products  21.8 us (6%)
  other arithmetic  13.9 us (4%)
  starting transfers between devices  5.02 us (1%)
  local copies, waits for them, and re-layouts  4.97 us (1%)
    pallas_call x1, Pallas kernels, scatter(): pl.pallas_call(functools.partial(scatter_kernel, chips, depth, count), ou...  148 us
    pallas_call x1, Pallas kernels, gather(): pl.pallas_call(functools.partial(gather_kernel, chips, depth, [len(g) for...  136 us
    pallas_call x1, Pallas kernels, feed_forward(): pl.pallas_call(feed_forward_kernel, grid=(tiles,), out_shape=[jax.ShapeDt...  28.5 us
    dot_general x2, matrix products, matmul_nt(): lax.dot_general(left, right, (((1,), (1,)), ((), ())), preferred_element_...  8.06 us
  transfers between devices with their start and end apart: 3, of which 2 were waited for; matrix products, arithmetic and copies ran while one was open for 1% of the time, Pallas kernels for 0%

profile of v8, /device:TPU:0, one launch (start us, length us, event | category | flops | bytes accessed | tf_op | source)
XLA Modules:
  0.0 366.9 jit_solution(1099021266467917582)
XLA Ops:
  0.7 1.3 fusion.12
  2.0 1.3 select_maximum_fusion.refs_4_
  3.3 136.4 %gather_weights.1 = (bf16[32,32,9216]{2,1,0:T(8,128)(2,1)}, bf16[32,144,1024]{2,1,0:T(8,128)(2,1)}, bf16[32,32,4224]{2,1,0:T(8,128)(2,1)}) custom-call(f32[32,9216]{1,0:T(8,128)} %refs_8_.1, f32[144,1024]{1,0:T(8,128)} %refs_9_.1, f32[32,3072]{1,0:T(8,128)} %refs_6_.1, f32[32,1024]{1,0:T(8,128)} %refs_7_.1, f32[32,128]{1,0:T(8,128)} %select_maximum_fusion.refs_4_), custom_call_target="tpu_custom_call" | custom-call | tf_op jit(solution)/shard_map/gather_weights/pallas_call | solution.py:237
  139.7 0.9 convert_bitcast_fusion
  140.8 4.7 %fusion.2 = f32[256,3072]{1,0:T(8,128)S(1)} fusion(bf16[1024,4224]{1,0:T(8,128)(2,1)} %bitcast.77, bf16[1,256,1024]{2,1,0:T(8,128)(2,1)S(1)} %copy-done.19, f32[1024]{0:T(1024)S(1)} %mul.260, f32[256]{0:T(256)S(1)} %get-tuple-element.117), kind=kOutput, calls=%fused_computation.3 | convolution fusion | flops 1611661312 | bytes 9966592 | tf_op jit(solution)/shard_map/dot_general | solution.py:514
  145.5 1.6 copy-done.16
  147.3 2.3 collective-permute-start
  150.6 1.7 multiply_convert_fusion.4
  152.3 2.5 multiply_reduce_fusion.5
  154.9 28.5 %feed_forward.1 = (f32[256,1024]{1,0:T(8,128)}, f32[256,1024]{1,0:T(8,128)S(1)}, bf16[4608,1024]{1,0:T(8,128)(2,1)}, bf16[2,1024,4608]{2,1,0:T(8,128)(2,1)}) custom-call(bf16[256,1024]{1,0:T(8,128)(2,1)S(1)} %multiply_convert_fusion.3.normed, f32[256,1024]{1,0:T(8,128)S(1)} %get-tuple-element.123.resid, bf16[256,1024]{1,0:T(8,128)(2,1)S(1)} %bitcast.72, ...), custom_call_target="tpu_custom_call" | custom-call | flops 21743271936 | bytes 56623104 | tf_op jit(solution)/shard_map/feed_forward/pallas_call | solution.py:616
  184.1 2.3 fusion.6
  186.4 2.5 multiply_reduce_fusion
  189.2 0.9 copy-done.18
  190.1 1.3 collective-permute-start.2
  191.4 1.5 collective-permute-start.1
  192.9 2.1 convolution_convert_fusion.1
  195.8 2.1 multiply_convert_fusion.2
  197.8 1.4 multiply_convert_fusion
  199.2 5.7 %fusion.21 = (bf16[1024]{0:T(1024)(128)(2,1)S(1)}, f32[256]{0:T(256)S(1)}, f32[256,1024]{1,0:T(8,128)}) fusion(bf16[1,256,1024]{2,1,0:T(8,128)(2,1)S(1)} %copy-done.20, f32[256]{0:T(256)S(1)} %get-tuple-element.117, f32[1024]{0:T(1024)S(1)} %mul.260, bf16[1024,4224]{1,0:T(8,128)(2,1)} %bitcast.80, bf16[256,1024]{1,0:T(8,128)(2,1)S(1)} %multiply_convert_fusion, ...), kind=kOutput, calls=%fused_computation.29 | convolution fusion | flops 1617165056 | bytes 9445376 | tf_op jit(solution)/shard_map/dot_general | solution.py:524
  205.0 4.5 %convolution_convert_fusion = bf16[1024,3072]{1,0:T(8,128)(2,1)} fusion(bf16[256,1024]{1,0:T(8,128)(2,1)S(1)} %multiply_convert_fusion, bf16[256,1024]{1,0:T(8,128)(2,1)S(1)} %copy-done.23, bf16[256,1024]{1,0:T(8,128)(2,1)S(1)} %get-tuple-element.109, bf16[1,256,1024]{2,1,0:T(8,128)(2,1)S(1)} %copy-done.20, f32[1024]{0:T(1024)S(1)} %mul.260, ...), kind=kOutput, calls=%fused_computation | convolution fusion | flops 1619525632 | bytes 8393728 | tf_op jit(solution)/shard_map/dot_general | solution.py:518
  210.0 0.8 copy-done.21
  211.1 1.3 fusion.18
  212.5 147.8 %scatter_gradients.1 = (f32[32,9216]{1,0:T(8,128)S(1)}, f32[32,3072]{1,0:T(8,128)S(1)}, f32[32,1152]{1,0:T(8,128)S(1)}, f32[144,1024]{1,0:T(8,128)S(1)}) custom-call(bf16[2,32,32,4608]{3,2,1,0:T(8,128)(2,1)} %bitcast.73, bf16[32,32,3072]{2,1,0:T(8,128)(2,1)} %bitcast.76, bf16[32,32,1152]{2,1,0:T(8,128)(2,1)S(1)} %fusion.5.refs_2_, ...), custom_call_target="tpu_custom_call" | custom-call | tf_op jit(solution)/shard_map/scatter_gradients/pallas_call | solution.py:483
  360.5 6.2 %adamw.1 = (f32[2,32]{1,0:T(2,128)}, f32[3,32]{1,0:T(4,128)}, f32[32,3072]{1,0:T(8,128)}, f32[32,1024]{1,0:T(8,128)}, f32[32,9216]{1,0:T(8,128)}, /*index=5*/f32...) custom-call(f32[32,1152]{1,0:T(8,128)S(1)} %get-tuple-element.68.ref, ...), custom_call_target="tpu_custom_call" | custom-call | tf_op jit(solution)/shard_map/adamw/pallas_call | solution.py:568
  (77 shorter events, 4.1 us)
Async XLA Ops:
  0.7 140.2 %copy-start.19 = (bf16[1,256,1024]{2,1,0:T(8,128)(2,1)S(1)}, bf16[1,256,1024]{2,1,0:T(8,128)(2,1)}, u32[]{:S(2)}) copy-start(bf16[1,256,1024]{2,1,0:T(8,128)(2,1)} %param.21) | copy-start | bytes 1572868
  140.8 8.8 %copy-start.24 = (s32[1,256]{1,0:T(1,128)S(1)}, s32[1,256]{1,0:T(1,128)}, u32[]{:S(2)}) copy-start(s32[1,256]{1,0:T(1,128)} %param.23) | copy-start | bytes 3076
  147.3 3.1 collective-permute-start
  152.3 2.7 copy-start.5
  190.1 5.2 %collective-permute-start.2 = (f32[1,2,1024]{2,1,0:T(2,128)S(1)}, f32[1,2,1024]{2,1,0:T(2,128)S(1)}, u32[]{:S(2)}, u32[]{:S(2)}) collective-permute-start(f32[1,2,1024]{2,1,0:T(2,128)S(1)} %slice.112), channel_id=1, source_target_pairs={{4,0},{8,4},{12,8},{16,12},{20,16},{24,20},{28,24},{5,1},{9,5},{13... | collective-permute-start | bytes 24584 | tf_op jit(solution)/shard_map/ppermute | solution.py:510
  191.4 4.4 %collective-permute-start.1 = (f32[1,2,1024]{2,1,0:T(2,128)S(1)}, f32[1,2,1024]{2,1,0:T(2,128)S(1)}, u32[]{:S(2)}, u32[]{:S(2)}) collective-permute-start(f32[1,2,1024]{2,1,0:T(2,128)S(1)} %slice.111), channel_id=1, source_target_pairs={{4,0},{8,4},{12,8},{16,12},{20,16},{24,20},{28,24},{5,1},{9,5},{13... | collective-permute-start | bytes 24584 | tf_op jit(solution)/shard_map/ppermute | solution.py:510
  195.3 3.9 %copy-start.20 = (bf16[1,256,1024]{2,1,0:T(8,128)(2,1)S(1)}, bf16[1,256,1024]{2,1,0:T(8,128)(2,1)}, u32[]{:S(2)}) copy-start(bf16[1,256,1024]{2,1,0:T(8,128)(2,1)} %param.21) | copy-start | bytes 1572868
  195.3 3.9 %copy-start.23 = (bf16[256,1024]{1,0:T(8,128)(2,1)S(1)}, bf16[256,1024]{1,0:T(8,128)(2,1)}, u32[]{:S(2)}) copy-start(bf16[256,1024]{1,0:T(8,128)(2,1)} %get-tuple-element.113) | copy-start | bytes 1572868
  205.0 4.8 %copy-start.17 = (bf16[1024,1024]{1,0:T(8,128)(2,1)S(1)}, bf16[1024,1024]{1,0:T(8,128)(2,1)}, u32[]{:S(2)}) copy-start(bf16[1024,1024]{1,0:T(8,128)(2,1)} %convolution_convert_fusion.1) | copy-start | bytes 6291460
  212.4 148.0 %copy-start = (f32[144,1024]{1,0:T(8,128)S(1)}, f32[144,1024]{1,0:T(8,128)}, u32[]{:S(2)}) copy-start(f32[144,1024]{1,0:T(8,128)} %refs_9_.1) | copy-start | bytes 1769476
  212.4 148.0 %copy-start.1 = (f32[32,3072]{1,0:T(8,128)S(1)}, f32[32,3072]{1,0:T(8,128)}, u32[]{:S(2)}) copy-start(f32[32,3072]{1,0:T(8,128)} %refs_6_.1) | copy-start | bytes 1179652
  212.4 148.0 %copy-start.2 = (f32[144,1024]{1,0:T(8,128)S(1)}, f32[144,1024]{1,0:T(8,128)}, u32[]{:S(2)}) copy-start(f32[144,1024]{1,0:T(8,128)} %refs_15_.1) | copy-start | bytes 1769476
  212.4 148.0 %copy-start.3 = (f32[144,1024]{1,0:T(8,128)S(1)}, f32[144,1024]{1,0:T(8,128)}, u32[]{:S(2)}) copy-start(f32[144,1024]{1,0:T(8,128)} %refs_21_.1) | copy-start | bytes 1769476
  212.4 148.0 %copy-start.4 = (f32[32,1024]{1,0:T(8,128)S(1)}, f32[32,1024]{1,0:T(8,128)}, u32[]{:S(2)}) copy-start(f32[32,1024]{1,0:T(8,128)} %refs_7_.1) | copy-start | bytes 393220
  212.4 148.0 %copy-start.6 = (f32[32,3072]{1,0:T(8,128)S(1)}, f32[32,3072]{1,0:T(8,128)}, u32[]{:S(2)}) copy-start(f32[32,3072]{1,0:T(8,128)} %refs_12_.1) | copy-start | bytes 1179652
  212.4 148.0 %copy-start.7 = (f32[32,3072]{1,0:T(8,128)S(1)}, f32[32,3072]{1,0:T(8,128)}, u32[]{:S(2)}) copy-start(f32[32,3072]{1,0:T(8,128)} %refs_18_.1) | copy-start | bytes 1179652
  212.4 148.0 %copy-start.8 = (f32[32,1024]{1,0:T(8,128)S(1)}, f32[32,1024]{1,0:T(8,128)}, u32[]{:S(2)}) copy-start(f32[32,1024]{1,0:T(8,128)} %refs_13_.1) | copy-start | bytes 393220
  212.4 148.0 %copy-start.9 = (f32[32,1024]{1,0:T(8,128)S(1)}, f32[32,1024]{1,0:T(8,128)}, u32[]{:S(2)}) copy-start(f32[32,1024]{1,0:T(8,128)} %refs_19_.1) | copy-start | bytes 393220
  212.4 148.0 %copy-start.10 = (f32[3,32]{1,0:T(4,128)S(1)}, f32[3,32]{1,0:T(4,128)}, u32[]{:S(2)}) copy-start(f32[3,32]{1,0:T(4,128)} %refs_5_.1) | copy-start | bytes 1156
  212.4 148.0 %copy-start.11 = (f32[2,32]{1,0:T(2,128)S(1)}, f32[2,32]{1,0:T(2,128)}, u32[]{:S(2)}) copy-start(f32[2,32]{1,0:T(2,128)} %refs_4_.1) | copy-start | bytes 772
  212.5 148.0 %copy-start.12 = (f32[3,32]{1,0:T(4,128)S(1)}, f32[3,32]{1,0:T(4,128)}, u32[]{:S(2)}) copy-start(f32[3,32]{1,0:T(4,128)} %refs_11_.1) | copy-start | bytes 1156
  212.5 148.0 %copy-start.13 = (f32[3,32]{1,0:T(4,128)S(1)}, f32[3,32]{1,0:T(4,128)}, u32[]{:S(2)}) copy-start(f32[3,32]{1,0:T(4,128)} %refs_17_.1) | copy-start | bytes 1156
  212.5 148.0 %copy-start.14 = (f32[2,32]{1,0:T(2,128)S(1)}, f32[2,32]{1,0:T(2,128)}, u32[]{:S(2)}) copy-start(f32[2,32]{1,0:T(2,128)} %refs_10_.1) | copy-start | bytes 772
  212.5 148.0 %copy-start.15 = (f32[2,32]{1,0:T(2,128)S(1)}, f32[2,32]{1,0:T(2,128)}, u32[]{:S(2)}) copy-start(f32[2,32]{1,0:T(2,128)} %refs_16_.1) | copy-start | bytes 772
  (4 other events, 5.1 us)
